TPU v7x, 32 devices: a whole 2x2x4 slice. The times are simulated.
32 devices in a mesh: groups: 2 (over y), seq: 16 (over z, x, core).
Axes of the slice: x: 2, y: 2, z: 4, core: 2. Of those that a mesh axis runs over, the one named last changes fastest.
Arguments:
- qkv: bfloat16 [4096, 32, 384], P(('groups', 'seq')), parts along dimension 0
- routes: int32 [4096, 32], P(('groups', 'seq')), parts along dimension 0, may hold values from 0 to 1, as said below
Outputs:
- attended: bfloat16 [4096, 32, 128], P(('groups', 'seq')), parts along dimension 0
There are 2 independent parts, one for each index of `groups`. A program takes and returns all parts, laid end to end along the dimension named above; each array names one. Nothing has to cross between parts.
Inputs may be any that keep to these rules, and one draw needn't show every extreme that they name: Every cluster of every head holds between 512 and 1536 tokens, and in every head some cluster holds exactly 1536. Numbering the pairs (head h, cluster c) as h * 2 + c, the tokens of one device name each aligned group of 4 pairs exactly 256 times. Integer counts, offsets and slot indices derived from routes may cross between devices packed several to a 32-bit word.
All inputs are finite; a program needn't handle non-finite values.
Results may differ from a plain program's by a relative error of at most 0.0047.
Values may be sent and summed in bfloat16 or wider, within the bound.
No kernel may reach another device: no remote copies, remote signals or barrier semaphores. Data moves between devices by JAX's collectives and lax.ppermute only.
A program may use at most 128 MiB of HBM per device.

v0:
```python
import math

import jax
import jax.numpy as jnp
from jax import lax
from jax.sharding import PartitionSpec as P

CLEN = 1024


def entering(part, axis, combine, identity):
    place = lax.axis_index(axis)
    gathered = lax.all_gather(part, axis)
    state = jnp.zeros_like(part) + jnp.asarray(identity, part.dtype)

    def one(turn, state):
        return combine(state, lax.dynamic_index_in_dim(gathered, turn, 0, False))

    return lax.fori_loop(0, place, one, state)


def attend(queries, keys, values, start, scale):
    block_rows = queries.shape[1]
    span = keys.shape[1]
    scores = jnp.einsum("pqd,pkd->pqk", queries, keys, preferred_element_type=jnp.float32) * scale
    rows = start + jnp.arange(block_rows, dtype=jnp.int32)[:, None]
    cols = jnp.arange(span, dtype=jnp.int32)[None, :]
    scores = jnp.where((cols <= rows)[None], scores, -1e30)
    peak = jnp.max(scores, axis=2, keepdims=True)
    expo = jnp.exp(scores - peak)
    weights = (expo / jnp.sum(expo, axis=2, keepdims=True)).astype(jnp.bfloat16)
    return jnp.einsum("pqk,pkd->pqd", weights, values, preferred_element_type=jnp.float32).astype(
        jnp.bfloat16
    )


def local(qkv, routes):
    tok, heads, width = qkv.shape
    head_size = width // 3
    nseq = lax.axis_size("seq")
    clusters = nseq * tok // CLEN
    pairs_dev = heads * tok // CLEN
    capacity = 3 * CLEN // 2
    block_rows = CLEN // 2
    share = CLEN // nseq
    rows_peer = pairs_dev * share
    total_pairs = heads * clusters
    scale = 1.0 / math.sqrt(head_size)
    member = routes[:, :, None] == jnp.arange(clusters, dtype=jnp.int32)[None, None, :]
    member_flat = member.reshape(tok, total_pairs)
    counts = jnp.sum(member_flat.astype(jnp.int32), axis=0)
    earlier = (jnp.arange(tok)[:, None] > jnp.arange(tok)[None, :]).astype(jnp.bfloat16)
    before = jnp.dot(earlier, member_flat.astype(jnp.bfloat16), preferred_element_type=jnp.float32)
    rank = jnp.sum(jnp.where(member, before.reshape(tok, heads, clusters), 0.0), axis=2).astype(
        jnp.int32
    )
    prefix = entering(counts, "seq", lambda first, second: first + second, jnp.zeros_like(counts))

    def lookup(table):
        return jnp.sum(jnp.where(member, table.reshape(heads, clusters)[None], 0), axis=2)

    group_counts = counts.reshape(total_pairs // pairs_dev, pairs_dev)
    within = (jnp.cumsum(group_counts, axis=1) - group_counts).reshape(total_pairs)
    slot = lookup(prefix) + rank
    pair_index = jnp.arange(heads, dtype=jnp.int32)[None, :] * clusters + routes
    owner = pair_index // pairs_dev
    local_pair = pair_index % pairs_dev
    position = (owner * rows_peer + lookup(within) + rank).reshape(tok * heads)
    target = (local_pair * capacity + slot).reshape(tok * heads)
    outgoing = (
        jnp.zeros((tok * heads, width), jnp.bfloat16)
        .at[position]
        .set(qkv.reshape(tok * heads, width))
    )
    labels = jnp.zeros((tok * heads,), jnp.int32).at[position].set(target)
    arrived, places = (
        lax.all_to_all(outgoing, "seq", split_axis=0, concat_axis=0, tiled=True),
        lax.all_to_all(labels, "seq", split_axis=0, concat_axis=0, tiled=True),
    )
    tiles = jnp.zeros((pairs_dev * capacity, width), jnp.bfloat16).at[places].set(arrived)
    tiles = tiles.reshape(pairs_dev, capacity, width)
    pieces = []
    for index in range(3):
        start = index * block_rows
        stop = start + block_rows
        pieces.append(
            attend(
                tiles[:, start:stop, :head_size],
                tiles[:, :stop, head_size : 2 * head_size],
                tiles[:, :stop, 2 * head_size :],
                start,
                scale,
            )
        )
    results = jnp.concatenate(pieces, axis=1)
    flat_results = results.reshape(pairs_dev * capacity, head_size)
    replies = flat_results[places]
    returned = lax.all_to_all(replies, "seq", split_axis=0, concat_axis=0, tiled=True)
    return returned[position].reshape(tok, heads, head_size)


def solution(mesh):
    placed = (P(("groups", "seq"), None, None), P(("groups", "seq"), None))
    return jax.shard_map(
        local,
        mesh=mesh,
        in_specs=placed,
        out_specs=P(("groups", "seq"), None, None),
        check_vma=False,
    )
```

profile of v0, /device:TPU:0, one launch (start us, length us, event | category | flops | bytes accessed | tf_op | source)
XLA Modules:
  0.0 282.5 jit_solution(1487217478119262765)
XLA Ops:
  0.0 0.8 convert_reduce_fusion
  0.9 0.1 reshape.224
  1.1 22.9 %all-gather = s32[16,1,64]{2,1,0:T(1,128)S(1)} all-gather(s32[1,1,64]{2,1,0:T(1,128)S(1)} %reshape.224), channel_id=1, replica_groups=mesh['groups'=2,'seq'=16] {'seq'}, dimensions={0}, use_global_device_ids=true | all-gather | bytes 4352 | tf_op jit(solution)/shard_map/all_gather | solution.py:13
  24.2 0.2 reduce_window_sum.13
  24.6 0.1 eq.32
  24.7 0.7 eq.27.clone
  25.5 0.9 fusion.30
  26.4 0.8 select_reduce_fusion
  27.2 0.8 fusion.47
  28.1 0.1 reshape.178
  28.4 16.1 %scatter_custom_fusion = s32[4096]{0:T(1024)} fusion(s32[4096]{0:T(1024)S(1)} %bitcast.33, s32[4096]{0:T(1024)S(1)} %reshape.204, s32[]{:T(128)} %constant.29.clone.1), kind=kCustom, calls=%fused_computation.84 | custom fusion | bytes 16388 | tf_op jit(solution)/shard_map/scatter | solution.py:75
  44.5 3.5 %all-to-all-start = ((s32[16,256,1]{1,2,0:T(1,128)}), s32[16,256,1]{1,2,0:T(1,128)S(1)}, u32[]{:S(2)}, u32[]{:S(2)}) async-start(s32[16,256,1]{1,2,0:T(1,128)} %bitcast.6), calls=%async_computation | async-start | bytes 32768 | tf_op jit(solution)/shard_map/all_to_all | solution.py:78
  48.0 20.5 %scatter_custom_fusion.1 = bf16[4096,384]{1,0:T(8,128)(2,1)} fusion(s32[4096]{0:T(1024)S(1)} %bitcast.34, bf16[4096,384]{1,0:T(8,128)(2,1)} %bitcast.40, bf16[]{:T(256)} %constant.27.clone.1), kind=kCustom, calls=%fused_computation.41 | custom fusion | bytes 3146240 | tf_op jit(solution)/shard_map/scatter | solution.py:73
  68.6 6.0 %all-to-all-start.1 = ((bf16[16,256,384]{2,1,0:T(8,128)(2,1)}), bf16[16,256,384]{2,1,0:T(8,128)(2,1)S(1)}, u32[]{:S(2)}, u32[]{:S(2)}) async-start(bf16[16,256,384]{2,1,0:T(8,128)(2,1)} %bitcast.10), calls=%async_computation.1 | async-start | bytes 6291456 | tf_op jit(solution)/shard_map/all_to_all | solution.py:77
  74.7 1.2 iota_compare_fusion.1
  75.8 1.4 iota_compare_fusion
  77.2 56.7 %all-to-all-done.1 = bf16[16,256,384]{2,1,0:T(8,128)(2,1)S(1)} async-done(((bf16[16,256,384]{2,1,0:T(8,128)(2,1)}), bf16[16,256,384]{2,1,0:T(8,128)(2,1)S(1)}, u32[]{:S(2)}, u32[]{:S(2)}) %all-to-all-start.1) | async-done | bytes 3145760 | tf_op jit(solution)/shard_map/all_to_all | solution.py:77
  133.9 21.1 %scatter_custom_fusion.2 = bf16[6144,384]{1,0:T(8,128)(2,1)} fusion(s32[4096]{0:T(1024)S(1)} %bitcast.38, bf16[4096,384]{1,0:T(8,128)(2,1)S(1)} %bitcast.31, bf16[]{:T(256)} %constant.27.clone.1), kind=kCustom, calls=%fused_computation.30 | custom fusion | bytes 4718594 | tf_op jit(solution)/shard_map/scatter | solution.py:80
  155.0 8.1 %fusion.21 = f32[4,512,1536]{2,1,0:T(8,128)} fusion(bf16[4,1536,384]{2,1,0:T(8,128)(2,1)} %bitcast.25), kind=kOutput, calls=%fused_computation.38 | convolution fusion | flops 805306368 | bytes 14680064 | tf_op jit(solution)/shard_map/pqd,pkd->pqk/dot_general | solution.py:25
  163.1 4.5 %fusion.32 = f32[4,512,1024]{2,1,0:T(8,128)} fusion(bf16[4,1536,384]{2,1,0:T(8,128)(2,1)S(1)} %bitcast.26), kind=kOutput, calls=%fused_computation.49 | convolution fusion | flops 536870912 | bytes 9961472 | tf_op jit(solution)/shard_map/pqd,pkd->pqk/dot_general | solution.py:25
  167.6 2.8 fusion.37
  170.3 16.0 %fusion.58 = (f32[4,512]{1,0:T(4,128)S(1)}, f32[4,512,1536]{2,1,0:T(8,128)}) fusion(f32[4,512,1536]{2,1,0:T(8,128)} %fusion.21, pred[512,1536]{1,0:T(8,128)(4,1)S(1)} %copy-done.2), kind=kOutput, calls=%fused_computation.95 | output fusion | flops 18875904 | bytes 25960448 | tf_op jit(solution)/shard_map/sub | solution.py:30
  186.3 6.6 %fusion.27 = bf16[4,512,128]{2,1,0:T(8,128)(2,1)S(1)} fusion(bf16[4,1536,384]{2,1,0:T(8,128)(2,1)S(1)} %bitcast.28, f32[4,512,1536]{2,1,0:T(8,128)} %get-tuple-element.42, f32[4,512]{1,0:T(4,128)S(1)} %get-tuple-element.41), kind=kOutput, calls=%fused_computation.45 | convolution fusion | flops 811859968 | bytes 14688256 | tf_op jit(solution)/shard_map/pqk,pkd->pqd/dot_general | solution.py:32
  192.9 13.0 %fusion.59 = (f32[4,512]{1,0:T(4,128)S(1)}, f32[4,512,1024]{2,1,0:T(8,128)}) fusion(f32[4,512,1024]{2,1,0:T(8,128)} %fusion.32, pred[512,1024]{1,0:T(8,128)(4,1)S(1)} %copy-done.3), kind=kOutput, calls=%fused_computation.96 | output fusion | flops 12583935 | bytes 17309696 | tf_op jit(solution)/shard_map/sub | solution.py:30
  205.9 4.9 %fusion.25 = bf16[4,512,128]{2,1,0:T(8,128)(2,1)S(1)} fusion(f32[4,512,1024]{2,1,0:T(8,128)} %get-tuple-element.44, f32[4,512]{1,0:T(4,128)S(1)} %get-tuple-element.43, bf16[4,1536,384]{2,1,0:T(8,128)(2,1)S(1)} %bitcast.29), kind=kOutput, calls=%fused_computation.43 | convolution fusion | flops 541327360 | bytes 9969664 | tf_op jit(solution)/shard_map/pqk,pkd->pqd/dot_general | solution.py:32
  210.8 2.1 fusion.60
  212.9 1.0 fusion.26
  213.9 0.1 pad_maximum_fusion
  214.0 15.0 %gather_fusion = bf16[4096,128]{1,0:T(8,128)(2,1)} fusion(bf16[6144,128]{1,0:T(8,128)(2,1)S(1)} %bitcast.24, s32[4096]{0:T(1024)S(1)} %broadcast_clamp_fusion.1), kind=kCustom, calls=%fused_computation | custom fusion | bytes 2113536 | tf_op jit(solution)/shard_map/gather | solution.py:97
  229.0 15.4 %all-to-all-start.2 = ((bf16[16,256,128]{2,1,0:T(8,128)(2,1)}), bf16[16,256,128]{2,1,0:T(8,128)(2,1)S(1)}, u32[]{:S(2)}, u32[]{:S(2)}) async-start(bf16[16,256,128]{2,1,0:T(8,128)(2,1)} %bitcast.14), calls=%async_computation.2 | async-start | bytes 2097152 | tf_op jit(solution)/shard_map/all_to_all | solution.py:98
  244.5 22.9 %all-to-all-done.2 = bf16[16,256,128]{2,1,0:T(8,128)(2,1)S(1)} async-done(((bf16[16,256,128]{2,1,0:T(8,128)(2,1)}), bf16[16,256,128]{2,1,0:T(8,128)(2,1)S(1)}, u32[]{:S(2)}, u32[]{:S(2)}) %all-to-all-start.2) | async-done | bytes 1048608 | tf_op jit(solution)/shard_map/all_to_all | solution.py:98
  267.4 15.0 %gather_fusion.1 = bf16[4096,128]{1,0:T(8,128)(2,1)} fusion(bf16[4096,128]{1,0:T(8,128)(2,1)S(1)} %bitcast.23, s32[4096]{0:T(1024)S(1)} %broadcast_clamp_fusion), kind=kCustom, calls=%fused_computation.1 | custom fusion | bytes 2113536 | tf_op jit(solution)/shard_map/gather | solution.py:99
  (32 shorter events, 1.0 us)
Async XLA Ops:
  44.5 24.0 %all-to-all-start = ((s32[16,256,1]{1,2,0:T(1,128)}), s32[16,256,1]{1,2,0:T(1,128)S(1)}, u32[]{:S(2)}, u32[]{:S(2)}) async-start(s32[16,256,1]{1,2,0:T(1,128)} %bitcast.6), calls=%async_computation | async-start | bytes 32768 | tf_op jit(solution)/shard_map/all_to_all | solution.py:78
  68.6 65.3 %all-to-all-start.1 = ((bf16[16,256,384]{2,1,0:T(8,128)(2,1)}), bf16[16,256,384]{2,1,0:T(8,128)(2,1)S(1)}, u32[]{:S(2)}, u32[]{:S(2)}) async-start(bf16[16,256,384]{2,1,0:T(8,128)(2,1)} %bitcast.10), calls=%async_computation.1 | async-start | bytes 6291456 | tf_op jit(solution)/shard_map/all_to_all | solution.py:77
  155.0 8.1 %copy-start = (bf16[6144,384]{1,0:T(8,128)(2,1)S(1)}, bf16[6144,384]{1,0:T(8,128)(2,1)}, u32[]{:S(2)}) copy-start(bf16[6144,384]{1,0:T(8,128)(2,1)} %scatter_custom_fusion.2) | copy-start | bytes 14155780
  167.6 2.8 copy-start.2
  186.3 6.6 %copy-start.3 = (pred[512,1024]{1,0:T(8,128)(4,1)S(1)}, pred[512,1024]{1,0:T(8,128)(4,1)}, u32[]{:S(2)}) copy-start(pred[512,1024]{1,0:T(8,128)(4,1)} %iota_compare_fusion.1) | copy-start | bytes 1572868
  205.9 4.9 %copy-start.1 = (f32[4,512,512]{1,2,0:T(8,128)S(1)}, f32[4,512,512]{1,2,0:T(8,128)}, u32[]{:S(2)}) copy-start(f32[4,512,512]{1,2,0:T(8,128)} %fusion.37) | copy-start | bytes 12582916
  229.0 38.4 %all-to-all-start.2 = ((bf16[16,256,128]{2,1,0:T(8,128)(2,1)}), bf16[16,256,128]{2,1,0:T(8,128)(2,1)S(1)}, u32[]{:S(2)}, u32[]{:S(2)}) async-start(bf16[16,256,128]{2,1,0:T(8,128)(2,1)} %bitcast.14), calls=%async_computation.2 | async-start | bytes 2097152 | tf_op jit(solution)/shard_map/all_to_all | solution.py:98
where the time goes:
time: 284 us; the launch traced here: 282 us
  local copies, waits for them, and re-layouts  89.7 us (32%)
  waiting for transfers between devices  79.6 us (28%)
  other arithmetic  36.6 us (13%)
  matrix products  28.6 us (10%)
  starting transfers between devices  24.9 us (9%)
  blocking collectives  22.9 us (8%)
    all_to_all x1, waiting for transfers between devices, local(): lax.all_to_all(outgoing, 'seq', split_axis=0, concat_axis=0, tiled=True)  56.7 us
    sub x3, other arithmetic, attend(): expo = jnp.exp(scores - peak)  31.1 us
    all_gather x1, blocking collectives, entering(): gathered = lax.all_gather(part, axis)  22.9 us
    all_to_all x1, waiting for transfers between devices, local(): lax.all_to_all(replies, 'seq', split_axis=0, concat_axis=0, tiled=True)  22.9 us
    scatter x1, local copies, waits for them, and re-layouts, local(): jnp.zeros((pairs_dev * capacity, width), jnp.bfloat16).at[places]  21.1 us
    scatter x1, local copies, waits for them, and re-layouts, local(): outgoing = jnp.zeros((tok * heads, width), jnp.bfloat16).at[position].set...  20.5 us
    scatter x1, local copies, waits for them, and re-layouts, local(): labels = jnp.zeros((tok * heads,), jnp.int32).at[position].set(target)  16.1 us
    all_to_all x1, starting transfers between devices, local(): lax.all_to_all(replies, 'seq', split_axis=0, concat_axis=0, tiled=True)  15.4 us
  transfers between devices with their start and end apart: 3, of which 2 were waited for; matrix products, arithmetic and copies ran while one was open for 8% of the time, Pallas kernels for 0%

commit v1 on v0

v1 whole, which is shorter than its diff:
```python
import functools
import math

import jax
import jax.numpy as jnp
from jax import lax
from jax.experimental import pallas as pl
from jax.experimental.pallas import tpu as pltpu
from jax.sharding import PartitionSpec as P

CLEN = 1024
QB = 256
KB = 512
NEG = -1e30


def attend_kernel(lab_ref, x_ref, o_ref, s_ref, *, head_size, rate):
    block = pl.program_id(0)
    row0 = pl.multiple_of(block * QB, QB)
    tiles = (row0 + QB + KB - 1) // KB
    q = x_ref[pl.ds(row0, QB), :head_size]
    pieces = []
    for part in range(QB // 128):
        lane = lab_ref[pl.ds(block * (QB // 128) + part, 1), :]
        pieces.append(jnp.transpose(jnp.broadcast_to(lane, (128, 128))))
    lab_q = jnp.concatenate(pieces, axis=0)
    rows = row0 + lax.broadcasted_iota(jnp.int32, (QB, 128), 0)
    lanes = lax.broadcasted_iota(jnp.int32, (QB, 128), 1)

    def score(tile, peak):
        col0 = pl.multiple_of(tile * KB, KB)
        k = x_ref[pl.ds(col0, KB), head_size : 2 * head_size]
        s = lax.dot_general(q, k, (((1,), (1,)), ((), ())), preferred_element_type=jnp.float32)
        for part in range(KB // 128):
            lab_k = lab_ref[pl.ds(tile * (KB // 128) + part, 1), :]
            keep = (lab_q == lab_k) & (lanes + (col0 + part * 128) <= rows)
            piece = jnp.where(keep, s[:, part * 128 : (part + 1) * 128], NEG)
            s_ref[:, pl.ds(col0 + part * 128, 128)] = piece
            peak = jnp.maximum(peak, piece)
        return peak

    peak = lax.fori_loop(0, tiles, score, jnp.full((QB, 128), NEG, jnp.float32))
    peak = jnp.broadcast_to(jnp.max(peak, axis=1, keepdims=True), (QB, 128))

    def blend(tile, carry):
        total, acc = carry
        col0 = pl.multiple_of(tile * KB, KB)
        parts = []
        for part in range(KB // 128):
            e = jnp.exp2((s_ref[:, pl.ds(col0 + part * 128, 128)] - peak) * rate)
            total = total + e
            parts.append(e.astype(jnp.bfloat16))
        v = x_ref[pl.ds(col0, KB), 2 * head_size :]
        acc = acc + jnp.dot(jnp.concatenate(parts, axis=1), v, preferred_element_type=jnp.float32)
        return total, acc

    total, acc = lax.fori_loop(
        0,
        tiles,
        blend,
        (jnp.zeros((QB, 128), jnp.float32), jnp.zeros((QB, head_size), jnp.float32)),
    )
    o_ref[...] = (acc / jnp.sum(total, axis=1, keepdims=True)).astype(jnp.bfloat16)


def attend(labels, x, head_size):
    rows, width = x.shape
    rate = math.log2(math.e) / math.sqrt(head_size)
    return pl.pallas_call(
        functools.partial(attend_kernel, head_size=head_size, rate=rate),
        out_shape=jax.ShapeDtypeStruct((rows, head_size), jnp.bfloat16),
        grid=(rows // QB,),
        in_specs=[
            pl.BlockSpec((rows // 128, 128), lambda i: (0, 0)),
            pl.BlockSpec((rows, width), lambda i: (0, 0)),
        ],
        out_specs=pl.BlockSpec((QB, head_size), lambda i: (i, 0)),
        scratch_shapes=[pltpu.VMEM((QB, rows), jnp.float32)],
        compiler_params=pltpu.CompilerParams(
            dimension_semantics=("arbitrary",), vmem_limit_bytes=32 << 20
        ),
        cost_estimate=pl.CostEstimate(
            flops=2 * rows * rows * head_size,
            bytes_accessed=2 * rows * (width + head_size),
            transcendentals=rows * rows // 2,
        ),
        name="attend",
    )(labels, x)


def local(qkv, routes):
    tok, heads, width = qkv.shape
    head_size = width // 3
    nseq = lax.axis_size("seq")
    clusters = nseq * tok // CLEN
    pairs_dev = heads * tok // CLEN
    chunks = max(1, pairs_dev // clusters)
    split = max(1, clusters // pairs_dev)
    share = tok // split

    def exchange(x):
        return lax.all_to_all(x, "seq", split_axis=0, concat_axis=0, tiled=True)

    by_head = jnp.transpose(qkv, (1, 0, 2))
    labels = jnp.transpose(routes)
    if split > 1:
        group = labels // pairs_dev
        member = group[:, :, None] == jnp.arange(split, dtype=jnp.int32)[None, None, :]
        rank = jnp.cumsum(member.astype(jnp.int32), axis=1) - 1
        slot = group * share + jnp.sum(jnp.where(member, rank, 0), axis=2)
        pick = slot[:, None, :] == jnp.arange(tok, dtype=jnp.int32)[None, :, None]
        by_head = jnp.einsum(
            "hst,htd->hsd", pick.astype(jnp.bfloat16), by_head, preferred_element_type=jnp.float32
        ).astype(jnp.bfloat16)
        labels = jnp.sum(jnp.where(pick, labels[:, None, :], 0), axis=2)

    by_head = by_head.reshape(nseq, chunks, share, width)
    labels = exchange(labels.reshape(nseq, chunks, share))
    outs = []
    for chunk in range(chunks):
        rows = exchange(by_head[:, chunk]).reshape(nseq * share, width)
        lab = labels[:, chunk].reshape(nseq * share // 128, 128)
        out = attend(lab, rows, head_size)
        outs.append(exchange(out.reshape(nseq, share, head_size)))
    back = jnp.stack(outs, axis=1).reshape(heads, tok, head_size)
    if split > 1:
        back = jnp.einsum(
            "hst,hsd->htd", pick.astype(jnp.bfloat16), back, preferred_element_type=jnp.float32
        ).astype(jnp.bfloat16)
    return jnp.transpose(back, (1, 0, 2))


def solution(mesh):
    placed = (P(("groups", "seq"), None, None), P(("groups", "seq"), None))
    return jax.shard_map(
        local,
        mesh=mesh,
        in_specs=placed,
        out_specs=P(("groups", "seq"), None, None),
        check_vma=False,
    )
```

time: 284 us -> 146 us (0.51)
  local copies, waits for them, and re-layouts: 89.7 us -> 20.5 us
  other arithmetic: 36.6 us -> 0.1 us
  waiting for transfers between devices: 79.6 us -> 46.2 us
  matrix products: 28.6 us -> 0 us
  Pallas kernels: 0 us -> 27.4 us
  starting transfers between devices: 24.9 us -> 31.6 us
  blocking collectives: 22.9 us -> 19.5 us
    scatter x3 -> x0, local copies, waits for them, and re-layouts: 57.8 us -> none  [the longest x1 21.1 us: local(): jnp.zeros((pairs_dev * capacity, width), jnp.bfloat16).at[places]]
    all_to_all x3 -> x4, waiting for transfers between devices: 79.6 us -> 46.2 us  [exchange(): return lax.all_to_all(x, 'seq', split_axis=0, concat_axis=0, tiled=True)]
    sub x4 -> x0, other arithmetic: 31.1 us -> none  [the longest x3 31.1 us: attend(): expo = jnp.exp(scores - peak)]
    gather x2 -> x0, local copies, waits for them, and re-layouts: 30.1 us -> none  [the longest x1 15 us: local(): replies = flat_results[places]]
    dot_general x7 -> x0, matrix products: 28.6 us -> none  [the longest x3 15.3 us: attend(): jnp.einsum('pqd,pkd->pqk', queries, keys, preferred_element_type=jnp.floa...]
    pallas_call x0 -> x2, Pallas kernels: none -> 27.4 us  [attend(): pl.pallas_call(functools.partial(attend_kernel, head_size=head_size, rate...]
    all_gather x1 -> x0, blocking collectives: 22.9 us -> none  [entering(): gathered = lax.all_gather(part, axis)]
    all_to_all x0 -> x1, blocking collectives: none -> 19.5 us  [exchange(): return lax.all_to_all(x, 'seq', split_axis=0, concat_axis=0, tiled=True)]
  transfers between devices with their start and end apart: 3 -> 4, of which waited for: 2 -> 3; matrix products, arithmetic and copies ran while one was open for 8% -> 12% of each run, Pallas kernels for 0% -> 19%
where the time goes in v1:
time: 146 us; the launch traced here: 145 us
  waiting for transfers between devices  46.2 us (32%)
  starting transfers between devices  31.6 us (22%)
  Pallas kernels  27.4 us (19%)
  local copies, waits for them, and re-layouts  20.5 us (14%)
  blocking collectives  19.5 us (13%)
    all_to_all x4, waiting for transfers between devices, exchange(): return lax.all_to_all(x, 'seq', split_axis=0, concat_axis=0, tiled=True)  46.2 us
    all_to_all x4, starting transfers between devices, exchange(): return lax.all_to_all(x, 'seq', split_axis=0, concat_axis=0, tiled=True)  31.6 us
    pallas_call x2, Pallas kernels, attend(): pl.pallas_call(functools.partial(attend_kernel, head_size=head_size, rate...  27.4 us
    all_to_all x1, blocking collectives, exchange(): return lax.all_to_all(x, 'seq', split_axis=0, concat_axis=0, tiled=True)  19.5 us
    unnamed x4, local copies, waits for them, and re-layouts  6.85 us
    reshape x1, local copies, waits for them, and re-layouts, local(): by_head = by_head.reshape(nseq, chunks, share, width)  6.09 us
    slice x1, local copies, waits for them, and re-layouts, local(): rows = exchange(by_head[:, chunk]).reshape(nseq * share, width)  5.47 us
  transfers between devices with their start and end apart: 4, of which 3 were waited for; matrix products, arithmetic and copies ran while one was open for 12% of the time, Pallas kernels for 19%

profile of v1, /device:TPU:0, one launch (start us, length us, event | category | flops | bytes accessed | tf_op | source)
XLA Modules:
  0.0 145.3 jit_solution(4890654794647941726)
XLA Ops:
  0.0 7.4 %all-to-all-start = ((s32[16,2,128]{2,1,0:T(2,128)}), s32[16,2,128]{2,1,0:T(2,128)S(1)}, u32[]{:S(2)}, u32[]{:S(2)}) async-start(s32[16,2,128]{2,1,0:T(2,128)} %bitcast.37), calls=%async_computation | async-start | bytes 32768 | tf_op jit(solution)/shard_map/all_to_all | solution.py:102
  7.4 6.1 %reshape.22 = bf16[16,2,128,384]{3,1,0,2:T(2,128)(2,1)S(1)} reshape(bf16[32,128,384]{2,0,1:T(8,128)(2,1)} %bitcast.34) | data formatting | bytes 6291456 | tf_op jit(solution)/shard_map/reshape | solution.py:117
  13.5 5.5 %fusion = (bf16[16,1,128,384]{3,1,0,2:T(2,128)(2,1)}, bf16[16,1,128,384]{3,1,0,2:T(2,128)(2,1)S(1)}) fusion(bf16[16,2,128,384]{3,1,0,2:T(2,128)(2,1)S(1)} %reshape.22), kind=kLoop, calls=%fused_computation.3 | loop fusion | bytes 6291456 | tf_op jit(solution)/shard_map/slice | solution.py:121
  18.9 2.1 %copy.21 = bf16[16,1,128,384]{3,2,0,1:T(8,128)(2,1)} copy(bf16[16,1,128,384]{3,1,0,2:T(2,128)(2,1)S(1)} %get-tuple-element.6) | data formatting | bytes 3145728
  21.0 0.0 all-to-all-done
  21.0 6.0 %all-to-all-start.3 = ((bf16[16,128,384]{2,1,0:T(8,128)(2,1)}), bf16[16,128,384]{2,1,0:T(8,128)(2,1)S(1)}, u32[]{:S(2)}, u32[]{:S(2)}) async-start(bf16[16,128,384]{2,1,0:T(8,128)(2,1)} %bitcast.25), calls=%async_computation.3 | async-start | bytes 3145728 | tf_op jit(solution)/shard_map/all_to_all | solution.py:102
  27.0 4.0 %copy.22 = bf16[16,1,128,384]{3,2,0,1:T(8,128)(2,1)} copy(bf16[16,1,128,384]{3,1,0,2:T(2,128)(2,1)} %get-tuple-element.5) | data formatting | bytes 3145728
  31.0 28.0 %all-to-all-done.3 = bf16[16,128,384]{2,1,0:T(8,128)(2,1)S(1)} async-done(((bf16[16,128,384]{2,1,0:T(8,128)(2,1)}), bf16[16,128,384]{2,1,0:T(8,128)(2,1)S(1)}, u32[]{:S(2)}, u32[]{:S(2)}) %all-to-all-start.3) | async-done | bytes 1572896 | tf_op jit(solution)/shard_map/all_to_all | solution.py:102
  59.0 9.1 %all-to-all-start.1 = ((bf16[16,128,384]{2,1,0:T(8,128)(2,1)}), bf16[16,128,384]{2,1,0:T(8,128)(2,1)S(1)}, u32[]{:S(2)}, u32[]{:S(2)}) async-start(bf16[16,128,384]{2,1,0:T(8,128)(2,1)} %bitcast.33), calls=%async_computation.1 | async-start | bytes 3145728 | tf_op jit(solution)/shard_map/all_to_all | solution.py:102
  68.1 13.7 %attend.3 = bf16[2048,128]{1,0:T(8,128)(2,1)S(1)} custom-call(s32[16,128]{1,0:T(8,128)S(1)} %bitcast.32, bf16[2048,384]{1,0:T(8,128)(2,1)S(1)} %bitcast.28), custom_call_target="tpu_custom_call" | custom-call | flops 1073741824 | bytes 2097152 | tf_op jit(solution)/shard_map/attend/pallas_call | solution.py:69
  81.8 0.0 copy-start
  81.9 0.8 copy-done
  82.6 17.5 %all-to-all-done.1 = bf16[16,128,384]{2,1,0:T(8,128)(2,1)S(1)} async-done(((bf16[16,128,384]{2,1,0:T(8,128)(2,1)}), bf16[16,128,384]{2,1,0:T(8,128)(2,1)S(1)}, u32[]{:S(2)}, u32[]{:S(2)}) %all-to-all-start.1) | async-done | bytes 1572896 | tf_op jit(solution)/shard_map/all_to_all | solution.py:102
  100.1 9.1 %all-to-all-start.4 = ((bf16[16,128,128]{2,1,0:T(8,128)(2,1)}), bf16[16,128,128]{2,1,0:T(8,128)(2,1)S(1)}, u32[]{:S(2)}, u32[]{:S(2)}) async-start(bf16[16,128,128]{2,1,0:T(8,128)(2,1)} %bitcast.29), calls=%async_computation.4 | async-start | bytes 1048576 | tf_op jit(solution)/shard_map/all_to_all | solution.py:102
  109.2 13.7 %attend.2 = bf16[2048,128]{1,0:T(8,128)(2,1)S(1)} custom-call(s32[16,128]{1,0:T(8,128)S(1)} %bitcast.31, bf16[2048,384]{1,0:T(8,128)(2,1)S(1)} %bitcast.27), custom_call_target="tpu_custom_call" | custom-call | flops 1073741824 | bytes 2097152 | tf_op jit(solution)/shard_map/attend/pallas_call | solution.py:69
  122.9 0.8 all-to-all-done.4
  123.7 19.5 %all_to_all.25 = bf16[16,128,128]{2,1,0:T(8,128)(2,1)S(1)} all-to-all(bf16[16,128,128]{2,1,0:T(8,128)(2,1)S(1)} %bitcast.30), channel_id=1, replica_groups=mesh['groups'=2,'seq'=16] {'seq'}, dimensions={0} | all-to-all | bytes 1048576 | tf_op jit(solution)/shard_map/all_to_all | solution.py:102
  143.2 0.1 pad_maximum_fusion
  143.3 2.0 %copy.14 = bf16[16,2,128,128]{3,1,0,2:T(2,128)(2,1)} copy(bf16[16,2,128,128]{3,2,0,1:T(8,128)(2,1)S(1)} %pad_maximum_fusion) | data formatting | bytes 2097152 | tf_op jit(solution)/shard_map/stack | solution.py:125
  (1 shorter events, 0.0 us)
Async XLA Ops:
  0.0 21.0 %all-to-all-start = ((s32[16,2,128]{2,1,0:T(2,128)}), s32[16,2,128]{2,1,0:T(2,128)S(1)}, u32[]{:S(2)}, u32[]{:S(2)}) async-start(s32[16,2,128]{2,1,0:T(2,128)} %bitcast.37), calls=%async_computation | async-start | bytes 32768 | tf_op jit(solution)/shard_map/all_to_all | solution.py:102
  21.0 38.0 %all-to-all-start.3 = ((bf16[16,128,384]{2,1,0:T(8,128)(2,1)}), bf16[16,128,384]{2,1,0:T(8,128)(2,1)S(1)}, u32[]{:S(2)}, u32[]{:S(2)}) async-start(bf16[16,128,384]{2,1,0:T(8,128)(2,1)} %bitcast.25), calls=%async_computation.3 | async-start | bytes 3145728 | tf_op jit(solution)/shard_map/all_to_all | solution.py:102
  59.0 41.1 %all-to-all-start.1 = ((bf16[16,128,384]{2,1,0:T(8,128)(2,1)}), bf16[16,128,384]{2,1,0:T(8,128)(2,1)S(1)}, u32[]{:S(2)}, u32[]{:S(2)}) async-start(bf16[16,128,384]{2,1,0:T(8,128)(2,1)} %bitcast.33), calls=%async_computation.1 | async-start | bytes 3145728 | tf_op jit(solution)/shard_map/all_to_all | solution.py:102
  81.8 0.8 copy-start
  100.1 23.6 %all-to-all-start.4 = ((bf16[16,128,128]{2,1,0:T(8,128)(2,1)}), bf16[16,128,128]{2,1,0:T(8,128)(2,1)S(1)}, u32[]{:S(2)}, u32[]{:S(2)}) async-start(bf16[16,128,128]{2,1,0:T(8,128)(2,1)} %bitcast.29), calls=%async_computation.4 | async-start | bytes 1048576 | tf_op jit(solution)/shard_map/all_to_all | solution.py:102

commit v2 on v1

v2 whole, which is shorter than its diff:
```python
import functools
import math

import jax
import jax.numpy as jnp
from jax import lax
from jax.experimental import pallas as pl
from jax.experimental.pallas import tpu as pltpu
from jax.sharding import PartitionSpec as P

CLEN = 1024
QB = 256
NEG = -1e30


def pack_kernel(x_ref, lab_ref, o_ref, *, chunks):
    tok, octet, width = x_ref.shape
    parts = width // 128
    turned = jnp.swapaxes(x_ref[...].astype(jnp.float32), 0, 1).astype(jnp.bfloat16)
    for dst in range(octet // chunks):
        for chunk in range(chunks):
            head = dst * chunks + chunk
            for part in range(parts):
                o_ref[dst, pl.ds((chunk * parts + part) * tok, tok), :] = turned[
                    head, :, part * 128 : (part + 1) * 128
                ]
        labels = lab_ref[dst * chunks : (dst + 1) * chunks, :]
        pad = jnp.zeros((8 - chunks, 128), jnp.float32)
        o_ref[dst, pl.ds(chunks * parts * tok, 8), :] = jnp.concatenate(
            [labels.astype(jnp.float32), pad], axis=0
        ).astype(jnp.bfloat16)


def pack(qkv, labels, chunks):
    tok, heads, width = qkv.shape
    rows = chunks * (width // 128) * tok + 8
    return pl.pallas_call(
        functools.partial(pack_kernel, chunks=chunks),
        out_shape=jax.ShapeDtypeStruct((heads // chunks, rows, 128), jnp.bfloat16),
        grid=(heads // 8,),
        in_specs=[
            pl.BlockSpec((tok, 8, width), lambda i: (0, i, 0)),
            pl.BlockSpec((8, 128), lambda i: (i, 0)),
        ],
        out_specs=pl.BlockSpec((8 // chunks, rows, 128), lambda i: (i, 0, 0)),
        compiler_params=pltpu.CompilerParams(vmem_limit_bytes=32 << 20),
        name="pack",
    )(qkv, labels)


def unpack_kernel(x_ref, o_ref):
    o_ref[...] = jnp.swapaxes(x_ref[...].astype(jnp.float32), 0, 1).astype(jnp.bfloat16)


def unpack(back):
    heads, tok, head_size = back.shape
    return pl.pallas_call(
        unpack_kernel,
        out_shape=jax.ShapeDtypeStruct((tok, heads, head_size), jnp.bfloat16),
        grid=(heads // 8,),
        in_specs=[pl.BlockSpec((8, tok, head_size), lambda i: (i, 0, 0))],
        out_specs=pl.BlockSpec((tok, 8, head_size), lambda i: (0, i, 0)),
        name="unpack",
    )(back)


def attend_kernel(lab_ref, x_ref, o_ref, *, share, rate):
    chunk = pl.program_id(0)
    nseq = x_ref.shape[0]
    rows = nseq * share
    head_size = x_ref.shape[2]
    base = pl.multiple_of(chunk * 3 * share, share)

    def rows_of(part, first, count):
        piece = x_ref[
            first // share : (first + count) // share, pl.ds(base + part * share, share), :
        ]
        return piece.reshape(count, head_size)

    ramp = lax.broadcasted_iota(jnp.int32, (QB, QB), 1) <= lax.broadcasted_iota(
        jnp.int32, (QB, QB), 0
    )
    for block in range(rows // QB):
        row0 = block * QB
        stop = row0 + QB
        q = rows_of(0, row0, QB)
        lab_q = jnp.concatenate(
            [
                jnp.transpose(jnp.broadcast_to(lab_ref[0, i : i + 1, :], (128, 128)))
                for i in range(row0 // 128, stop // 128)
            ],
            axis=0,
        )
        s = lax.dot_general(
            q, rows_of(1, 0, stop), (((1,), (1,)), ((), ())), preferred_element_type=jnp.float32
        )
        pieces = []
        for i in range(stop // 128):
            keep = lab_q == lab_ref[0, i : i + 1, :]
            if i * 128 >= row0:
                keep = keep & ramp[:, i * 128 - row0 : i * 128 - row0 + 128]
            pieces.append(jnp.where(keep, s[:, i * 128 : (i + 1) * 128], NEG))
        peak = functools.reduce(jnp.maximum, pieces)
        peak = jnp.broadcast_to(jnp.max(peak, axis=1, keepdims=True), (QB, 128))
        pieces = [jnp.exp2((piece - peak) * rate) for piece in pieces]
        total = jnp.sum(functools.reduce(jnp.add, pieces), axis=1, keepdims=True)
        weights = jnp.concatenate([piece.astype(jnp.bfloat16) for piece in pieces], axis=1)
        out = jnp.dot(weights, rows_of(2, 0, stop), preferred_element_type=jnp.float32) / total
        o_ref[row0 // share : stop // share] = out.astype(jnp.bfloat16).reshape(
            QB // share, share, head_size
        )


def attend(labels, x, chunks, share):
    nseq, _, head_size = x.shape
    rows = nseq * share
    rate = math.log2(math.e) / math.sqrt(head_size)
    return pl.pallas_call(
        functools.partial(attend_kernel, share=share, rate=rate),
        out_shape=jax.ShapeDtypeStruct((nseq, chunks * share, head_size), jnp.bfloat16),
        grid=(chunks,),
        in_specs=[
            pl.BlockSpec((1, rows // 128, 128), lambda c: (c, 0, 0)),
            pl.BlockSpec(memory_space=pltpu.VMEM),
        ],
        out_specs=pl.BlockSpec((nseq, share, head_size), lambda c: (0, c, 0)),
        compiler_params=pltpu.CompilerParams(
            dimension_semantics=("arbitrary",), vmem_limit_bytes=40 << 20
        ),
        name="attend",
    )(labels, x)


def local(qkv, routes):
    tok, heads, width = qkv.shape
    head_size = width // 3
    nseq = lax.axis_size("seq")
    clusters = nseq * tok // CLEN
    pairs_dev = heads * tok // CLEN
    chunks = max(1, pairs_dev // clusters)
    split = max(1, clusters // pairs_dev)
    share = tok // split

    def exchange(x):
        return lax.all_to_all(x, "seq", split_axis=0, concat_axis=0, tiled=True)

    labels = jnp.transpose(routes)
    if split == 1:
        rows = exchange(pack(qkv, labels, chunks))
    else:
        group = labels // pairs_dev
        member = group[:, :, None] == jnp.arange(split, dtype=jnp.int32)[None, None, :]
        rank = jnp.cumsum(member.astype(jnp.int32), axis=1) - 1
        slot = group * share + jnp.sum(jnp.where(member, rank, 0), axis=2)
        pick = slot[:, None, :] == jnp.arange(tok, dtype=jnp.int32)[None, :, None]
        moved = jnp.einsum(
            "hst,thd->hsd", pick.astype(jnp.bfloat16), qkv, preferred_element_type=jnp.float32
        ).astype(jnp.bfloat16)
        labels = jnp.sum(jnp.where(pick, labels[:, None, :], 0), axis=2)
        moved = moved.reshape(nseq, share, 3, head_size)
        moved = jnp.transpose(moved, (0, 2, 1, 3)).reshape(nseq, 3 * share, head_size)
        extra = labels.reshape(nseq, 1, share).astype(jnp.bfloat16)
        extra = jnp.pad(extra, ((0, 0), (0, 7), (0, head_size - share)))
        rows = exchange(jnp.concatenate([moved, extra], axis=1))
    first = chunks * 3 * share
    arrived = rows[:, first : first + chunks, :share].astype(jnp.int32)
    arrived = jnp.transpose(arrived, (1, 0, 2)).reshape(chunks, nseq * share // 128, 128)
    back = exchange(attend(arrived, rows, chunks, share)).reshape(heads, tok, head_size)
    if split > 1:
        back = jnp.einsum(
            "hst,hsd->htd", pick.astype(jnp.bfloat16), back, preferred_element_type=jnp.float32
        ).astype(jnp.bfloat16)
    return unpack(back)


def solution(mesh):
    placed = (P(("groups", "seq"), None, None), P(("groups", "seq"), None))
    return jax.shard_map(
        local,
        mesh=mesh,
        in_specs=placed,
        out_specs=P(("groups", "seq"), None, None),
        check_vma=False,
    )
```

time: 146 us -> 128 us (0.88)
  blocking collectives: 19.5 us -> 108 us
  waiting for transfers between devices: 46.2 us -> 0 us
  starting transfers between devices: 31.6 us -> 0 us
  local copies, waits for them, and re-layouts: 20.5 us -> 2.61 us
  Pallas kernels: 27.4 us -> 16.2 us
    all_to_all x1 -> x2, blocking collectives: 19.5 us -> 108 us  [exchange(): return lax.all_to_all(x, 'seq', split_axis=0, concat_axis=0, tiled=True)]
    all_to_all x4 -> x0, waiting for transfers between devices: 46.2 us -> none  [exchange(): return lax.all_to_all(x, 'seq', split_axis=0, concat_axis=0, tiled=True)]
    all_to_all x4 -> x0, starting transfers between devices: 31.6 us -> none  [exchange(): return lax.all_to_all(x, 'seq', split_axis=0, concat_axis=0, tiled=True)]
    pallas_call x2 -> x3, Pallas kernels: 27.4 us -> 16.2 us  [the longest x1 10.6 us: attend(): pl.pallas_call(functools.partial(attend_kernel, share=share, rate=rate),...]
    reshape x1 -> x0, local copies, waits for them, and re-layouts: 6.09 us -> none  [local(): by_head = by_head.reshape(nseq, chunks, share, width)]
    slice x2 -> x0, local copies, waits for them, and re-layouts: 5.48 us -> none  [the longest x1 5.47 us: local(): rows = exchange(by_head[:, chunk]).reshape(nseq * share, width)]
    unnamed x4, local copies, waits for them, and re-layouts: 6.85 us -> 2.61 us
    another operation x1 -> x0, local copies, waits for them, and re-layouts: 2.05 us -> none  [local(): back = jnp.stack(outs, axis=1).reshape(heads, tok, head_size)]
  transfers between devices with their start and end apart: 4 -> 0, of which waited for: 3 -> 0; matrix products, arithmetic and copies ran while one was open for 12% -> 0% of each run, Pallas kernels for 19% -> 0%
where the time goes in v2:
time: 128 us; the launch traced here: 127 us
  blocking collectives  108 us (84%)
  Pallas kernels  16.2 us (13%)
  local copies, waits for them, and re-layouts  2.61 us (2%)
    all_to_all x2, blocking collectives, exchange(): return lax.all_to_all(x, 'seq', split_axis=0, concat_axis=0, tiled=True)  108 us
    pallas_call x1, Pallas kernels, attend(): pl.pallas_call(functools.partial(attend_kernel, share=share, rate=rate),...  10.6 us
    pallas_call x1, Pallas kernels, unpack(): pl.pallas_call(unpack_kernel, out_shape=jax.ShapeDtypeStruct((tok, heads,...  3.55 us
    unnamed x4, local copies, waits for them, and re-layouts  2.61 us

profile of v2, /device:TPU:0, one launch (start us, length us, event | category | flops | bytes accessed | tf_op | source)
XLA Modules:
  0.0 127.1 jit_solution(15031621874119349933)
XLA Ops:
  0.0 0.0 copy-start
  0.0 1.9 %copy-done = bf16[128,32,384]{2,1,0:T(8,128)(2,1)S(1)} copy-done((bf16[128,32,384]{2,1,0:T(8,128)(2,1)S(1)}, bf16[128,32,384]{2,1,0:T(8,128)(2,1)}, u32[]{:S(2)}) %copy-start) | copy-done | bytes 3145752
  1.9 0.0 copy-start.1
  1.9 0.7 copy-done.1
  2.6 2.1 %pack.1 = bf16[16,776,128]{2,1,0:T(8,128)(2,1)S(1)} custom-call(bf16[128,32,384]{2,1,0:T(8,128)(2,1)S(1)} %copy-done, s32[32,128]{1,0:T(8,128)S(1)} %bitcast.4), custom_call_target="tpu_custom_call" | custom-call | tf_op jit(solution)/shard_map/pack/pallas_call | solution.py:37
  4.7 80.1 %all_to_all.10.x_ref = bf16[16,776,128]{2,1,0:T(8,128)(2,1)S(1)} all-to-all(bf16[16,776,128]{2,1,0:T(8,128)(2,1)S(1)} %pack.1), channel_id=1, replica_groups=mesh['groups'=2,'seq'=16] {'seq'}, dimensions={0} | all-to-all | bytes 6356992 | tf_op jit(solution)/shard_map/all_to_all | solution.py:145
  84.8 10.6 %attend.1 = bf16[16,256,128]{2,1,0:T(8,128)(2,1)S(1)} custom-call(s32[2,16,128]{2,1,0:T(8,128)S(1)} %copy.3.lab_ref, bf16[16,776,128]{2,1,0:T(8,128)(2,1)S(1)} %all_to_all.10.x_ref), custom_call_target="tpu_custom_call" | custom-call | tf_op jit(solution)/shard_map/attend/pallas_call | solution.py:118
  95.4 28.1 %all_to_all.11 = bf16[16,256,128]{2,1,0:T(8,128)(2,1)} all-to-all(bf16[16,256,128]{2,1,0:T(8,128)(2,1)S(1)} %attend.1), channel_id=1, replica_groups=mesh['groups'=2,'seq'=16] {'seq'}, dimensions={0} | all-to-all | bytes 2097152 | tf_op jit(solution)/shard_map/all_to_all | solution.py:145
  123.5 3.5 %unpack.1 = bf16[128,32,128]{2,1,0:T(8,128)(2,1)} custom-call(bf16[32,128,128]{2,1,0:T(8,128)(2,1)} %bitcast.5), custom_call_target="tpu_custom_call" | custom-call | tf_op jit(solution)/shard_map/unpack/pallas_call | solution.py:57
  (2 shorter events, 0.0 us)
Async XLA Ops:
  0.0 1.9 %copy-start = (bf16[128,32,384]{2,1,0:T(8,128)(2,1)S(1)}, bf16[128,32,384]{2,1,0:T(8,128)(2,1)}, u32[]{:S(2)}) copy-start(bf16[128,32,384]{2,1,0:T(8,128)(2,1)} %x_ref.1) | copy-start | bytes 9437188
  1.9 0.7 copy-start.1

commit v3 on v2

v3 whole, which is shorter than its diff:
```python
import functools
import math

import jax
import jax.numpy as jnp
from jax import lax
from jax.experimental import pallas as pl
from jax.experimental.pallas import tpu as pltpu
from jax.sharding import PartitionSpec as P

CLEN = 1024
QB = 256
STEP = 64
NEG = -1e30


def pack_kernel(x_ref, lab_ref, o_ref, *, chunks):
    tok, heads, width = x_ref.shape
    parts = width // 128
    pad = jnp.zeros((8 - chunks, 128), jnp.float32)
    for dst in range(heads // chunks):
        labels = lab_ref[dst * chunks : (dst + 1) * chunks, :]
        o_ref[dst, pl.ds(chunks * parts * tok, 8), :] = jnp.concatenate(
            [labels.astype(jnp.float32), pad], axis=0
        ).astype(jnp.bfloat16)
    for first in range(0, tok, 32):
        piece = x_ref[first : first + 32].astype(jnp.float32)
        turned = jnp.swapaxes(piece, 0, 1).astype(jnp.bfloat16)
        for head in range(heads):
            for part in range(parts):
                row = (head % chunks * parts + part) * tok + first
                o_ref[head // chunks, row : row + 32, :] = turned[
                    head, :, part * 128 : (part + 1) * 128
                ]


def pack(qkv, labels, chunks):
    tok, heads, width = qkv.shape
    rows = chunks * (width // 128) * tok + 8
    whole = pl.BlockSpec(memory_space=pltpu.VMEM)
    return pl.pallas_call(
        functools.partial(pack_kernel, chunks=chunks),
        out_shape=jax.ShapeDtypeStruct((heads // chunks, rows, 128), jnp.bfloat16),
        in_specs=[whole, whole],
        out_specs=whole,
        compiler_params=pltpu.CompilerParams(vmem_limit_bytes=32 << 20),
        name="pack",
    )(qkv, labels)


def unpack_kernel(x_ref, o_ref):
    o_ref[...] = jnp.swapaxes(x_ref[...].astype(jnp.float32), 0, 1).astype(jnp.bfloat16)


def unpack(back):
    heads, tok, head_size = back.shape
    return pl.pallas_call(
        unpack_kernel,
        out_shape=jax.ShapeDtypeStruct((tok, heads, head_size), jnp.bfloat16),
        grid=(tok // STEP,),
        in_specs=[pl.BlockSpec((heads, STEP, head_size), lambda i: (0, i, 0))],
        out_specs=pl.BlockSpec((STEP, heads, head_size), lambda i: (i, 0, 0)),
        name="unpack",
    )(back)


def attend_kernel(lab_ref, x_ref, o_ref, v_ref, *, share, rate):
    nseq, _, head_size = x_ref.shape
    chunks = lab_ref.shape[0]
    rows = nseq * share
    ramp = lax.broadcasted_iota(jnp.int32, (QB, QB), 1) <= lax.broadcasted_iota(
        jnp.int32, (QB, QB), 0
    )

    def rows_of(chunk, part, first, count):
        base = (chunk * 3 + part) * share
        piece = x_ref[first // share : (first + count) // share, base : base + share, :]
        return piece.reshape(count, head_size)

    for chunk in range(chunks):
        v_ref[chunk, :, :head_size] = rows_of(chunk, 2, 0, rows)
        v_ref[chunk, :, head_size:] = jnp.ones((rows, 128), jnp.bfloat16)

    def score(chunk, block):
        return lax.dot_general(
            rows_of(chunk, 0, block * QB, QB),
            rows_of(chunk, 1, 0, (block + 1) * QB),
            (((1,), (1,)), ((), ())),
            preferred_element_type=jnp.float32,
        )

    def weigh(chunk, block, s):
        row0 = block * QB
        stop = row0 + QB
        lab_q = jnp.concatenate(
            [
                jnp.transpose(jnp.broadcast_to(lab_ref[chunk, i : i + 1, :], (128, 128)))
                for i in range(row0 // 128, stop // 128)
            ],
            axis=0,
        )
        pieces = []
        for i in range(stop // 128):
            keep = lab_q == lab_ref[chunk, i : i + 1, :]
            if i * 128 >= row0:
                keep = keep & ramp[:, i * 128 - row0 : i * 128 - row0 + 128]
            pieces.append(jnp.where(keep, s[:, i * 128 : (i + 1) * 128], NEG))
        peak = functools.reduce(jnp.maximum, pieces)
        peak = jnp.broadcast_to(jnp.max(peak, axis=1, keepdims=True), (QB, 128))
        pieces = [jnp.exp2((piece - peak) * rate).astype(jnp.bfloat16) for piece in pieces]
        return jnp.concatenate(pieces, axis=1)

    def blend(chunk, block, weights):
        row0 = block * QB
        stop = row0 + QB
        both = jnp.dot(weights, v_ref[chunk, :stop, :], preferred_element_type=jnp.float32)
        out = both[:, :head_size] / both[:, head_size:]
        o_ref[row0 // share : stop // share, chunk * share : (chunk + 1) * share] = out.astype(
            jnp.bfloat16
        ).reshape(QB // share, share, head_size)

    blocks = rows // QB
    tasks = [
        (chunk, step if chunk % 2 == 0 else blocks - 1 - step)
        for step in range(blocks)
        for chunk in range(chunks)
    ]
    ahead = score(*tasks[0])
    behind = None
    for place, task in enumerate(tasks):
        s = ahead
        if place + 1 < len(tasks):
            ahead = score(*tasks[place + 1])
        weights = weigh(*task, s)
        if behind is not None:
            blend(*behind)
        behind = (*task, weights)
    blend(*behind)


def attend(labels, x, chunks, share):
    nseq, _, head_size = x.shape
    rows = nseq * share
    rate = math.log2(math.e) / math.sqrt(head_size)
    whole = pl.BlockSpec(memory_space=pltpu.VMEM)
    return pl.pallas_call(
        functools.partial(attend_kernel, share=share, rate=rate),
        out_shape=jax.ShapeDtypeStruct((nseq, chunks * share, head_size), jnp.bfloat16),
        in_specs=[whole, whole],
        out_specs=whole,
        scratch_shapes=[pltpu.VMEM((chunks, rows, head_size + 128), jnp.bfloat16)],
        compiler_params=pltpu.CompilerParams(vmem_limit_bytes=40 << 20),
        name="attend",
    )(labels, x)


def local(qkv, routes):
    tok, heads, width = qkv.shape
    head_size = width // 3
    nseq = lax.axis_size("seq")
    clusters = nseq * tok // CLEN
    pairs_dev = heads * tok // CLEN
    chunks = max(1, pairs_dev // clusters)
    split = max(1, clusters // pairs_dev)
    share = tok // split

    def exchange(x):
        return lax.all_to_all(x, "seq", split_axis=0, concat_axis=0, tiled=True)

    labels = jnp.transpose(routes)
    if split == 1:
        rows = exchange(pack(qkv, labels, chunks))
    else:
        group = labels // pairs_dev
        member = group[:, :, None] == jnp.arange(split, dtype=jnp.int32)[None, None, :]
        rank = jnp.cumsum(member.astype(jnp.int32), axis=1) - 1
        slot = group * share + jnp.sum(jnp.where(member, rank, 0), axis=2)
        pick = slot[:, None, :] == jnp.arange(tok, dtype=jnp.int32)[None, :, None]
        moved = jnp.einsum(
            "hst,thd->hsd", pick.astype(jnp.bfloat16), qkv, preferred_element_type=jnp.float32
        ).astype(jnp.bfloat16)
        labels = jnp.sum(jnp.where(pick, labels[:, None, :], 0), axis=2)
        moved = moved.reshape(nseq, share, 3, head_size)
        moved = jnp.transpose(moved, (0, 2, 1, 3)).reshape(nseq, 3 * share, head_size)
        extra = labels.reshape(nseq, 1, share).astype(jnp.bfloat16)
        extra = jnp.pad(extra, ((0, 0), (0, 7), (0, head_size - share)))
        rows = exchange(jnp.concatenate([moved, extra], axis=1))
    first = chunks * 3 * share
    arrived = rows[:, first : first + chunks, :share].astype(jnp.int32)
    arrived = jnp.transpose(arrived, (1, 0, 2)).reshape(chunks, nseq * share // 128, 128)
    back = exchange(attend(arrived, rows, chunks, share)).reshape(heads, tok, head_size)
    if split > 1:
        back = jnp.einsum(
            "hst,hsd->htd", pick.astype(jnp.bfloat16), back, preferred_element_type=jnp.float32
        ).astype(jnp.bfloat16)
    return unpack(back)


def solution(mesh):
    placed = (P(("groups", "seq"), None, None), P(("groups", "seq"), None))
    return jax.shard_map(
        local,
        mesh=mesh,
        in_specs=placed,
        out_specs=P(("groups", "seq"), None, None),
        check_vma=False,
    )
```

time: 128 us -> 122 us (0.953)
  Pallas kernels: 16.2 us -> 10.8 us
    pallas_call x1, Pallas kernels: 10.6 us -> 6.8 us  [attend(): pl.pallas_call(functools.partial(attend_kernel, share=share, rate=rate),...]
where the time goes in v3:
time: 122 us
  blocking collectives  108 us (89%)
  Pallas kernels  10.8 us (9%)
  local copies, waits for them, and re-layouts  2.61 us (2%)
    all_to_all x2, blocking collectives, exchange(): return lax.all_to_all(x, 'seq', split_axis=0, concat_axis=0, tiled=True)  108 us
    pallas_call x1, Pallas kernels, attend(): pl.pallas_call(functools.partial(attend_kernel, share=share, rate=rate),...  6.8 us
    unnamed x4, local copies, waits for them, and re-layouts  2.61 us

profile of v3, /device:TPU:0, one launch (start us, length us, event | category | flops | bytes accessed | tf_op | source)
XLA Modules:
  0.0 121.6 jit_solution(7047071742126665407)
XLA Ops:
  0.0 0.0 copy-start
  0.0 1.9 %copy-done = bf16[128,32,384]{2,1,0:T(8,128)(2,1)S(1)} copy-done((bf16[128,32,384]{2,1,0:T(8,128)(2,1)S(1)}, bf16[128,32,384]{2,1,0:T(8,128)(2,1)}, u32[]{:S(2)}) %copy-start) | copy-done | bytes 3145752
  1.9 0.0 copy-start.1
  1.9 0.7 copy-done.1
  2.6 1.6 %pack.1 = bf16[16,776,128]{2,1,0:T(8,128)(2,1)S(1)} custom-call(bf16[128,32,384]{2,1,0:T(8,128)(2,1)S(1)} %copy-done, s32[32,128]{1,0:T(8,128)S(1)} %bitcast.4), custom_call_target="tpu_custom_call" | custom-call | tf_op jit(solution)/shard_map/pack/pallas_call | solution.py:41
  4.2 80.1 %all_to_all.10.x_ref = bf16[16,776,128]{2,1,0:T(8,128)(2,1)S(1)} all-to-all(bf16[16,776,128]{2,1,0:T(8,128)(2,1)S(1)} %pack.1), channel_id=1, replica_groups=mesh['groups'=2,'seq'=16] {'seq'}, dimensions={0} | all-to-all | bytes 6356992 | tf_op jit(solution)/shard_map/all_to_all | solution.py:168
  84.3 6.8 %attend.1 = bf16[16,256,128]{2,1,0:T(8,128)(2,1)S(1)} custom-call(s32[2,16,128]{2,1,0:T(8,128)S(1)} %copy.3.lab_ref, bf16[16,776,128]{2,1,0:T(8,128)(2,1)S(1)} %all_to_all.10.x_ref), custom_call_target="tpu_custom_call" | custom-call | tf_op jit(solution)/shard_map/attend/pallas_call | solution.py:146
  91.1 28.1 %all_to_all.11 = bf16[16,256,128]{2,1,0:T(8,128)(2,1)} all-to-all(bf16[16,256,128]{2,1,0:T(8,128)(2,1)S(1)} %attend.1), channel_id=1, replica_groups=mesh['groups'=2,'seq'=16] {'seq'}, dimensions={0} | all-to-all | bytes 2097152 | tf_op jit(solution)/shard_map/all_to_all | solution.py:168
  119.2 2.4 %unpack.1 = bf16[128,32,128]{2,1,0:T(8,128)(2,1)} custom-call(bf16[32,128,128]{2,1,0:T(8,128)(2,1)} %bitcast.5), custom_call_target="tpu_custom_call" | custom-call | tf_op jit(solution)/shard_map/unpack/pallas_call | solution.py:57
  (2 shorter events, 0.0 us)
Async XLA Ops:
  0.0 1.9 %copy-start = (bf16[128,32,384]{2,1,0:T(8,128)(2,1)S(1)}, bf16[128,32,384]{2,1,0:T(8,128)(2,1)}, u32[]{:S(2)}) copy-start(bf16[128,32,384]{2,1,0:T(8,128)(2,1)} %x_ref.1) | copy-start | bytes 9437188
  1.9 0.7 copy-start.1

commit v4 on v3

--- a/solution.py
+++ b/solution.py
@@ -154,6 +154,374 @@
     )(labels, x)
 
 
+def spread_kernel(me_ref, x_ref, lab_ref, cross_ref, *rest):
+    near_refs, turn_ref = rest[:-1], rest[-1]
+    tok, heads, width = x_ref.shape
+    nseq = cross_ref.shape[0]
+    half = nseq // 2
+    me = me_ref[0]
+    pad = jnp.zeros((4, 128), jnp.float32)
+    for dst in range(nseq):
+        other = dst ^ half
+        labels = [lab_ref[2 * dst : 2 * dst + 2, :], lab_ref[2 * other : 2 * other + 2, :]]
+        labels = [piece.astype(jnp.float32) for piece in labels]
+        cross_ref[dst, 4 * tok : 4 * tok + 8, :] = jnp.concatenate(labels + [pad], axis=0).astype(
+            jnp.bfloat16
+        )
+    for first in range(0, tok, 32):
+        piece = x_ref[first : first + 32].astype(jnp.float32)
+        turned = jnp.swapaxes(piece, 0, 1).astype(jnp.bfloat16)
+        for head in range(heads):
+            for part in range(3):
+                value = turned[head, :, part * 128 : (part + 1) * 128]
+                turn_ref[head, part, first : first + 32, :] = value
+                side = 0 if head // 2 < half else 2
+                if part == 1 or part == side:
+                    row = (head % 2 + (0 if part == 1 else 2)) * tok + first
+                    cross_ref[head // 2, row : row + 32, :] = value
+    near_part = jnp.where(me >= half, 0, 2)
+    for k, near_ref in enumerate(near_refs):
+        dst = me ^ k
+        other = dst ^ half
+        for j in range(2):
+            near_ref[j * tok : (j + 1) * tok, :] = turn_ref[2 * dst + j, near_part]
+            for part in range(3):
+                row = (2 + 2 * part + j) * tok
+                near_ref[row : row + tok, :] = turn_ref[2 * other + j, part]
+
+
+def spread(me, qkv, labels, nseq):
+    tok, heads, width = qkv.shape
+    whole = pl.BlockSpec(memory_space=pltpu.VMEM)
+    near = jax.ShapeDtypeStruct((8 * tok, 128), jnp.bfloat16)
+    out = pl.pallas_call(
+        spread_kernel,
+        out_shape=[jax.ShapeDtypeStruct((nseq, 4 * tok + 8, 128), jnp.bfloat16)]
+        + [near] * (nseq // 2),
+        in_specs=[pl.BlockSpec(memory_space=pltpu.SMEM), whole, whole],
+        out_specs=[whole] * (1 + nseq // 2),
+        scratch_shapes=[pltpu.VMEM((heads, 3, tok, 128), jnp.bfloat16)],
+        compiler_params=pltpu.CompilerParams(vmem_limit_bytes=32 << 20),
+        name="spread",
+    )(me, qkv, labels)
+    return out[0], out[1:]
+
+
+def run_tasks(tasks, score, weigh, blend):
+    ahead = score(*tasks[0])
+    behind = None
+    for place, task in enumerate(tasks):
+        s = ahead
+        if place + 1 < len(tasks):
+            ahead = score(*tasks[place + 1])
+        found = weigh(*task, s)
+        if behind is not None:
+            blend(*behind)
+        behind = (*task, *found)
+    blend(*behind)
+
+
+def dot_t(a, b):
+    return lax.dot_general(a, b, (((1,), (1,)), ((), ())), preferred_element_type=jnp.float32)
+
+
+def soften(s, lab_q, lab_k, diagonal, rate):
+    pieces = []
+    for i, lab in enumerate(lab_k):
+        keep = lab_q == lab
+        if diagonal is not None and i * 128 >= diagonal:
+            lanes = lax.broadcasted_iota(jnp.int32, (QB, 128), 1) + (i * 128 - diagonal)
+            keep = keep & (lanes <= lax.broadcasted_iota(jnp.int32, (QB, 128), 0))
+        pieces.append(jnp.where(keep, s[:, i * 128 : (i + 1) * 128], NEG))
+    peak = functools.reduce(jnp.maximum, pieces)
+    peak = jnp.broadcast_to(jnp.max(peak, axis=1, keepdims=True), (QB, 128))
+    pieces = [jnp.exp2((piece - peak) * rate).astype(jnp.bfloat16) for piece in pieces]
+    return jnp.concatenate(pieces, axis=1), peak
+
+
+def columns(rows):
+    return jnp.concatenate(
+        [jnp.transpose(jnp.broadcast_to(row, (128, 128))) for row in rows], axis=0
+    )
+
+
+def three_parts(stats):
+    rows = []
+    for row in stats:
+        for _ in range(3):
+            part = row.astype(jnp.bfloat16).astype(jnp.float32)
+            rows.append(part)
+            row = row - part
+    rows.append(jnp.zeros((8 - len(rows), 128), jnp.float32))
+    return jnp.concatenate(rows, axis=0).astype(jnp.bfloat16)
+
+
+def own_kernel(me_ref, lab_ref, x_ref, *rest, tok, rate):
+    nseq = x_ref.shape[0]
+    half = nseq // 2
+    span = half * tok
+    near_refs, o_ref = rest[:half], rest[half]
+    q_ref, v_ref, num_ref, sum_ref, peak_ref, stat_ref = rest[half + 1 :]
+    me = me_ref[0]
+    upper = me >= half
+    up = upper.astype(jnp.int32)
+    for j in range(2):
+        for slot in range(2):
+            v_ref[j, slot, :, 128:] = jnp.ones((span, 128), jnp.bfloat16)
+
+    @pl.when(upper)
+    def _():
+        for j in range(2):
+            for k, near_ref in enumerate(near_refs):
+                place = pl.multiple_of(((me ^ k) % half) * tok, tok)
+                q_ref[j, 1, pl.ds(place, tok), :] = near_ref[j * tok : (j + 1) * tok, :]
+            for slot in range(2):
+                v_ref[j, slot, :, :128] = x_ref[
+                    slot * half : (slot + 1) * half, (2 + j) * tok : (3 + j) * tok, :
+                ].reshape(span, 128)
+
+    @pl.when(jnp.logical_not(upper))
+    def _():
+        for j in range(2):
+            for k, near_ref in enumerate(near_refs):
+                place = pl.multiple_of(((me ^ k) % half) * tok, tok)
+                v_ref[j, 0, pl.ds(place, tok), :128] = near_ref[j * tok : (j + 1) * tok, :]
+            for slot in range(2):
+                q_ref[j, slot] = x_ref[
+                    slot * half : (slot + 1) * half, (2 + j) * tok : (3 + j) * tok, :
+                ].reshape(span, 128)
+
+    def keys(j, first, count):
+        return x_ref[pl.ds(first, count), j * tok : (j + 1) * tok, :].reshape(count * tok, 128)
+
+    def lab_of(j, first, count):
+        return [lab_ref[j, pl.ds(first + i, 1), :] for i in range(count)]
+
+    per = QB // tok
+
+    def score(cross, j, block):
+        rows = pl.ds(block * QB, QB)
+        if cross:
+            return dot_t(q_ref[j, 1, rows, :], keys(j, 0, half))
+        return dot_t(q_ref[j, up, rows, :], keys(j, up * half, (block + 1) * per))
+
+    def weigh(cross, j, block, s):
+        if cross:
+            lab_q = columns(lab_of(j, half + block * per, per))
+            return soften(s, lab_q, lab_of(j, 0, half), None, rate)
+        lab_q = columns(lab_of(j, up * half + block * per, per))
+        lab_k = lab_of(j, up * half, (block + 1) * per)
+        return soften(s, lab_q, lab_k, block * QB, rate)
+
+    def blend(cross, j, block, weights, peak):
+        rows = pl.ds(block * QB, QB)
+        if cross:
+            both = jnp.dot(weights, v_ref[j, 0], preferred_element_type=jnp.float32)
+            num, total = both[:, :128], both[:, 128:]
+            num_ref[j, rows, :] = num
+            sum_ref[j, rows, :] = total
+            peak_ref[j, rows, :] = peak
+            lse = peak * rate + jnp.log2(total)
+            for i in range(per):
+                turned = jnp.transpose(lse[i * tok : (i + 1) * tok, :])
+                stat_ref[j, block * per + i : block * per + i + 1, :] = turned[:1, :]
+            out = num / total
+            first = (1 - up) * half + block * per
+        else:
+            both = jnp.dot(
+                weights, v_ref[j, up, : (block + 1) * QB, :], preferred_element_type=jnp.float32
+            )
+            far = jnp.where(upper, peak_ref[j, rows, :], NEG)
+            top = jnp.maximum(peak, far)
+            here = jnp.exp2((peak - top) * rate)
+            there = jnp.exp2((far - top) * rate)
+            num = both[:, :128] * here + num_ref[j, rows, :] * there
+            out = num / (both[:, 128:] * here + sum_ref[j, rows, :] * there)
+            first = up * half + block * per
+        o_ref[pl.ds(first, per), j * tok : (j + 1) * tok, :] = out.astype(jnp.bfloat16).reshape(
+            per, tok, 128
+        )
+
+    blocks = span // QB
+    tasks = [(True, j, block) for block in range(blocks) for j in range(2)]
+    tasks += [
+        (False, j, block if j == 0 else blocks - 1 - block)
+        for block in range(blocks)
+        for j in range(2)
+    ]
+    run_tasks(tasks, score, weigh, blend)
+    for i in range(half):
+        stats = three_parts([stat_ref[j, i : i + 1, :] for j in range(2)])
+        o_ref[(1 - up) * half + i, 2 * tok : 2 * tok + 8, :] = stats
+        o_ref[up * half + i, 2 * tok : 2 * tok + 8, :] = jnp.zeros((8, 128), jnp.bfloat16)
+
+
+def own(me, labels, x, near, tok, rate):
+    nseq = x.shape[0]
+    half = nseq // 2
+    span = half * tok
+    whole = pl.BlockSpec(memory_space=pltpu.VMEM)
+    return pl.pallas_call(
+        functools.partial(own_kernel, tok=tok, rate=rate),
+        out_shape=jax.ShapeDtypeStruct((nseq, 2 * tok + 8, 128), jnp.bfloat16),
+        in_specs=[pl.BlockSpec(memory_space=pltpu.SMEM)] + [whole] * (2 + half),
+        out_specs=whole,
+        scratch_shapes=[
+            pltpu.VMEM((2, 2, span, 128), jnp.bfloat16),
+            pltpu.VMEM((2, 2, span, 256), jnp.bfloat16),
+            pltpu.VMEM((2, span, 128), jnp.float32),
+            pltpu.VMEM((2, span, 128), jnp.float32),
+            pltpu.VMEM((2, span, 128), jnp.float32),
+            pltpu.VMEM((2, half, 128), jnp.float32),
+        ],
+        compiler_params=pltpu.CompilerParams(vmem_limit_bytes=40 << 20),
+        name="own",
+    )(me, labels, x, *near)
+
+
+def partner_kernel(me_ref, lab_ref, *rest, tok, rate):
+    half = (len(rest) - 5) // 2
+    near_refs, o_refs = rest[:half], rest[half : 2 * half]
+    q_ref, k_ref, v_ref, out_ref, stat_ref = rest[2 * half :]
+    span = half * tok
+    me = me_ref[0]
+    up = (me >= half).astype(jnp.int32)
+    for j in range(2):
+        v_ref[j, :, 128:] = jnp.ones((span, 128), jnp.bfloat16)
+        for k, near_ref in enumerate(near_refs):
+            place = pl.ds(pl.multiple_of(((me ^ k) % half) * tok, tok), tok)
+            q_ref[j, place, :] = near_ref[(2 + j) * tok : (3 + j) * tok, :]
+            k_ref[j, place, :] = near_ref[(4 + j) * tok : (5 + j) * tok, :]
+            v_ref[j, place, :128] = near_ref[(6 + j) * tok : (7 + j) * tok, :]
+
+    def lab_of(j, first, count):
+        return [lab_ref[2 + j, pl.ds(up * half + first + i, 1), :] for i in range(count)]
+
+    per = QB // tok
+
+    def score(j, block):
+        return dot_t(q_ref[j, pl.ds(block * QB, QB), :], k_ref[j, : (block + 1) * QB, :])
+
+    def weigh(j, block, s):
+        lab_q = columns(lab_of(j, block * per, per))
+        return soften(s, lab_q, lab_of(j, 0, (block + 1) * per), block * QB, rate)
+
+    def blend(j, block, weights, peak):
+        both = jnp.dot(
+            weights, v_ref[j, : (block + 1) * QB, :], preferred_element_type=jnp.float32
+        )
+        num, total = both[:, :128], both[:, 128:]
+        lse = peak * rate + jnp.log2(total)
+        out = (num / total).astype(jnp.bfloat16)
+        for i in range(per):
+            turned = jnp.transpose(lse[i * tok : (i + 1) * tok, :])
+            stat_ref[j, block * per + i : block * per + i + 1, :] = turned[:1, :]
+            out_ref[block * per + i, j * tok : (j + 1) * tok, :] = out[i * tok : (i + 1) * tok, :]
+
+    blocks = span // QB
+    tasks = [
+        (j, block if j == 0 else blocks - 1 - block) for block in range(blocks) for j in range(2)
+    ]
+    run_tasks(tasks, score, weigh, blend)
+    for i in range(half):
+        stats = three_parts([stat_ref[j, i : i + 1, :] for j in range(2)])
+        out_ref[i, 2 * tok : 2 * tok + 8, :] = stats
+    for k, o_ref in enumerate(o_refs):
+        o_ref[...] = out_ref[(me ^ k) % half]
+
+
+def partner(me, labels, near, tok, rate):
+    half = len(near)
+    span = half * tok
+    whole = pl.BlockSpec(memory_space=pltpu.VMEM)
+    return pl.pallas_call(
+        functools.partial(partner_kernel, tok=tok, rate=rate),
+        out_shape=[jax.ShapeDtypeStruct((2 * tok + 8, 128), jnp.bfloat16)] * half,
+        in_specs=[pl.BlockSpec(memory_space=pltpu.SMEM)] + [whole] * (1 + half),
+        out_specs=[whole] * half,
+        scratch_shapes=[
+            pltpu.VMEM((2, span, 128), jnp.bfloat16),
+            pltpu.VMEM((2, span, 128), jnp.bfloat16),
+            pltpu.VMEM((2, span, 256), jnp.bfloat16),
+            pltpu.VMEM((half, 2 * tok + 8, 128), jnp.bfloat16),
+            pltpu.VMEM((2, half, 128), jnp.float32),
+        ],
+        compiler_params=pltpu.CompilerParams(vmem_limit_bytes=32 << 20),
+        name="partner",
+    )(me, labels, *near)
+
+
+def merge_kernel(me_ref, x_ref, *rest, tok):
+    nseq = x_ref.shape[0]
+    half = nseq // 2
+    near_refs, o_ref, head_ref = rest[:half], rest[half], rest[half + 1]
+    me = me_ref[0]
+    upper = me >= half
+    up = upper.astype(jnp.int32)
+    down = 1 - up
+    heads = 2 * nseq
+    for i in range(half):
+        for j in range(2):
+            head_ref[up * (heads // 2) + 2 * i + j] = x_ref[
+                up * half + i, j * tok : (j + 1) * tok, :
+            ].astype(jnp.float32)
+    for k, near_ref in enumerate(near_refs):
+        place = (me ^ k) % half
+        far_stats = x_ref[down * half + place, 2 * tok : 2 * tok + 8, :].astype(jnp.float32)
+        near_stats = near_ref[2 * tok : 2 * tok + 8, :].astype(jnp.float32)
+        for j in range(2):
+            near_lse = sum(near_stats[3 * j + c : 3 * j + c + 1, :] for c in range(3))
+            far_lse = sum(far_stats[3 * j + c : 3 * j + c + 1, :] for c in range(3))
+            weight = jnp.where(upper, 1.0 / (1.0 + jnp.exp2(near_lse - far_lse)), 0.0)
+            weight = jnp.transpose(jnp.broadcast_to(weight, (128, tok)))
+            far = x_ref[down * half + place, j * tok : (j + 1) * tok, :].astype(jnp.float32)
+            near = near_ref[j * tok : (j + 1) * tok, :].astype(jnp.float32)
+            head_ref[down * (heads // 2) + 2 * place + j] = near + (far - near) * weight
+    for first in range(0, tok, 32):
+        piece = head_ref[:, first : first + 32, :]
+        o_ref[first : first + 32] = jnp.swapaxes(piece, 0, 1).astype(jnp.bfloat16)
+
+
+def merge(me, x, near, tok):
+    nseq = x.shape[0]
+    whole = pl.BlockSpec(memory_space=pltpu.VMEM)
+    return pl.pallas_call(
+        functools.partial(merge_kernel, tok=tok),
+        out_shape=jax.ShapeDtypeStruct((tok, 2 * nseq, 128), jnp.bfloat16),
+        in_specs=[pl.BlockSpec(memory_space=pltpu.SMEM)] + [whole] * (1 + nseq // 2),
+        out_specs=whole,
+        scratch_shapes=[pltpu.VMEM((2 * nseq, tok, 128), jnp.float32)],
+        compiler_params=pltpu.CompilerParams(vmem_limit_bytes=32 << 20),
+        name="merge",
+    )(me, x, *near)
+
+
+def two_halves(qkv, labels):
+    tok, heads, width = qkv.shape
+    nseq = lax.axis_size("seq")
+    rate = math.log2(math.e) / math.sqrt(width // 3)
+    me = lax.axis_index("seq").astype(jnp.int32).reshape(1)
+
+    def exchange(x):
+        return lax.all_to_all(x, "seq", split_axis=0, concat_axis=0, tiled=True)
+
+    def swap(blocks):
+        moved = [
+            lax.ppermute(block, "seq", [(i, i ^ k) for i in range(nseq)])
+            for k, block in enumerate(blocks)
+            if k
+        ]
+        return [blocks[0]] + moved
+
+    cross, near = spread(me, qkv, labels, nseq)
+    near = swap(near)
+    cross = exchange(cross)
+    labels = jnp.transpose(cross[:, 4 * tok : 4 * tok + 4, :].astype(jnp.int32), (1, 0, 2))
+    back = exchange(own(me, labels, cross, near, tok, rate))
+    near_back = swap(partner(me, labels, near, tok, rate))
+    return merge(me, back, near_back, tok)
+
+
 def local(qkv, routes):
     tok, heads, width = qkv.shape
     head_size = width // 3
@@ -168,6 +536,9 @@
         return lax.all_to_all(x, "seq", split_axis=0, concat_axis=0, tiled=True)
 
     labels = jnp.transpose(routes)
+    paired = nseq & (nseq - 1) == 0 and nseq * tok // 2 % QB == 0
+    if split == 1 and chunks == 2 and paired and tok == 128 and head_size == 128:
+        return two_halves(qkv, labels)
     if split == 1:
         rows = exchange(pack(qkv, labels, chunks))
     else:

time: 122 us -> 118 us (0.967)
  blocking collectives: 108 us -> 0 us
  waiting for transfers between devices: 0 us -> 70.7 us
  starting transfers between devices: 0 us -> 24.4 us
  Pallas kernels: 10.8 us -> 15.7 us
  local copies, waits for them, and re-layouts: 2.61 us -> 6.76 us
    all_to_all x2 -> x0, blocking collectives: 108 us -> none  [exchange(): return lax.all_to_all(x, 'seq', split_axis=0, concat_axis=0, tiled=True)]
    ppermute x0 -> x14, waiting for transfers between devices: none -> 54.3 us  [swap(): lax.ppermute(block, 'seq', [(i, i ^ k) for i in range(nseq)])]
    all_to_all x0 -> x2, waiting for transfers between devices: none -> 16.4 us  [exchange(): return lax.all_to_all(x, 'seq', split_axis=0, concat_axis=0, tiled=True)]
    ppermute x0 -> x14, starting transfers between devices: none -> 13 us  [swap(): lax.ppermute(block, 'seq', [(i, i ^ k) for i in range(nseq)])]
    all_to_all x0 -> x2, starting transfers between devices: none -> 11.4 us  [exchange(): return lax.all_to_all(x, 'seq', split_axis=0, concat_axis=0, tiled=True)]
    pallas_call x3 -> x4, Pallas kernels: 10.8 us -> 15.7 us  [the longest x1 7.56 us: own(): pl.pallas_call(functools.partial(own_kernel, tok=tok, rate=rate), out_sha...]
    unnamed x4 -> x14, local copies, waits for them, and re-layouts: 2.61 us -> 6.75 us
  transfers between devices with their start and end apart: 0 -> 16, of which waited for: 0 -> 11; matrix products, arithmetic and copies ran while one was open for 0% -> 0% of each run, Pallas kernels for 0% -> 3%
where the time goes in v4:
time: 118 us
  waiting for transfers between devices  70.7 us (60%)
  starting transfers between devices  24.4 us (21%)
  Pallas kernels  15.7 us (13%)
  local copies, waits for them, and re-layouts  6.76 us (6%)
    ppermute x14, waiting for transfers between devices, swap(): lax.ppermute(block, 'seq', [(i, i ^ k) for i in range(nseq)])  54.3 us
    all_to_all x2, waiting for transfers between devices, exchange(): return lax.all_to_all(x, 'seq', split_axis=0, concat_axis=0, tiled=True)  16.4 us
    ppermute x14, starting transfers between devices, swap(): lax.ppermute(block, 'seq', [(i, i ^ k) for i in range(nseq)])  13 us
    all_to_all x2, starting transfers between devices, exchange(): return lax.all_to_all(x, 'seq', split_axis=0, concat_axis=0, tiled=True)  11.4 us
    pallas_call x1, Pallas kernels, own(): pl.pallas_call(functools.partial(own_kernel, tok=tok, rate=rate), out_sha...  7.56 us
    unnamed x14, local copies, waits for them, and re-layouts  6.75 us
    pallas_call x1, Pallas kernels, partner(): pl.pallas_call(functools.partial(partner_kernel, tok=tok, rate=rate), out...  3.52 us
    pallas_call x1, Pallas kernels, spread(): pl.pallas_call(spread_kernel, out_shape=[jax.ShapeDtypeStruct((nseq, 4 *...  2.87 us
  transfers between devices with their start and end apart: 16, of which 11 were waited for; matrix products, arithmetic and copies ran while one was open for 0% of the time, Pallas kernels for 3%

profile of v4, /device:TPU:0, one launch (start us, length us, event | category | flops | bytes accessed | tf_op | source)
XLA Modules:
  0.0 117.6 jit_solution(6057718059487137489)
XLA Ops:
  0.0 1.9 %copy-done = bf16[128,32,384]{2,1,0:T(8,128)(2,1)S(1)} copy-done((bf16[128,32,384]{2,1,0:T(8,128)(2,1)S(1)}, bf16[128,32,384]{2,1,0:T(8,128)(2,1)}, u32[]{:S(2)}) %copy-start) | copy-done | bytes 3145752
  1.9 0.7 copy-done.2
  2.6 2.9 %spread.1 = (bf16[16,520,128]{2,1,0:T(8,128)(2,1)S(1)}, bf16[1024,128]{1,0:T(8,128)(2,1)S(1)}, bf16[1024,128]{1,0:T(8,128)(2,1)}, bf16[1024,128]{1,0:T(8,128)(2,...) custom-call(s32[1]{0:T(128)} %bitcast.me_ref, ...), custom_call_target="tpu_custom_call" | custom-call | tf_op jit(solution)/shard_map/spread/pallas_call | solution.py:197
  5.5 1.4 %copy-done.1 = bf16[16,520,128]{2,1,0:T(8,128)(2,1)} copy-done((bf16[16,520,128]{2,1,0:T(8,128)(2,1)}, bf16[16,520,128]{2,1,0:T(8,128)(2,1)S(1)}, u32[]{:S(2)}) %copy-start.1) | copy-done | bytes 2129944
  6.8 0.7 copy-done.3
  7.5 0.7 copy-done.4
  8.2 0.7 copy-done.5
  8.9 0.7 copy-done.6
  9.6 7.4 %all-to-all-start = ((bf16[16,520,128]{2,1,0:T(8,128)(2,1)}), bf16[16,520,128]{2,1,0:T(8,128)(2,1)S(1)}, u32[]{:S(2)}, u32[]{:S(2)}) async-start(bf16[16,520,128]{2,1,0:T(8,128)(2,1)} %copy-done.1), calls=%async_computation | async-start | bytes 4259840 | tf_op jit(solution)/shard_map/all_to_all | solution.py:506
  17.0 0.4 collective-permute-start
  17.4 1.7 %collective-permute-start.1 = (bf16[1024,128]{1,0:T(8,128)(2,1)}, bf16[1024,128]{1,0:T(8,128)(2,1)S(1)}, u32[]{:S(2)}, u32[]{:S(2)}) collective-permute-start(bf16[1024,128]{1,0:T(8,128)(2,1)} %get-tuple-element.25), channel_id=1, source_target_pairs={{0,2},{1,3},{2,0},{3,1},{4,6},{5,7},{6,4},{7,5},{8,10},{9,11},{10,... | collective-permute-start | bytes 786440 | tf_op jit(solution)/shard_map/ppermute | solution.py:510
  19.1 1.7 %collective-permute-start.3 = (bf16[1024,128]{1,0:T(8,128)(2,1)}, bf16[1024,128]{1,0:T(8,128)(2,1)S(1)}, u32[]{:S(2)}, u32[]{:S(2)}) collective-permute-start(bf16[1024,128]{1,0:T(8,128)(2,1)} %copy-done.6), channel_id=1, source_target_pairs={{0,4},{1,5},{2,6},{3,7},{4,0},{5,1},{6,2},{7,3},{8,12},{9,13},{10,... | collective-permute-start | bytes 786440 | tf_op jit(solution)/shard_map/ppermute | solution.py:510
  20.9 2.6 %collective-permute-start.5 = (bf16[1024,128]{1,0:T(8,128)(2,1)}, bf16[1024,128]{1,0:T(8,128)(2,1)}, u32[]{:S(2)}, u32[]{:S(2)}) collective-permute-start(bf16[1024,128]{1,0:T(8,128)(2,1)} %copy-done.4), channel_id=1, source_target_pairs={{0,6},{1,7},{2,4},{3,5},{4,2},{5,3},{6,0},{7,1},{8,14},{9,15},{10,... | collective-permute-start | bytes 786440 | tf_op jit(solution)/shard_map/ppermute | solution.py:510
  23.5 19.0 %collective-permute-done.1.rest_2_ = bf16[1024,128]{1,0:T(8,128)(2,1)S(1)} collective-permute-done((bf16[1024,128]{1,0:T(8,128)(2,1)}, bf16[1024,128]{1,0:T(8,128)(2,1)S(1)}, u32[]{:S(2)}, u32[]{:S(2)}) %collective-permute-start.1) | collective-permute-done | bytes 262176 | tf_op jit(solution)/shard_map/ppermute | solution.py:510
  42.4 16.4 %all-to-all-done.x_ref = bf16[16,520,128]{2,1,0:T(8,128)(2,1)S(1)} async-done(((bf16[16,520,128]{2,1,0:T(8,128)(2,1)}), bf16[16,520,128]{2,1,0:T(8,128)(2,1)S(1)}, u32[]{:S(2)}, u32[]{:S(2)}) %all-to-all-start) | async-done | bytes 2129952 | tf_op jit(solution)/shard_map/all_to_all | solution.py:506
  58.9 6.3 %collective-permute-done.4.rest_5_ = bf16[1024,128]{1,0:T(8,128)(2,1)} collective-permute-done((bf16[1024,128]{1,0:T(8,128)(2,1)}, bf16[1024,128]{1,0:T(8,128)(2,1)}, u32[]{:S(2)}, u32[]{:S(2)}) %collective-permute-start.4) | collective-permute-done | bytes 262176 | tf_op jit(solution)/shard_map/ppermute | solution.py:510
  65.3 7.6 %collective-permute-done.5.rest_6_ = bf16[1024,128]{1,0:T(8,128)(2,1)} collective-permute-done((bf16[1024,128]{1,0:T(8,128)(2,1)}, bf16[1024,128]{1,0:T(8,128)(2,1)}, u32[]{:S(2)}, u32[]{:S(2)}) %collective-permute-start.5) | collective-permute-done | bytes 262176 | tf_op jit(solution)/shard_map/ppermute | solution.py:510
  72.9 4.7 %collective-permute-done.6.rest_7_ = bf16[1024,128]{1,0:T(8,128)(2,1)} collective-permute-done((bf16[1024,128]{1,0:T(8,128)(2,1)}, bf16[1024,128]{1,0:T(8,128)(2,1)}, u32[]{:S(2)}, u32[]{:S(2)}) %collective-permute-start.6) | collective-permute-done | bytes 262176 | tf_op jit(solution)/shard_map/ppermute | solution.py:510
  77.5 7.6 %own.1 = bf16[16,264,128]{2,1,0:T(8,128)(2,1)} custom-call(s32[1]{0:T(128)} %bitcast.me_ref, s32[4,16,128]{2,1,0:T(8,128)S(1)} %convert_bitcast_fusion.lab_ref, bf16[16,520,128]{2,1,0:T(8,128)(2,1)S(1)} %all-to-all-done.x_ref, bf16[1024,128]{1,0:T(8,128)(2,1)S(1)} %get-tuple-element.23.rest_0_, bf16[1024,128]{1,0:T(8,128)(2,1)S(1)} %collective-permute-done.rest_1_, ...), custom_call_target="tpu_custom_call" | custom-call | tf_op jit(solution)/shard_map/own/pallas_call | solution.py:364
  85.1 4.0 %all-to-all-start.1 = ((bf16[16,264,128]{2,1,0:T(8,128)(2,1)}), bf16[16,264,128]{2,1,0:T(8,128)(2,1)S(1)}, u32[]{:S(2)}, u32[]{:S(2)}) async-start(bf16[16,264,128]{2,1,0:T(8,128)(2,1)} %own.1), calls=%async_computation.1 | async-start | bytes 2162688 | tf_op jit(solution)/shard_map/all_to_all | solution.py:506
  89.1 3.5 %partner.1 = (bf16[264,128]{1,0:T(8,128)(2,1)S(1)}, bf16[264,128]{1,0:T(8,128)(2,1)S(1)}, bf16[264,128]{1,0:T(8,128)(2,1)S(1)}, bf16[264,128]{1,0:T(8,128)(2,1)S...) custom-call(s32[1]{0:T(128)} %bitcast.me_ref, ...), custom_call_target="tpu_custom_call" | custom-call | tf_op jit(solution)/shard_map/partner/pallas_call | solution.py:437
  92.7 0.5 collective-permute-start.7
  93.1 1.7 %collective-permute-start.8 = (bf16[264,128]{1,0:T(8,128)(2,1)S(1)}, bf16[264,128]{1,0:T(8,128)(2,1)S(1)}, u32[]{:S(2)}, u32[]{:S(2)}) collective-permute-start(bf16[264,128]{1,0:T(8,128)(2,1)S(1)} %get-tuple-element.33), channel_id=1, source_target_pairs={{0,2},{1,3},{2,0},{3,1},{4,6},{5,7},{6,4},{7,5},{8,10},{9,11},{10,... | collective-permute-start | bytes 202760 | tf_op jit(solution)/shard_map/ppermute | solution.py:510
  94.8 1.7 %collective-permute-start.10 = (bf16[264,128]{1,0:T(8,128)(2,1)S(1)}, bf16[264,128]{1,0:T(8,128)(2,1)S(1)}, u32[]{:S(2)}, u32[]{:S(2)}) collective-permute-start(bf16[264,128]{1,0:T(8,128)(2,1)S(1)} %get-tuple-element.35), channel_id=1, source_target_pairs={{0,4},{1,5},{2,6},{3,7},{4,0},{5,1},{6,2},{7,3},{8,12},{9,13},{10,... | collective-permute-start | bytes 202760 | tf_op jit(solution)/shard_map/ppermute | solution.py:510
  96.6 2.6 %collective-permute-start.12 = (bf16[264,128]{1,0:T(8,128)(2,1)S(1)}, bf16[264,128]{1,0:T(8,128)(2,1)S(1)}, u32[]{:S(2)}, u32[]{:S(2)}) collective-permute-start(bf16[264,128]{1,0:T(8,128)(2,1)S(1)} %get-tuple-element.37), channel_id=1, source_target_pairs={{0,6},{1,7},{2,4},{3,5},{4,2},{5,3},{6,0},{7,1},{8,14},{9,15},{10,... | collective-permute-start | bytes 202760 | tf_op jit(solution)/shard_map/ppermute | solution.py:510
  99.2 1.8 %collective-permute-done.8.rest_2_ = bf16[264,128]{1,0:T(8,128)(2,1)S(1)} collective-permute-done((bf16[264,128]{1,0:T(8,128)(2,1)S(1)}, bf16[264,128]{1,0:T(8,128)(2,1)S(1)}, u32[]{:S(2)}, u32[]{:S(2)}) %collective-permute-start.8) | collective-permute-done | bytes 67616 | tf_op jit(solution)/shard_map/ppermute | solution.py:510
  101.0 1.4 %collective-permute-done.9.rest_3_ = bf16[264,128]{1,0:T(8,128)(2,1)S(1)} collective-permute-done((bf16[264,128]{1,0:T(8,128)(2,1)S(1)}, bf16[264,128]{1,0:T(8,128)(2,1)S(1)}, u32[]{:S(2)}, u32[]{:S(2)}) %collective-permute-start.9) | collective-permute-done | bytes 67616 | tf_op jit(solution)/shard_map/ppermute | solution.py:510
  102.4 7.0 %collective-permute-done.10.rest_4_ = bf16[264,128]{1,0:T(8,128)(2,1)S(1)} collective-permute-done((bf16[264,128]{1,0:T(8,128)(2,1)S(1)}, bf16[264,128]{1,0:T(8,128)(2,1)S(1)}, u32[]{:S(2)}, u32[]{:S(2)}) %collective-permute-start.10) | collective-permute-done | bytes 67616 | tf_op jit(solution)/shard_map/ppermute | solution.py:510
  109.4 1.4 %collective-permute-done.11.rest_5_ = bf16[264,128]{1,0:T(8,128)(2,1)S(1)} collective-permute-done((bf16[264,128]{1,0:T(8,128)(2,1)S(1)}, bf16[264,128]{1,0:T(8,128)(2,1)S(1)}, u32[]{:S(2)}, u32[]{:S(2)}) %collective-permute-start.11) | collective-permute-done | bytes 67616 | tf_op jit(solution)/shard_map/ppermute | solution.py:510
  110.8 4.6 %collective-permute-done.12.rest_6_ = bf16[264,128]{1,0:T(8,128)(2,1)S(1)} collective-permute-done((bf16[264,128]{1,0:T(8,128)(2,1)S(1)}, bf16[264,128]{1,0:T(8,128)(2,1)S(1)}, u32[]{:S(2)}, u32[]{:S(2)}) %collective-permute-start.12) | collective-permute-done | bytes 67616 | tf_op jit(solution)/shard_map/ppermute | solution.py:510
  115.4 0.5 collective-permute-done.13.rest_7_
  115.9 1.7 %merge.1 = bf16[128,32,128]{2,1,0:T(8,128)(2,1)} custom-call(s32[1]{0:T(128)} %bitcast.me_ref, bf16[16,264,128]{2,1,0:T(8,128)(2,1)S(1)} %all-to-all-done.1.x_ref, bf16[264,128]{1,0:T(8,128)(2,1)S(1)} %get-tuple-element.31.rest_0_, bf16[264,128]{1,0:T(8,128)(2,1)S(1)} %collective-permute-done.7.rest_1_, bf16[264,128]{1,0:T(8,128)(2,1)S(1)} %collective-permute-done.8.rest_2_, ...), custom_call_target="tpu_custom_call" | custom-call | tf_op jit(solution)/shard_map/merge/pallas_call | solution.py:488
  (20 shorter events, 0.3 us)
Async XLA Ops:
  0.0 1.9 %copy-start = (bf16[128,32,384]{2,1,0:T(8,128)(2,1)S(1)}, bf16[128,32,384]{2,1,0:T(8,128)(2,1)}, u32[]{:S(2)}) copy-start(bf16[128,32,384]{2,1,0:T(8,128)(2,1)} %x_ref.1) | copy-start | bytes 9437188
  1.9 0.7 copy-start.2
  5.5 1.4 %copy-start.1 = (bf16[16,520,128]{2,1,0:T(8,128)(2,1)}, bf16[16,520,128]{2,1,0:T(8,128)(2,1)S(1)}, u32[]{:S(2)}) copy-start(bf16[16,520,128]{2,1,0:T(8,128)(2,1)S(1)} %get-tuple-element.22) | copy-start | bytes 6389764
  6.8 0.7 copy-start.3
  7.5 0.7 copy-start.4
  8.2 0.7 copy-start.5
  8.9 0.7 copy-start.6
  9.6 49.2 %all-to-all-start = ((bf16[16,520,128]{2,1,0:T(8,128)(2,1)}), bf16[16,520,128]{2,1,0:T(8,128)(2,1)S(1)}, u32[]{:S(2)}, u32[]{:S(2)}) async-start(bf16[16,520,128]{2,1,0:T(8,128)(2,1)} %copy-done.1), calls=%async_computation | async-start | bytes 4259840 | tf_op jit(solution)/shard_map/all_to_all | solution.py:506
  17.0 3.9 %collective-permute-start = (bf16[1024,128]{1,0:T(8,128)(2,1)}, bf16[1024,128]{1,0:T(8,128)(2,1)S(1)}, u32[]{:S(2)}, u32[]{:S(2)}) collective-permute-start(bf16[1024,128]{1,0:T(8,128)(2,1)} %get-tuple-element.24), channel_id=1, source_target_pairs={{0,1},{1,0},{2,3},{3,2},{4,5},{5,4},{6,7},{7,6},{8,9},{9,8},{10,11... | collective-permute-start | bytes 786440 | tf_op jit(solution)/shard_map/ppermute | solution.py:510
  17.4 25.0 %collective-permute-start.1 = (bf16[1024,128]{1,0:T(8,128)(2,1)}, bf16[1024,128]{1,0:T(8,128)(2,1)S(1)}, u32[]{:S(2)}, u32[]{:S(2)}) collective-permute-start(bf16[1024,128]{1,0:T(8,128)(2,1)} %get-tuple-element.25), channel_id=1, source_target_pairs={{0,2},{1,3},{2,0},{3,1},{4,6},{5,7},{6,4},{7,5},{8,10},{9,11},{10,... | collective-permute-start | bytes 786440 | tf_op jit(solution)/shard_map/ppermute | solution.py:510
  19.1 39.8 %collective-permute-start.2 = (bf16[1024,128]{1,0:T(8,128)(2,1)}, bf16[1024,128]{1,0:T(8,128)(2,1)S(1)}, u32[]{:S(2)}, u32[]{:S(2)}) collective-permute-start(bf16[1024,128]{1,0:T(8,128)(2,1)} %get-tuple-element.26), channel_id=1, source_target_pairs={{0,3},{1,2},{2,1},{3,0},{4,7},{5,6},{6,5},{7,4},{8,11},{9,10},{10,... | collective-permute-start | bytes 786440 | tf_op jit(solution)/shard_map/ppermute | solution.py:510
  19.1 39.8 %collective-permute-start.3 = (bf16[1024,128]{1,0:T(8,128)(2,1)}, bf16[1024,128]{1,0:T(8,128)(2,1)S(1)}, u32[]{:S(2)}, u32[]{:S(2)}) collective-permute-start(bf16[1024,128]{1,0:T(8,128)(2,1)} %copy-done.6), channel_id=1, source_target_pairs={{0,4},{1,5},{2,6},{3,7},{4,0},{5,1},{6,2},{7,3},{8,12},{9,13},{10,... | collective-permute-start | bytes 786440 | tf_op jit(solution)/shard_map/ppermute | solution.py:510
  20.8 44.5 %collective-permute-start.4 = (bf16[1024,128]{1,0:T(8,128)(2,1)}, bf16[1024,128]{1,0:T(8,128)(2,1)}, u32[]{:S(2)}, u32[]{:S(2)}) collective-permute-start(bf16[1024,128]{1,0:T(8,128)(2,1)} %copy-done.5), channel_id=1, source_target_pairs={{0,5},{1,4},{2,7},{3,6},{4,1},{5,0},{6,3},{7,2},{8,13},{9,12},{10,... | collective-permute-start | bytes 786440 | tf_op jit(solution)/shard_map/ppermute | solution.py:510
  20.9 52.0 %collective-permute-start.5 = (bf16[1024,128]{1,0:T(8,128)(2,1)}, bf16[1024,128]{1,0:T(8,128)(2,1)}, u32[]{:S(2)}, u32[]{:S(2)}) collective-permute-start(bf16[1024,128]{1,0:T(8,128)(2,1)} %copy-done.4), channel_id=1, source_target_pairs={{0,6},{1,7},{2,4},{3,5},{4,2},{5,3},{6,0},{7,1},{8,14},{9,15},{10,... | collective-permute-start | bytes 786440 | tf_op jit(solution)/shard_map/ppermute | solution.py:510
  42.4 35.1 %collective-permute-start.6 = (bf16[1024,128]{1,0:T(8,128)(2,1)}, bf16[1024,128]{1,0:T(8,128)(2,1)}, u32[]{:S(2)}, u32[]{:S(2)}) collective-permute-start(bf16[1024,128]{1,0:T(8,128)(2,1)} %copy-done.3), channel_id=1, source_target_pairs={{0,7},{1,6},{2,5},{3,4},{4,3},{5,2},{6,1},{7,0},{8,15},{9,14},{10,... | collective-permute-start | bytes 786440 | tf_op jit(solution)/shard_map/ppermute | solution.py:510
  85.1 30.8 %all-to-all-start.1 = ((bf16[16,264,128]{2,1,0:T(8,128)(2,1)}), bf16[16,264,128]{2,1,0:T(8,128)(2,1)S(1)}, u32[]{:S(2)}, u32[]{:S(2)}) async-start(bf16[16,264,128]{2,1,0:T(8,128)(2,1)} %own.1), calls=%async_computation.1 | async-start | bytes 2162688 | tf_op jit(solution)/shard_map/all_to_all | solution.py:506
  92.7 4.0 %collective-permute-start.7 = (bf16[264,128]{1,0:T(8,128)(2,1)S(1)}, bf16[264,128]{1,0:T(8,128)(2,1)S(1)}, u32[]{:S(2)}, u32[]{:S(2)}) collective-permute-start(bf16[264,128]{1,0:T(8,128)(2,1)S(1)} %get-tuple-element.32), channel_id=1, source_target_pairs={{0,1},{1,0},{2,3},{3,2},{4,5},{5,4},{6,7},{7,6},{8,9},{9,8},{10,11... | collective-permute-start | bytes 202760 | tf_op jit(solution)/shard_map/ppermute | solution.py:510
  93.1 7.8 %collective-permute-start.8 = (bf16[264,128]{1,0:T(8,128)(2,1)S(1)}, bf16[264,128]{1,0:T(8,128)(2,1)S(1)}, u32[]{:S(2)}, u32[]{:S(2)}) collective-permute-start(bf16[264,128]{1,0:T(8,128)(2,1)S(1)} %get-tuple-element.33), channel_id=1, source_target_pairs={{0,2},{1,3},{2,0},{3,1},{4,6},{5,7},{6,4},{7,5},{8,10},{9,11},{10,... | collective-permute-start | bytes 202760 | tf_op jit(solution)/shard_map/ppermute | solution.py:510
  94.8 7.5 %collective-permute-start.9 = (bf16[264,128]{1,0:T(8,128)(2,1)S(1)}, bf16[264,128]{1,0:T(8,128)(2,1)S(1)}, u32[]{:S(2)}, u32[]{:S(2)}) collective-permute-start(bf16[264,128]{1,0:T(8,128)(2,1)S(1)} %get-tuple-element.34), channel_id=1, source_target_pairs={{0,3},{1,2},{2,1},{3,0},{4,7},{5,6},{6,5},{7,4},{8,11},{9,10},{10,... | collective-permute-start | bytes 202760 | tf_op jit(solution)/shard_map/ppermute | solution.py:510
  94.8 14.6 %collective-permute-start.10 = (bf16[264,128]{1,0:T(8,128)(2,1)S(1)}, bf16[264,128]{1,0:T(8,128)(2,1)S(1)}, u32[]{:S(2)}, u32[]{:S(2)}) collective-permute-start(bf16[264,128]{1,0:T(8,128)(2,1)S(1)} %get-tuple-element.35), channel_id=1, source_target_pairs={{0,4},{1,5},{2,6},{3,7},{4,0},{5,1},{6,2},{7,3},{8,12},{9,13},{10,... | collective-permute-start | bytes 202760 | tf_op jit(solution)/shard_map/ppermute | solution.py:510
  96.5 14.3 %collective-permute-start.11 = (bf16[264,128]{1,0:T(8,128)(2,1)S(1)}, bf16[264,128]{1,0:T(8,128)(2,1)S(1)}, u32[]{:S(2)}, u32[]{:S(2)}) collective-permute-start(bf16[264,128]{1,0:T(8,128)(2,1)S(1)} %get-tuple-element.36), channel_id=1, source_target_pairs={{0,5},{1,4},{2,7},{3,6},{4,1},{5,0},{6,3},{7,2},{8,13},{9,12},{10,... | collective-permute-start | bytes 202760 | tf_op jit(solution)/shard_map/ppermute | solution.py:510
  96.6 18.8 %collective-permute-start.12 = (bf16[264,128]{1,0:T(8,128)(2,1)S(1)}, bf16[264,128]{1,0:T(8,128)(2,1)S(1)}, u32[]{:S(2)}, u32[]{:S(2)}) collective-permute-start(bf16[264,128]{1,0:T(8,128)(2,1)S(1)} %get-tuple-element.37), channel_id=1, source_target_pairs={{0,6},{1,7},{2,4},{3,5},{4,2},{5,3},{6,0},{7,1},{8,14},{9,15},{10,... | collective-permute-start | bytes 202760 | tf_op jit(solution)/shard_map/ppermute | solution.py:510
  101.0 14.9 %collective-permute-start.13 = (bf16[264,128]{1,0:T(8,128)(2,1)S(1)}, bf16[264,128]{1,0:T(8,128)(2,1)S(1)}, u32[]{:S(2)}, u32[]{:S(2)}) collective-permute-start(bf16[264,128]{1,0:T(8,128)(2,1)S(1)} %get-tuple-element.38), channel_id=1, source_target_pairs={{0,7},{1,6},{2,5},{3,4},{4,3},{5,2},{6,1},{7,0},{8,15},{9,14},{10,... | collective-permute-start | bytes 202760 | tf_op jit(solution)/shard_map/ppermute | solution.py:510

commit v5 on v4

--- a/solution.py
+++ b/solution.py
@@ -11,6 +11,7 @@
 CLEN = 1024
 QB = 256
 STEP = 64
+SPREAD_MB = 12
 NEG = -1e30
 
 
@@ -154,31 +155,42 @@
     )(labels, x)
 
 
-def spread_kernel(me_ref, x_ref, lab_ref, cross_ref, *rest):
-    near_refs, turn_ref = rest[:-1], rest[-1]
+def cross_kernel(x_ref, lab_ref, o_ref):
     tok, heads, width = x_ref.shape
-    nseq = cross_ref.shape[0]
+    nseq = o_ref.shape[0]
     half = nseq // 2
-    me = me_ref[0]
     pad = jnp.zeros((4, 128), jnp.float32)
     for dst in range(nseq):
         other = dst ^ half
         labels = [lab_ref[2 * dst : 2 * dst + 2, :], lab_ref[2 * other : 2 * other + 2, :]]
         labels = [piece.astype(jnp.float32) for piece in labels]
-        cross_ref[dst, 4 * tok : 4 * tok + 8, :] = jnp.concatenate(labels + [pad], axis=0).astype(
+        o_ref[dst, 4 * tok : 4 * tok + 8, :] = jnp.concatenate(labels + [pad], axis=0).astype(
             jnp.bfloat16
         )
+    for first in range(0, tok, 32):
+        for part in range(3):
+            low = heads // 2 if part == 2 else 0
+            high = heads // 2 if part == 0 else heads
+            piece = x_ref[first : first + 32, low:high, part * 128 : (part + 1) * 128]
+            turned = jnp.swapaxes(piece.astype(jnp.float32), 0, 1).astype(jnp.bfloat16)
+            for head in range(low, high):
+                row = (head % 2 + (0 if part == 1 else 2)) * tok + first
+                o_ref[head // 2, row : row + 32, :] = turned[head - low]
+
+
+def near_kernel(me_ref, x_ref, *rest):
+    near_refs, turn_ref = rest[:-1], rest[-1]
+    tok, heads, width = x_ref.shape
+    half = len(near_refs)
+    me = me_ref[0]
     for first in range(0, tok, 32):
         piece = x_ref[first : first + 32].astype(jnp.float32)
         turned = jnp.swapaxes(piece, 0, 1).astype(jnp.bfloat16)
         for head in range(heads):
             for part in range(3):
-                value = turned[head, :, part * 128 : (part + 1) * 128]
-                turn_ref[head, part, first : first + 32, :] = value
-                side = 0 if head // 2 < half else 2
-                if part == 1 or part == side:
-                    row = (head % 2 + (0 if part == 1 else 2)) * tok + first
-                    cross_ref[head // 2, row : row + 32, :] = value
+                turn_ref[head, part, first : first + 32, :] = turned[
+                    head, :, part * 128 : (part + 1) * 128
+                ]
     near_part = jnp.where(me >= half, 0, 2)
     for k, near_ref in enumerate(near_refs):
         dst = me ^ k
@@ -193,18 +205,26 @@
 def spread(me, qkv, labels, nseq):
     tok, heads, width = qkv.shape
     whole = pl.BlockSpec(memory_space=pltpu.VMEM)
+    params = pltpu.CompilerParams(vmem_limit_bytes=SPREAD_MB << 20)
+    cross = pl.pallas_call(
+        cross_kernel,
+        out_shape=jax.ShapeDtypeStruct((nseq, 4 * tok + 8, 128), jnp.bfloat16),
+        in_specs=[whole, whole],
+        out_specs=whole,
+        compiler_params=params,
+        name="cross",
+    )(qkv, labels)
     near = jax.ShapeDtypeStruct((8 * tok, 128), jnp.bfloat16)
-    out = pl.pallas_call(
-        spread_kernel,
-        out_shape=[jax.ShapeDtypeStruct((nseq, 4 * tok + 8, 128), jnp.bfloat16)]
-        + [near] * (nseq // 2),
-        in_specs=[pl.BlockSpec(memory_space=pltpu.SMEM), whole, whole],
-        out_specs=[whole] * (1 + nseq // 2),
+    near = pl.pallas_call(
+        near_kernel,
+        out_shape=[near] * (nseq // 2),
+        in_specs=[pl.BlockSpec(memory_space=pltpu.SMEM), whole],
+        out_specs=[whole] * (nseq // 2),
         scratch_shapes=[pltpu.VMEM((heads, 3, tok, 128), jnp.bfloat16)],
-        compiler_params=pltpu.CompilerParams(vmem_limit_bytes=32 << 20),
-        name="spread",
-    )(me, qkv, labels)
-    return out[0], out[1:]
+        compiler_params=params,
+        name="near",
+    )(me, qkv)
+    return cross, near
 
 
 def run_tasks(tasks, score, weigh, blend):
@@ -374,7 +394,7 @@
             pltpu.VMEM((2, span, 128), jnp.float32),
             pltpu.VMEM((2, half, 128), jnp.float32),
         ],
-        compiler_params=pltpu.CompilerParams(vmem_limit_bytes=40 << 20),
+        compiler_params=pltpu.CompilerParams(vmem_limit_bytes=20 << 20),
         name="own",
     )(me, labels, x, *near)
 
@@ -446,7 +466,7 @@
             pltpu.VMEM((half, 2 * tok + 8, 128), jnp.bfloat16),
             pltpu.VMEM((2, half, 128), jnp.float32),
         ],
-        compiler_params=pltpu.CompilerParams(vmem_limit_bytes=32 << 20),
+        compiler_params=pltpu.CompilerParams(vmem_limit_bytes=16 << 20),
         name="partner",
     )(me, labels, *near)
 
@@ -491,7 +511,7 @@
         in_specs=[pl.BlockSpec(memory_space=pltpu.SMEM)] + [whole] * (1 + nseq // 2),
         out_specs=whole,
         scratch_shapes=[pltpu.VMEM((2 * nseq, tok, 128), jnp.float32)],
-        compiler_params=pltpu.CompilerParams(vmem_limit_bytes=32 << 20),
+        compiler_params=pltpu.CompilerParams(vmem_limit_bytes=12 << 20),
         name="merge",
     )(me, x, *near)
 
@@ -506,12 +526,10 @@
         return lax.all_to_all(x, "seq", split_axis=0, concat_axis=0, tiled=True)
 
     def swap(blocks):
-        moved = [
-            lax.ppermute(block, "seq", [(i, i ^ k) for i in range(nseq)])
-            for k, block in enumerate(blocks)
-            if k
-        ]
-        return [blocks[0]] + moved
+        moved = list(blocks)
+        for k in reversed(range(1, len(blocks))):
+            moved[k] = lax.ppermute(blocks[k], "seq", [(i, i ^ k) for i in range(nseq)])
+        return moved
 
     cross, near = spread(me, qkv, labels, nseq)
     near = swap(near)

time: 118 us -> 114 us (0.966)
  waiting for transfers between devices: 70.7 us -> 68.1 us
  local copies, waits for them, and re-layouts: 6.76 us -> 4.67 us
    unnamed x14 -> x8, local copies, waits for them, and re-layouts: 6.75 us -> 3.91 us
    ppermute x14, waiting for transfers between devices: 54.3 us -> 51.6 us  [swap(): moved[k] = lax.ppermute(blocks[k], 'seq', [(i, i ^ k) for i in range(nseq)])]
    pallas_call x1 -> x2, Pallas kernels: 2.87 us -> 3.8 us  [the longest x1 2.81 us: spread(): pl.pallas_call(near_kernel, out_shape=[near] * (nseq // 2), in_specs=[pl....]
  transfers between devices with their start and end apart: 16 -> 16, of which waited for: 11 -> 11; matrix products, arithmetic and copies ran while one was open for 0% -> 1% of each run, Pallas kernels for 3% -> 5%
where the time goes in v5:
time: 114 us
  waiting for transfers between devices  68.1 us (60%)
  starting transfers between devices  24.7 us (22%)
  Pallas kernels  16.1 us (14%)
  local copies, waits for them, and re-layouts  4.67 us (4%)
    ppermute x14, waiting for transfers between devices, swap(): moved[k] = lax.ppermute(blocks[k], 'seq', [(i, i ^ k) for i in range(nseq)])  51.6 us
    all_to_all x2, waiting for transfers between devices, exchange(): return lax.all_to_all(x, 'seq', split_axis=0, concat_axis=0, tiled=True)  16.5 us
    ppermute x14, starting transfers between devices, swap(): moved[k] = lax.ppermute(blocks[k], 'seq', [(i, i ^ k) for i in range(nseq)])  13 us
    all_to_all x2, starting transfers between devices, exchange(): return lax.all_to_all(x, 'seq', split_axis=0, concat_axis=0, tiled=True)  11.7 us
    pallas_call x1, Pallas kernels, own(): pl.pallas_call(functools.partial(own_kernel, tok=tok, rate=rate), out_sha...  8.14 us
    unnamed x8, local copies, waits for them, and re-layouts  3.91 us
    pallas_call x1, Pallas kernels, spread(): pl.pallas_call(near_kernel, out_shape=[near] * (nseq // 2), in_specs=[pl....  2.81 us
    pallas_call x1, Pallas kernels, partner(): pl.pallas_call(functools.partial(partner_kernel, tok=tok, rate=rate), out...  2.42 us
  transfers between devices with their start and end apart: 16, of which 11 were waited for; matrix products, arithmetic and copies ran while one was open for 1% of the time, Pallas kernels for 5%

profile of v5, /device:TPU:0, one launch (start us, length us, event | category | flops | bytes accessed | tf_op | source)
XLA Modules:
  0.0 113.7 jit_solution(7195654798920714420)
XLA Ops:
  0.0 1.9 %copy-done = bf16[128,32,384]{2,1,0:T(8,128)(2,1)S(1)} copy-done((bf16[128,32,384]{2,1,0:T(8,128)(2,1)S(1)}, bf16[128,32,384]{2,1,0:T(8,128)(2,1)}, u32[]{:S(2)}) %copy-start) | copy-done | bytes 3145752
  1.9 0.7 copy-done.3
  2.6 1.0 cross.1
  3.6 1.3 %copy-done.2 = bf16[16,520,128]{2,1,0:T(8,128)(2,1)} copy-done((bf16[16,520,128]{2,1,0:T(8,128)(2,1)}, bf16[16,520,128]{2,1,0:T(8,128)(2,1)S(1)}, u32[]{:S(2)}) %copy-start.2) | copy-done | bytes 2129944
  4.9 7.7 %all-to-all-start = ((bf16[16,520,128]{2,1,0:T(8,128)(2,1)}), bf16[16,520,128]{2,1,0:T(8,128)(2,1)}, u32[]{:S(2)}, u32[]{:S(2)}) async-start(bf16[16,520,128]{2,1,0:T(8,128)(2,1)} %copy-done.2), calls=%async_computation | async-start | bytes 4259840 | tf_op jit(solution)/shard_map/all_to_all | solution.py:526
  12.6 2.8 %near.1 = (bf16[1024,128]{1,0:T(8,128)(2,1)S(1)}, bf16[1024,128]{1,0:T(8,128)(2,1)S(1)}, bf16[1024,128]{1,0:T(8,128)(2,1)S(1)}, bf16[1024,128]{1,0:T(8,128)(2,1)...) custom-call(s32[1]{0:T(128)} %bitcast.me_ref, ...), custom_call_target="tpu_custom_call" | custom-call | tf_op jit(solution)/shard_map/near/pallas_call | solution.py:218
  15.4 0.4 collective-permute-start
  15.8 1.7 %collective-permute-start.1 = (bf16[1024,128]{1,0:T(8,128)(2,1)S(1)}, bf16[1024,128]{1,0:T(8,128)(2,1)S(1)}, u32[]{:S(2)}, u32[]{:S(2)}) collective-permute-start(bf16[1024,128]{1,0:T(8,128)(2,1)S(1)} %get-tuple-element.23), channel_id=1, source_target_pairs={{0,2},{1,3},{2,0},{3,1},{4,6},{5,7},{6,4},{7,5},{8,10},{9,11},{10,... | collective-permute-start | bytes 786440 | tf_op jit(solution)/shard_map/ppermute | solution.py:531
  17.4 1.7 %collective-permute-start.3 = (bf16[1024,128]{1,0:T(8,128)(2,1)}, bf16[1024,128]{1,0:T(8,128)(2,1)S(1)}, u32[]{:S(2)}, u32[]{:S(2)}) collective-permute-start(bf16[1024,128]{1,0:T(8,128)(2,1)} %get-tuple-element.25), channel_id=1, source_target_pairs={{0,4},{1,5},{2,6},{3,7},{4,0},{5,1},{6,2},{7,3},{8,12},{9,13},{10,... | collective-permute-start | bytes 786440 | tf_op jit(solution)/shard_map/ppermute | solution.py:531
  19.1 0.1 collective-permute-start.4
  19.3 2.6 %collective-permute-start.5 = (bf16[1024,128]{1,0:T(8,128)(2,1)}, bf16[1024,128]{1,0:T(8,128)(2,1)S(1)}, u32[]{:S(2)}, u32[]{:S(2)}) collective-permute-start(bf16[1024,128]{1,0:T(8,128)(2,1)} %get-tuple-element.27), channel_id=1, source_target_pairs={{0,6},{1,7},{2,4},{3,5},{4,2},{5,3},{6,0},{7,1},{8,14},{9,15},{10,... | collective-permute-start | bytes 786440 | tf_op jit(solution)/shard_map/ppermute | solution.py:531
  21.8 16.1 %collective-permute-done.1.rest_2_ = bf16[1024,128]{1,0:T(8,128)(2,1)S(1)} collective-permute-done((bf16[1024,128]{1,0:T(8,128)(2,1)S(1)}, bf16[1024,128]{1,0:T(8,128)(2,1)S(1)}, u32[]{:S(2)}, u32[]{:S(2)}) %collective-permute-start.1) | collective-permute-done | bytes 262176 | tf_op jit(solution)/shard_map/ppermute | solution.py:531
  38.0 16.5 %all-to-all-done.x_ref = bf16[16,520,128]{2,1,0:T(8,128)(2,1)} async-done(((bf16[16,520,128]{2,1,0:T(8,128)(2,1)}), bf16[16,520,128]{2,1,0:T(8,128)(2,1)}, u32[]{:S(2)}, u32[]{:S(2)}) %all-to-all-start) | async-done | bytes 2129952 | tf_op jit(solution)/shard_map/all_to_all | solution.py:526
  54.5 0.8 slice.4
  55.3 5.4 %collective-permute-done.4.rest_5_ = bf16[1024,128]{1,0:T(8,128)(2,1)S(1)} collective-permute-done((bf16[1024,128]{1,0:T(8,128)(2,1)}, bf16[1024,128]{1,0:T(8,128)(2,1)S(1)}, u32[]{:S(2)}, u32[]{:S(2)}) %collective-permute-start.4) | collective-permute-done | bytes 262176 | tf_op jit(solution)/shard_map/ppermute | solution.py:531
  60.7 7.6 %collective-permute-done.5.rest_6_ = bf16[1024,128]{1,0:T(8,128)(2,1)S(1)} collective-permute-done((bf16[1024,128]{1,0:T(8,128)(2,1)}, bf16[1024,128]{1,0:T(8,128)(2,1)S(1)}, u32[]{:S(2)}, u32[]{:S(2)}) %collective-permute-start.5) | collective-permute-done | bytes 262176 | tf_op jit(solution)/shard_map/ppermute | solution.py:531
  68.3 4.7 %collective-permute-done.6.rest_7_ = bf16[1024,128]{1,0:T(8,128)(2,1)S(1)} collective-permute-done((bf16[1024,128]{1,0:T(8,128)(2,1)}, bf16[1024,128]{1,0:T(8,128)(2,1)S(1)}, u32[]{:S(2)}, u32[]{:S(2)}) %collective-permute-start.6) | collective-permute-done | bytes 262176 | tf_op jit(solution)/shard_map/ppermute | solution.py:531
  73.0 8.1 %own.1 = bf16[16,264,128]{2,1,0:T(8,128)(2,1)} custom-call(s32[1]{0:T(128)} %bitcast.me_ref, s32[4,16,128]{2,1,0:T(8,128)S(1)} %convert_bitcast_fusion.lab_ref, bf16[16,520,128]{2,1,0:T(8,128)(2,1)} %all-to-all-done.x_ref, bf16[1024,128]{1,0:T(8,128)(2,1)S(1)} %get-tuple-element.21.rest_0_, bf16[1024,128]{1,0:T(8,128)(2,1)S(1)} %collective-permute-done.rest_1_, ...), custom_call_target="tpu_custom_call" | custom-call | tf_op jit(solution)/shard_map/own/pallas_call | solution.py:384
  81.1 4.0 %all-to-all-start.1 = ((bf16[16,264,128]{2,1,0:T(8,128)(2,1)}), bf16[16,264,128]{2,1,0:T(8,128)(2,1)S(1)}, u32[]{:S(2)}, u32[]{:S(2)}) async-start(bf16[16,264,128]{2,1,0:T(8,128)(2,1)} %own.1), calls=%async_computation.1 | async-start | bytes 2162688 | tf_op jit(solution)/shard_map/all_to_all | solution.py:526
  85.2 2.4 %partner.1 = (bf16[264,128]{1,0:T(8,128)(2,1)S(1)}, bf16[264,128]{1,0:T(8,128)(2,1)S(1)}, bf16[264,128]{1,0:T(8,128)(2,1)S(1)}, bf16[264,128]{1,0:T(8,128)(2,1)S...) custom-call(s32[1]{0:T(128)} %bitcast.me_ref, ...), custom_call_target="tpu_custom_call" | custom-call | tf_op jit(solution)/shard_map/partner/pallas_call | solution.py:457
  87.6 0.5 collective-permute-start.7
  88.0 1.7 %collective-permute-start.8 = (bf16[264,128]{1,0:T(8,128)(2,1)S(1)}, bf16[264,128]{1,0:T(8,128)(2,1)S(1)}, u32[]{:S(2)}, u32[]{:S(2)}) collective-permute-start(bf16[264,128]{1,0:T(8,128)(2,1)S(1)} %get-tuple-element.31), channel_id=1, source_target_pairs={{0,2},{1,3},{2,0},{3,1},{4,6},{5,7},{6,4},{7,5},{8,10},{9,11},{10,... | collective-permute-start | bytes 202760 | tf_op jit(solution)/shard_map/ppermute | solution.py:531
  89.7 1.7 %collective-permute-start.10 = (bf16[264,128]{1,0:T(8,128)(2,1)S(1)}, bf16[264,128]{1,0:T(8,128)(2,1)S(1)}, u32[]{:S(2)}, u32[]{:S(2)}) collective-permute-start(bf16[264,128]{1,0:T(8,128)(2,1)S(1)} %get-tuple-element.33), channel_id=1, source_target_pairs={{0,4},{1,5},{2,6},{3,7},{4,0},{5,1},{6,2},{7,3},{8,12},{9,13},{10,... | collective-permute-start | bytes 202760 | tf_op jit(solution)/shard_map/ppermute | solution.py:531
  91.4 0.1 collective-permute-start.11
  91.5 2.6 %collective-permute-start.12 = (bf16[264,128]{1,0:T(8,128)(2,1)S(1)}, bf16[264,128]{1,0:T(8,128)(2,1)S(1)}, u32[]{:S(2)}, u32[]{:S(2)}) collective-permute-start(bf16[264,128]{1,0:T(8,128)(2,1)S(1)} %get-tuple-element.35), channel_id=1, source_target_pairs={{0,6},{1,7},{2,4},{3,5},{4,2},{5,3},{6,0},{7,1},{8,14},{9,15},{10,... | collective-permute-start | bytes 202760 | tf_op jit(solution)/shard_map/ppermute | solution.py:531
  94.1 2.9 %collective-permute-done.8.rest_2_ = bf16[264,128]{1,0:T(8,128)(2,1)S(1)} collective-permute-done((bf16[264,128]{1,0:T(8,128)(2,1)S(1)}, bf16[264,128]{1,0:T(8,128)(2,1)S(1)}, u32[]{:S(2)}, u32[]{:S(2)}) %collective-permute-start.8) | collective-permute-done | bytes 67616 | tf_op jit(solution)/shard_map/ppermute | solution.py:531
  97.0 0.7 collective-permute-done.9.rest_3_
  97.7 7.8 %collective-permute-done.10.rest_4_ = bf16[264,128]{1,0:T(8,128)(2,1)S(1)} collective-permute-done((bf16[264,128]{1,0:T(8,128)(2,1)S(1)}, bf16[264,128]{1,0:T(8,128)(2,1)S(1)}, u32[]{:S(2)}, u32[]{:S(2)}) %collective-permute-start.10) | collective-permute-done | bytes 67616 | tf_op jit(solution)/shard_map/ppermute | solution.py:531
  105.4 1.4 %collective-permute-done.11.rest_5_ = bf16[264,128]{1,0:T(8,128)(2,1)S(1)} collective-permute-done((bf16[264,128]{1,0:T(8,128)(2,1)S(1)}, bf16[264,128]{1,0:T(8,128)(2,1)S(1)}, u32[]{:S(2)}, u32[]{:S(2)}) %collective-permute-start.11) | collective-permute-done | bytes 67616 | tf_op jit(solution)/shard_map/ppermute | solution.py:531
  106.9 4.5 %collective-permute-done.12.rest_6_ = bf16[264,128]{1,0:T(8,128)(2,1)S(1)} collective-permute-done((bf16[264,128]{1,0:T(8,128)(2,1)S(1)}, bf16[264,128]{1,0:T(8,128)(2,1)S(1)}, u32[]{:S(2)}, u32[]{:S(2)}) %collective-permute-start.12) | collective-permute-done | bytes 67616 | tf_op jit(solution)/shard_map/ppermute | solution.py:531
  111.4 0.5 collective-permute-done.13.rest_7_
  111.9 1.7 %merge.1 = bf16[128,32,128]{2,1,0:T(8,128)(2,1)} custom-call(s32[1]{0:T(128)} %bitcast.me_ref, bf16[16,264,128]{2,1,0:T(8,128)(2,1)S(1)} %all-to-all-done.1.x_ref, bf16[264,128]{1,0:T(8,128)(2,1)S(1)} %get-tuple-element.29.rest_0_, bf16[264,128]{1,0:T(8,128)(2,1)S(1)} %collective-permute-done.7.rest_1_, bf16[264,128]{1,0:T(8,128)(2,1)S(1)} %collective-permute-done.8.rest_2_, ...), custom_call_target="tpu_custom_call" | custom-call | tf_op jit(solution)/shard_map/merge/pallas_call | solution.py:508
  (15 shorter events, 0.0 us)
Async XLA Ops:
  0.0 1.9 %copy-start = (bf16[128,32,384]{2,1,0:T(8,128)(2,1)S(1)}, bf16[128,32,384]{2,1,0:T(8,128)(2,1)}, u32[]{:S(2)}) copy-start(bf16[128,32,384]{2,1,0:T(8,128)(2,1)} %x_ref.3) | copy-start | bytes 9437188
  1.9 0.7 copy-start.3
  3.6 1.3 %copy-start.2 = (bf16[16,520,128]{2,1,0:T(8,128)(2,1)}, bf16[16,520,128]{2,1,0:T(8,128)(2,1)S(1)}, u32[]{:S(2)}) copy-start(bf16[16,520,128]{2,1,0:T(8,128)(2,1)S(1)} %cross.1) | copy-start | bytes 6389764
  4.9 7.7 %copy-start.1 = (bf16[128,32,384]{2,1,0:T(8,128)(2,1)S(1)}, bf16[128,32,384]{2,1,0:T(8,128)(2,1)}, u32[]{:S(2)}) copy-start(bf16[128,32,384]{2,1,0:T(8,128)(2,1)} %x_ref.3) | copy-start | bytes 9437188
  4.9 49.6 %all-to-all-start = ((bf16[16,520,128]{2,1,0:T(8,128)(2,1)}), bf16[16,520,128]{2,1,0:T(8,128)(2,1)}, u32[]{:S(2)}, u32[]{:S(2)}) async-start(bf16[16,520,128]{2,1,0:T(8,128)(2,1)} %copy-done.2), calls=%async_computation | async-start | bytes 4259840 | tf_op jit(solution)/shard_map/all_to_all | solution.py:526
  15.4 3.9 %collective-permute-start = (bf16[1024,128]{1,0:T(8,128)(2,1)S(1)}, bf16[1024,128]{1,0:T(8,128)(2,1)S(1)}, u32[]{:S(2)}, u32[]{:S(2)}) collective-permute-start(bf16[1024,128]{1,0:T(8,128)(2,1)S(1)} %get-tuple-element.22), channel_id=1, source_target_pairs={{0,1},{1,0},{2,3},{3,2},{4,5},{5,4},{6,7},{7,6},{8,9},{9,8},{10,11... | collective-permute-start | bytes 786440 | tf_op jit(solution)/shard_map/ppermute | solution.py:531
  15.8 22.2 %collective-permute-start.1 = (bf16[1024,128]{1,0:T(8,128)(2,1)S(1)}, bf16[1024,128]{1,0:T(8,128)(2,1)S(1)}, u32[]{:S(2)}, u32[]{:S(2)}) collective-permute-start(bf16[1024,128]{1,0:T(8,128)(2,1)S(1)} %get-tuple-element.23), channel_id=1, source_target_pairs={{0,2},{1,3},{2,0},{3,1},{4,6},{5,7},{6,4},{7,5},{8,10},{9,11},{10,... | collective-permute-start | bytes 786440 | tf_op jit(solution)/shard_map/ppermute | solution.py:531
  17.4 37.8 %collective-permute-start.2 = (bf16[1024,128]{1,0:T(8,128)(2,1)}, bf16[1024,128]{1,0:T(8,128)(2,1)S(1)}, u32[]{:S(2)}, u32[]{:S(2)}) collective-permute-start(bf16[1024,128]{1,0:T(8,128)(2,1)} %get-tuple-element.24), channel_id=1, source_target_pairs={{0,3},{1,2},{2,1},{3,0},{4,7},{5,6},{6,5},{7,4},{8,11},{9,10},{10,... | collective-permute-start | bytes 786440 | tf_op jit(solution)/shard_map/ppermute | solution.py:531
  17.4 37.9 %collective-permute-start.3 = (bf16[1024,128]{1,0:T(8,128)(2,1)}, bf16[1024,128]{1,0:T(8,128)(2,1)S(1)}, u32[]{:S(2)}, u32[]{:S(2)}) collective-permute-start(bf16[1024,128]{1,0:T(8,128)(2,1)} %get-tuple-element.25), channel_id=1, source_target_pairs={{0,4},{1,5},{2,6},{3,7},{4,0},{5,1},{6,2},{7,3},{8,12},{9,13},{10,... | collective-permute-start | bytes 786440 | tf_op jit(solution)/shard_map/ppermute | solution.py:531
  19.1 41.6 %collective-permute-start.4 = (bf16[1024,128]{1,0:T(8,128)(2,1)}, bf16[1024,128]{1,0:T(8,128)(2,1)S(1)}, u32[]{:S(2)}, u32[]{:S(2)}) collective-permute-start(bf16[1024,128]{1,0:T(8,128)(2,1)} %get-tuple-element.26), channel_id=1, source_target_pairs={{0,5},{1,4},{2,7},{3,6},{4,1},{5,0},{6,3},{7,2},{8,13},{9,12},{10,... | collective-permute-start | bytes 786440 | tf_op jit(solution)/shard_map/ppermute | solution.py:531
  19.3 49.0 %collective-permute-start.5 = (bf16[1024,128]{1,0:T(8,128)(2,1)}, bf16[1024,128]{1,0:T(8,128)(2,1)S(1)}, u32[]{:S(2)}, u32[]{:S(2)}) collective-permute-start(bf16[1024,128]{1,0:T(8,128)(2,1)} %get-tuple-element.27), channel_id=1, source_target_pairs={{0,6},{1,7},{2,4},{3,5},{4,2},{5,3},{6,0},{7,1},{8,14},{9,15},{10,... | collective-permute-start | bytes 786440 | tf_op jit(solution)/shard_map/ppermute | solution.py:531
  38.0 35.0 %collective-permute-start.6 = (bf16[1024,128]{1,0:T(8,128)(2,1)}, bf16[1024,128]{1,0:T(8,128)(2,1)S(1)}, u32[]{:S(2)}, u32[]{:S(2)}) collective-permute-start(bf16[1024,128]{1,0:T(8,128)(2,1)} %get-tuple-element.28), channel_id=1, source_target_pairs={{0,7},{1,6},{2,5},{3,4},{4,3},{5,2},{6,1},{7,0},{8,15},{9,14},{10,... | collective-permute-start | bytes 786440 | tf_op jit(solution)/shard_map/ppermute | solution.py:531
  81.1 30.8 %all-to-all-start.1 = ((bf16[16,264,128]{2,1,0:T(8,128)(2,1)}), bf16[16,264,128]{2,1,0:T(8,128)(2,1)S(1)}, u32[]{:S(2)}, u32[]{:S(2)}) async-start(bf16[16,264,128]{2,1,0:T(8,128)(2,1)} %own.1), calls=%async_computation.1 | async-start | bytes 2162688 | tf_op jit(solution)/shard_map/all_to_all | solution.py:526
  87.6 4.0 %collective-permute-start.7 = (bf16[264,128]{1,0:T(8,128)(2,1)S(1)}, bf16[264,128]{1,0:T(8,128)(2,1)S(1)}, u32[]{:S(2)}, u32[]{:S(2)}) collective-permute-start(bf16[264,128]{1,0:T(8,128)(2,1)S(1)} %get-tuple-element.30), channel_id=1, source_target_pairs={{0,1},{1,0},{2,3},{3,2},{4,5},{5,4},{6,7},{7,6},{8,9},{9,8},{10,11... | collective-permute-start | bytes 202760 | tf_op jit(solution)/shard_map/ppermute | solution.py:531
  88.0 9.0 %collective-permute-start.8 = (bf16[264,128]{1,0:T(8,128)(2,1)S(1)}, bf16[264,128]{1,0:T(8,128)(2,1)S(1)}, u32[]{:S(2)}, u32[]{:S(2)}) collective-permute-start(bf16[264,128]{1,0:T(8,128)(2,1)S(1)} %get-tuple-element.31), channel_id=1, source_target_pairs={{0,2},{1,3},{2,0},{3,1},{4,6},{5,7},{6,4},{7,5},{8,10},{9,11},{10,... | collective-permute-start | bytes 202760 | tf_op jit(solution)/shard_map/ppermute | solution.py:531
  89.7 7.9 %collective-permute-start.9 = (bf16[264,128]{1,0:T(8,128)(2,1)S(1)}, bf16[264,128]{1,0:T(8,128)(2,1)S(1)}, u32[]{:S(2)}, u32[]{:S(2)}) collective-permute-start(bf16[264,128]{1,0:T(8,128)(2,1)S(1)} %get-tuple-element.32), channel_id=1, source_target_pairs={{0,3},{1,2},{2,1},{3,0},{4,7},{5,6},{6,5},{7,4},{8,11},{9,10},{10,... | collective-permute-start | bytes 202760 | tf_op jit(solution)/shard_map/ppermute | solution.py:531
  89.7 15.7 %collective-permute-start.10 = (bf16[264,128]{1,0:T(8,128)(2,1)S(1)}, bf16[264,128]{1,0:T(8,128)(2,1)S(1)}, u32[]{:S(2)}, u32[]{:S(2)}) collective-permute-start(bf16[264,128]{1,0:T(8,128)(2,1)S(1)} %get-tuple-element.33), channel_id=1, source_target_pairs={{0,4},{1,5},{2,6},{3,7},{4,0},{5,1},{6,2},{7,3},{8,12},{9,13},{10,... | collective-permute-start | bytes 202760 | tf_op jit(solution)/shard_map/ppermute | solution.py:531
  91.4 15.5 %collective-permute-start.11 = (bf16[264,128]{1,0:T(8,128)(2,1)S(1)}, bf16[264,128]{1,0:T(8,128)(2,1)S(1)}, u32[]{:S(2)}, u32[]{:S(2)}) collective-permute-start(bf16[264,128]{1,0:T(8,128)(2,1)S(1)} %get-tuple-element.34), channel_id=1, source_target_pairs={{0,5},{1,4},{2,7},{3,6},{4,1},{5,0},{6,3},{7,2},{8,13},{9,12},{10,... | collective-permute-start | bytes 202760 | tf_op jit(solution)/shard_map/ppermute | solution.py:531
  91.5 19.9 %collective-permute-start.12 = (bf16[264,128]{1,0:T(8,128)(2,1)S(1)}, bf16[264,128]{1,0:T(8,128)(2,1)S(1)}, u32[]{:S(2)}, u32[]{:S(2)}) collective-permute-start(bf16[264,128]{1,0:T(8,128)(2,1)S(1)} %get-tuple-element.35), channel_id=1, source_target_pairs={{0,6},{1,7},{2,4},{3,5},{4,2},{5,3},{6,0},{7,1},{8,14},{9,15},{10,... | collective-permute-start | bytes 202760 | tf_op jit(solution)/shard_map/ppermute | solution.py:531
  97.0 14.9 %collective-permute-start.13 = (bf16[264,128]{1,0:T(8,128)(2,1)S(1)}, bf16[264,128]{1,0:T(8,128)(2,1)S(1)}, u32[]{:S(2)}, u32[]{:S(2)}) collective-permute-start(bf16[264,128]{1,0:T(8,128)(2,1)S(1)} %get-tuple-element.36), channel_id=1, source_target_pairs={{0,7},{1,6},{2,5},{3,4},{4,3},{5,2},{6,1},{7,0},{8,15},{9,14},{10,... | collective-permute-start | bytes 202760 | tf_op jit(solution)/shard_map/ppermute | solution.py:531

commit v6 on v5

--- a/solution.py
+++ b/solution.py
@@ -11,7 +11,6 @@
 CLEN = 1024
 QB = 256
 STEP = 64
-SPREAD_MB = 12
 NEG = -1e30
 
 
@@ -155,10 +154,11 @@
     )(labels, x)
 
 
-def cross_kernel(x_ref, lab_ref, o_ref):
+def cross_kernel(me_ref, x_ref, lab_ref, o_ref):
     tok, heads, width = x_ref.shape
     nseq = o_ref.shape[0]
     half = nseq // 2
+    lane = pl.multiple_of(jnp.where(me_ref[0] >= half, 0, 128), 128)
     pad = jnp.zeros((4, 128), jnp.float32)
     for dst in range(nseq):
         other = dst ^ half
@@ -168,14 +168,14 @@
             jnp.bfloat16
         )
     for first in range(0, tok, 32):
-        for part in range(3):
-            low = heads // 2 if part == 2 else 0
-            high = heads // 2 if part == 0 else heads
-            piece = x_ref[first : first + 32, low:high, part * 128 : (part + 1) * 128]
-            turned = jnp.swapaxes(piece.astype(jnp.float32), 0, 1).astype(jnp.bfloat16)
-            for head in range(low, high):
-                row = (head % 2 + (0 if part == 1 else 2)) * tok + first
-                o_ref[head // 2, row : row + 32, :] = turned[head - low]
+        piece = x_ref[first : first + 32, :, pl.ds(lane, 256)].astype(jnp.float32)
+        turned = jnp.swapaxes(piece, 0, 1).astype(jnp.bfloat16)
+        for head in range(heads):
+            for part in range(2):
+                row = (2 * part + head % 2) * tok + first
+                o_ref[head // 2, row : row + 32, :] = turned[
+                    head, :, part * 128 : (part + 1) * 128
+                ]
 
 
 def near_kernel(me_ref, x_ref, *rest):
@@ -191,7 +191,7 @@
                 turn_ref[head, part, first : first + 32, :] = turned[
                     head, :, part * 128 : (part + 1) * 128
                 ]
-    near_part = jnp.where(me >= half, 0, 2)
+    near_part = jnp.where(me >= half, 2, 0)
     for k, near_ref in enumerate(near_refs):
         dst = me ^ k
         other = dst ^ half
@@ -205,20 +205,20 @@
 def spread(me, qkv, labels, nseq):
     tok, heads, width = qkv.shape
     whole = pl.BlockSpec(memory_space=pltpu.VMEM)
-    params = pltpu.CompilerParams(vmem_limit_bytes=SPREAD_MB << 20)
+    scalar = pl.BlockSpec(memory_space=pltpu.SMEM)
+    params = pltpu.CompilerParams(vmem_limit_bytes=12 << 20)
     cross = pl.pallas_call(
         cross_kernel,
         out_shape=jax.ShapeDtypeStruct((nseq, 4 * tok + 8, 128), jnp.bfloat16),
-        in_specs=[whole, whole],
+        in_specs=[scalar, whole, whole],
         out_specs=whole,
         compiler_params=params,
         name="cross",
-    )(qkv, labels)
-    near = jax.ShapeDtypeStruct((8 * tok, 128), jnp.bfloat16)
+    )(me, qkv, labels)
     near = pl.pallas_call(
         near_kernel,
-        out_shape=[near] * (nseq // 2),
-        in_specs=[pl.BlockSpec(memory_space=pltpu.SMEM), whole],
+        out_shape=[jax.ShapeDtypeStruct((8 * tok, 128), jnp.bfloat16)] * (nseq // 2),
+        in_specs=[scalar, whole],
         out_specs=[whole] * (nseq // 2),
         scratch_shapes=[pltpu.VMEM((heads, 3, tok, 128), jnp.bfloat16)],
         compiler_params=params,
@@ -276,107 +276,131 @@
     return jnp.concatenate(rows, axis=0).astype(jnp.bfloat16)
 
 
-def own_kernel(me_ref, lab_ref, x_ref, *rest, tok, rate):
+def finish(both, peak, rate, tok):
+    num, total = both[:, :128], both[:, 128:]
+    lse = peak * rate + jnp.log2(total)
+    rows = [jnp.transpose(lse[i : i + tok, :])[:1, :] for i in range(0, QB, tok)]
+    return num / total, rows
+
+
+def far_kernel(lab_ref, x_ref, o_ref, stat_ref, v_ref, *, tok, rate):
     nseq = x_ref.shape[0]
     half = nseq // 2
     span = half * tok
+    per = QB // tok
+    for j in range(2):
+        v_ref[j, :, :128] = x_ref[:half, (2 + j) * tok : (3 + j) * tok, :].reshape(span, 128)
+        v_ref[j, :, 128:] = jnp.ones((span, 128), jnp.bfloat16)
+
+    def score(j, block):
+        first = half + block * per
+        q = x_ref[first : first + per, j * tok : (j + 1) * tok, :].reshape(QB, 128)
+        return dot_t(q, x_ref[:half, j * tok : (j + 1) * tok, :].reshape(span, 128))
+
+    def weigh(j, block, s):
+        first = half + block * per
+        lab_q = columns([lab_ref[j, first + i : first + i + 1, :] for i in range(per)])
+        return soften(s, lab_q, [lab_ref[j, i : i + 1, :] for i in range(half)], None, rate)
+
+    def blend(j, block, weights, peak):
+        both = jnp.dot(weights, v_ref[j], preferred_element_type=jnp.float32)
+        out, rows = finish(both, peak, rate, tok)
+        for i, row in enumerate(rows):
+            stat_ref[j, block * per + i : block * per + i + 1, :] = row
+        o_ref[j, block * QB : (block + 1) * QB, :] = out
+
+    run_tasks([(j, block) for block in range(span // QB) for j in range(2)], score, weigh, blend)
+
+
+def far_of(labels, x, tok, rate):
+    half = x.shape[0] // 2
+    whole = pl.BlockSpec(memory_space=pltpu.VMEM)
+    return pl.pallas_call(
+        functools.partial(far_kernel, tok=tok, rate=rate),
+        out_shape=[
+            jax.ShapeDtypeStruct((2, half * tok, 128), jnp.float32),
+            jax.ShapeDtypeStruct((2, half, 128), jnp.float32),
+        ],
+        in_specs=[whole, whole],
+        out_specs=[whole, whole],
+        scratch_shapes=[pltpu.VMEM((2, half * tok, 256), jnp.bfloat16)],
+        compiler_params=pltpu.CompilerParams(vmem_limit_bytes=16 << 20),
+        name="far",
+    )(labels, x)
+
+
+def own_kernel(me_ref, lab_ref, x_ref, far_ref, far_stat_ref, *rest, tok, rate):
+    half = x_ref.shape[0] // 2
     near_refs, o_ref = rest[:half], rest[half]
-    q_ref, v_ref, num_ref, sum_ref, peak_ref, stat_ref = rest[half + 1 :]
+    q_ref, k_ref, v_ref = rest[half + 1 :]
+    span = half * tok
+    per = QB // tok
     me = me_ref[0]
     upper = me >= half
     up = upper.astype(jnp.int32)
-    for j in range(2):
-        for slot in range(2):
-            v_ref[j, slot, :, 128:] = jnp.ones((span, 128), jnp.bfloat16)
+    places = [pl.ds(pl.multiple_of(((me ^ k) % half) * tok, tok), tok) for k in range(half)]
 
     @pl.when(upper)
     def _():
         for j in range(2):
-            for k, near_ref in enumerate(near_refs):
-                place = pl.multiple_of(((me ^ k) % half) * tok, tok)
-                q_ref[j, 1, pl.ds(place, tok), :] = near_ref[j * tok : (j + 1) * tok, :]
-            for slot in range(2):
-                v_ref[j, slot, :, :128] = x_ref[
-                    slot * half : (slot + 1) * half, (2 + j) * tok : (3 + j) * tok, :
-                ].reshape(span, 128)
+            q_ref[j] = x_ref[half:, j * tok : (j + 1) * tok, :].reshape(span, 128)
+            k_ref[j] = x_ref[half:, (2 + j) * tok : (3 + j) * tok, :].reshape(span, 128)
+            for place, near_ref in zip(places, near_refs):
+                v_ref[j, place, :128] = near_ref[j * tok : (j + 1) * tok, :]
 
     @pl.when(jnp.logical_not(upper))
     def _():
         for j in range(2):
-            for k, near_ref in enumerate(near_refs):
-                place = pl.multiple_of(((me ^ k) % half) * tok, tok)
-                v_ref[j, 0, pl.ds(place, tok), :128] = near_ref[j * tok : (j + 1) * tok, :]
-            for slot in range(2):
-                q_ref[j, slot] = x_ref[
-                    slot * half : (slot + 1) * half, (2 + j) * tok : (3 + j) * tok, :
-                ].reshape(span, 128)
-
-    def keys(j, first, count):
-        return x_ref[pl.ds(first, count), j * tok : (j + 1) * tok, :].reshape(count * tok, 128)
+            k_ref[j] = x_ref[:half, j * tok : (j + 1) * tok, :].reshape(span, 128)
+            v_ref[j, :, :128] = x_ref[:half, (2 + j) * tok : (3 + j) * tok, :].reshape(span, 128)
+            for place, near_ref in zip(places, near_refs):
+                q_ref[j, place, :] = near_ref[j * tok : (j + 1) * tok, :]
+
+    for j in range(2):
+        v_ref[j, :, 128:] = jnp.ones((span, 128), jnp.bfloat16)
 
     def lab_of(j, first, count):
-        return [lab_ref[j, pl.ds(first + i, 1), :] for i in range(count)]
-
-    per = QB // tok
-
-    def score(cross, j, block):
-        rows = pl.ds(block * QB, QB)
-        if cross:
-            return dot_t(q_ref[j, 1, rows, :], keys(j, 0, half))
-        return dot_t(q_ref[j, up, rows, :], keys(j, up * half, (block + 1) * per))
-
-    def weigh(cross, j, block, s):
-        if cross:
-            lab_q = columns(lab_of(j, half + block * per, per))
-            return soften(s, lab_q, lab_of(j, 0, half), None, rate)
-        lab_q = columns(lab_of(j, up * half + block * per, per))
-        lab_k = lab_of(j, up * half, (block + 1) * per)
-        return soften(s, lab_q, lab_k, block * QB, rate)
-
-    def blend(cross, j, block, weights, peak):
-        rows = pl.ds(block * QB, QB)
-        if cross:
-            both = jnp.dot(weights, v_ref[j, 0], preferred_element_type=jnp.float32)
-            num, total = both[:, :128], both[:, 128:]
-            num_ref[j, rows, :] = num
-            sum_ref[j, rows, :] = total
-            peak_ref[j, rows, :] = peak
-            lse = peak * rate + jnp.log2(total)
-            for i in range(per):
-                turned = jnp.transpose(lse[i * tok : (i + 1) * tok, :])
-                stat_ref[j, block * per + i : block * per + i + 1, :] = turned[:1, :]
-            out = num / total
-            first = (1 - up) * half + block * per
-        else:
-            both = jnp.dot(
-                weights, v_ref[j, up, : (block + 1) * QB, :], preferred_element_type=jnp.float32
-            )
-            far = jnp.where(upper, peak_ref[j, rows, :], NEG)
-            top = jnp.maximum(peak, far)
-            here = jnp.exp2((peak - top) * rate)
-            there = jnp.exp2((far - top) * rate)
-            num = both[:, :128] * here + num_ref[j, rows, :] * there
-            out = num / (both[:, 128:] * here + sum_ref[j, rows, :] * there)
-            first = up * half + block * per
-        o_ref[pl.ds(first, per), j * tok : (j + 1) * tok, :] = out.astype(jnp.bfloat16).reshape(
-            per, tok, 128
+        return [lab_ref[j, pl.ds(up * half + first + i, 1), :] for i in range(count)]
+
+    def score(j, block):
+        return dot_t(q_ref[j, block * QB : (block + 1) * QB, :], k_ref[j, : (block + 1) * QB, :])
+
+    def weigh(j, block, s):
+        lab_q = columns(lab_of(j, block * per, per))
+        return soften(s, lab_q, lab_of(j, 0, (block + 1) * per), block * QB, rate)
+
+    def blend(j, block, weights, peak):
+        both = jnp.dot(
+            weights, v_ref[j, : (block + 1) * QB, :], preferred_element_type=jnp.float32
         )
+        total = both[:, 128:]
+        near = both[:, :128] / total
+        rows = [
+            far_stat_ref[j, i : i + 1, :] for i in range(block * per, (block + 1) * per)
+        ]
+        gap = peak * rate + jnp.log2(total) - columns(rows)
+        weight = jnp.where(upper, 1.0 / (1.0 + jnp.exp2(gap)), 0.0)
+        far = far_ref[j, block * QB : (block + 1) * QB, :]
+        out = near + (far - near) * weight
+        o_ref[pl.ds(up * half + block * per, per), j * tok : (j + 1) * tok, :] = out.astype(
+            jnp.bfloat16
+        ).reshape(per, tok, 128)
+        o_ref[pl.ds((1 - up) * half + block * per, per), j * tok : (j + 1) * tok, :] = far.astype(
+            jnp.bfloat16
+        ).reshape(per, tok, 128)
 
     blocks = span // QB
-    tasks = [(True, j, block) for block in range(blocks) for j in range(2)]
-    tasks += [
-        (False, j, block if j == 0 else blocks - 1 - block)
-        for block in range(blocks)
-        for j in range(2)
+    tasks = [
+        (j, block if j == 0 else blocks - 1 - block) for block in range(blocks) for j in range(2)
     ]
     run_tasks(tasks, score, weigh, blend)
     for i in range(half):
-        stats = three_parts([stat_ref[j, i : i + 1, :] for j in range(2)])
+        stats = three_parts([far_stat_ref[j, i : i + 1, :] for j in range(2)])
         o_ref[(1 - up) * half + i, 2 * tok : 2 * tok + 8, :] = stats
         o_ref[up * half + i, 2 * tok : 2 * tok + 8, :] = jnp.zeros((8, 128), jnp.bfloat16)
 
 
-def own(me, labels, x, near, tok, rate):
+def own(me, labels, x, far, near, tok, rate):
     nseq = x.shape[0]
     half = nseq // 2
     span = half * tok
@@ -384,19 +408,16 @@
     return pl.pallas_call(
         functools.partial(own_kernel, tok=tok, rate=rate),
         out_shape=jax.ShapeDtypeStruct((nseq, 2 * tok + 8, 128), jnp.bfloat16),
-        in_specs=[pl.BlockSpec(memory_space=pltpu.SMEM)] + [whole] * (2 + half),
+        in_specs=[pl.BlockSpec(memory_space=pltpu.SMEM)] + [whole] * (4 + half),
         out_specs=whole,
         scratch_shapes=[
-            pltpu.VMEM((2, 2, span, 128), jnp.bfloat16),
-            pltpu.VMEM((2, 2, span, 256), jnp.bfloat16),
-            pltpu.VMEM((2, span, 128), jnp.float32),
-            pltpu.VMEM((2, span, 128), jnp.float32),
-            pltpu.VMEM((2, span, 128), jnp.float32),
-            pltpu.VMEM((2, half, 128), jnp.float32),
+            pltpu.VMEM((2, span, 128), jnp.bfloat16),
+            pltpu.VMEM((2, span, 128), jnp.bfloat16),
+            pltpu.VMEM((2, span, 256), jnp.bfloat16),
         ],
-        compiler_params=pltpu.CompilerParams(vmem_limit_bytes=20 << 20),
+        compiler_params=pltpu.CompilerParams(vmem_limit_bytes=16 << 20),
         name="own",
-    )(me, labels, x, *near)
+    )(me, labels, x, *far, *near)
 
 
 def partner_kernel(me_ref, lab_ref, *rest, tok, rate):
@@ -535,7 +556,8 @@
     near = swap(near)
     cross = exchange(cross)
     labels = jnp.transpose(cross[:, 4 * tok : 4 * tok + 4, :].astype(jnp.int32), (1, 0, 2))
-    back = exchange(own(me, labels, cross, near, tok, rate))
+    far = far_of(labels, cross, tok, rate)
+    back = exchange(own(me, labels, cross, far, near, tok, rate))
     near_back = swap(partner(me, labels, near, tok, rate))
     return merge(me, back, near_back, tok)
 

time: 114 us -> 111 us (0.974)
  waiting for transfers between devices: 68.1 us -> 62.8 us
  local copies, waits for them, and re-layouts: 4.67 us -> 5.83 us
    ppermute x14, waiting for transfers between devices: 51.6 us -> 46.4 us  [swap(): moved[k] = lax.ppermute(blocks[k], 'seq', [(i, i ^ k) for i in range(nseq)])]
    pallas_call x1, Pallas kernels: 8.14 us -> 4.79 us  [own(): pl.pallas_call(functools.partial(own_kernel, tok=tok, rate=rate), out_sha...]
    pallas_call x1 -> x2, Pallas kernels: 2.81 us -> 6.04 us  [the longest x1 3.25 us: far_of(): pl.pallas_call(functools.partial(far_kernel, tok=tok, rate=rate), out_sha...]
    unnamed x8, local copies, waits for them, and re-layouts: 3.91 us -> 5.82 us
  transfers between devices with their start and end apart: 16 -> 16, of which waited for: 11 -> 11; matrix products, arithmetic and copies ran while one was open for 1% -> 0% of each run, Pallas kernels for 5% -> 9%
where the time goes in v6:
time: 111 us; the launch traced here: 110 us
  waiting for transfers between devices  62.8 us (57%)
  starting transfers between devices  24.4 us (22%)
  Pallas kernels  17.2 us (15%)
  local copies, waits for them, and re-layouts  5.83 us (5%)
    ppermute x14, waiting for transfers between devices, swap(): moved[k] = lax.ppermute(blocks[k], 'seq', [(i, i ^ k) for i in range(nseq)])  46.4 us
    all_to_all x2, waiting for transfers between devices, exchange(): return lax.all_to_all(x, 'seq', split_axis=0, concat_axis=0, tiled=True)  16.4 us
    ppermute x14, starting transfers between devices, swap(): moved[k] = lax.ppermute(blocks[k], 'seq', [(i, i ^ k) for i in range(nseq)])  13 us
    all_to_all x2, starting transfers between devices, exchange(): return lax.all_to_all(x, 'seq', split_axis=0, concat_axis=0, tiled=True)  11.3 us
    unnamed x8, local copies, waits for them, and re-layouts  5.82 us
    pallas_call x1, Pallas kernels, own(): pl.pallas_call(functools.partial(own_kernel, tok=tok, rate=rate), out_sha...  4.79 us
    pallas_call x1, Pallas kernels, partner(): pl.pallas_call(functools.partial(partner_kernel, tok=tok, rate=rate), out...  3.52 us
    pallas_call x1, Pallas kernels, far_of(): pl.pallas_call(functools.partial(far_kernel, tok=tok, rate=rate), out_sha...  3.25 us
  transfers between devices with their start and end apart: 16, of which 11 were waited for; matrix products, arithmetic and copies ran while one was open for 0% of the time, Pallas kernels for 9%

profile of v6, /device:TPU:0, one launch (start us, length us, event | category | flops | bytes accessed | tf_op | source)
XLA Modules:
  0.0 110.2 jit_solution(3177122317818646574)
XLA Ops:
  0.0 1.9 %copy-done = bf16[128,32,384]{2,1,0:T(8,128)(2,1)S(1)} copy-done((bf16[128,32,384]{2,1,0:T(8,128)(2,1)S(1)}, bf16[128,32,384]{2,1,0:T(8,128)(2,1)}, u32[]{:S(2)}) %copy-start) | copy-done | bytes 3145752
  1.9 0.7 copy-done.3
  2.6 1.1 cross.1
  3.7 1.3 %copy-done.2 = bf16[16,520,128]{2,1,0:T(8,128)(2,1)} copy-done((bf16[16,520,128]{2,1,0:T(8,128)(2,1)}, bf16[16,520,128]{2,1,0:T(8,128)(2,1)S(1)}, u32[]{:S(2)}) %copy-start.2) | copy-done | bytes 2129944
  5.0 7.4 %all-to-all-start = ((bf16[16,520,128]{2,1,0:T(8,128)(2,1)}), bf16[16,520,128]{2,1,0:T(8,128)(2,1)S(1)}, u32[]{:S(2)}, u32[]{:S(2)}) async-start(bf16[16,520,128]{2,1,0:T(8,128)(2,1)} %copy-done.2), calls=%async_computation | async-start | bytes 4259840 | tf_op jit(solution)/shard_map/all_to_all | solution.py:547
  12.4 1.9 %copy-done.1 = bf16[128,32,384]{2,1,0:T(8,128)(2,1)S(1)} copy-done((bf16[128,32,384]{2,1,0:T(8,128)(2,1)S(1)}, bf16[128,32,384]{2,1,0:T(8,128)(2,1)}, u32[]{:S(2)}) %copy-start.1) | copy-done | bytes 3145752
  14.3 2.8 %near.1 = (bf16[1024,128]{1,0:T(8,128)(2,1)S(1)}, bf16[1024,128]{1,0:T(8,128)(2,1)S(1)}, bf16[1024,128]{1,0:T(8,128)(2,1)S(1)}, bf16[1024,128]{1,0:T(8,128)(2,1)...) custom-call(s32[1]{0:T(128)} %bitcast.me_ref, ...), custom_call_target="tpu_custom_call" | custom-call | tf_op jit(solution)/shard_map/near/pallas_call | solution.py:218
  17.1 0.4 collective-permute-start
  17.5 1.7 %collective-permute-start.1 = (bf16[1024,128]{1,0:T(8,128)(2,1)S(1)}, bf16[1024,128]{1,0:T(8,128)(2,1)S(1)}, u32[]{:S(2)}, u32[]{:S(2)}) collective-permute-start(bf16[1024,128]{1,0:T(8,128)(2,1)S(1)} %get-tuple-element.27), channel_id=1, source_target_pairs={{0,2},{1,3},{2,0},{3,1},{4,6},{5,7},{6,4},{7,5},{8,10},{9,11},{10,... | collective-permute-start | bytes 786440 | tf_op jit(solution)/shard_map/ppermute | solution.py:552
  19.2 1.7 %collective-permute-start.3 = (bf16[1024,128]{1,0:T(8,128)(2,1)}, bf16[1024,128]{1,0:T(8,128)(2,1)S(1)}, u32[]{:S(2)}, u32[]{:S(2)}) collective-permute-start(bf16[1024,128]{1,0:T(8,128)(2,1)} %get-tuple-element.29), channel_id=1, source_target_pairs={{0,4},{1,5},{2,6},{3,7},{4,0},{5,1},{6,2},{7,3},{8,12},{9,13},{10,... | collective-permute-start | bytes 786440 | tf_op jit(solution)/shard_map/ppermute | solution.py:552
  21.0 2.6 %collective-permute-start.5 = (bf16[1024,128]{1,0:T(8,128)(2,1)}, bf16[1024,128]{1,0:T(8,128)(2,1)}, u32[]{:S(2)}, u32[]{:S(2)}) collective-permute-start(bf16[1024,128]{1,0:T(8,128)(2,1)} %get-tuple-element.31), channel_id=1, source_target_pairs={{0,6},{1,7},{2,4},{3,5},{4,2},{5,3},{6,0},{7,1},{8,14},{9,15},{10,... | collective-permute-start | bytes 786440 | tf_op jit(solution)/shard_map/ppermute | solution.py:552
  23.6 14.3 %collective-permute-done.1.rest_2_ = bf16[1024,128]{1,0:T(8,128)(2,1)S(1)} collective-permute-done((bf16[1024,128]{1,0:T(8,128)(2,1)S(1)}, bf16[1024,128]{1,0:T(8,128)(2,1)S(1)}, u32[]{:S(2)}, u32[]{:S(2)}) %collective-permute-start.1) | collective-permute-done | bytes 262176 | tf_op jit(solution)/shard_map/ppermute | solution.py:552
  37.8 16.4 %all-to-all-done.x_ref = bf16[16,520,128]{2,1,0:T(8,128)(2,1)S(1)} async-done(((bf16[16,520,128]{2,1,0:T(8,128)(2,1)}), bf16[16,520,128]{2,1,0:T(8,128)(2,1)S(1)}, u32[]{:S(2)}, u32[]{:S(2)}) %all-to-all-start) | async-done | bytes 2129952 | tf_op jit(solution)/shard_map/all_to_all | solution.py:547
  54.3 3.2 %far.1 = (f32[2,1024,128]{2,1,0:T(8,128)S(1)}, f32[2,8,128]{2,1,0:T(8,128)S(1)}) custom-call(s32[4,16,128]{2,1,0:T(8,128)S(1)} %convert_bitcast_fusion.lab_ref, bf16[16,520,128]{2,1,0:T(8,128)(2,1)S(1)} %all-to-all-done.x_ref), custom_call_target="tpu_custom_call" | custom-call | tf_op jit(solution)/shard_map/far/pallas_call | solution.py:318
  57.5 3.1 %collective-permute-done.4.rest_5_ = bf16[1024,128]{1,0:T(8,128)(2,1)} collective-permute-done((bf16[1024,128]{1,0:T(8,128)(2,1)}, bf16[1024,128]{1,0:T(8,128)(2,1)}, u32[]{:S(2)}, u32[]{:S(2)}) %collective-permute-start.4) | collective-permute-done | bytes 262176 | tf_op jit(solution)/shard_map/ppermute | solution.py:552
  60.7 7.6 %collective-permute-done.5.rest_6_ = bf16[1024,128]{1,0:T(8,128)(2,1)} collective-permute-done((bf16[1024,128]{1,0:T(8,128)(2,1)}, bf16[1024,128]{1,0:T(8,128)(2,1)}, u32[]{:S(2)}, u32[]{:S(2)}) %collective-permute-start.5) | collective-permute-done | bytes 262176 | tf_op jit(solution)/shard_map/ppermute | solution.py:552
  68.2 4.7 %collective-permute-done.6.rest_7_ = bf16[1024,128]{1,0:T(8,128)(2,1)} collective-permute-done((bf16[1024,128]{1,0:T(8,128)(2,1)}, bf16[1024,128]{1,0:T(8,128)(2,1)}, u32[]{:S(2)}, u32[]{:S(2)}) %collective-permute-start.6) | collective-permute-done | bytes 262176 | tf_op jit(solution)/shard_map/ppermute | solution.py:552
  72.9 4.8 %own.1 = bf16[16,264,128]{2,1,0:T(8,128)(2,1)} custom-call(s32[1]{0:T(128)} %bitcast.me_ref, s32[4,16,128]{2,1,0:T(8,128)S(1)} %convert_bitcast_fusion.lab_ref, bf16[16,520,128]{2,1,0:T(8,128)(2,1)S(1)} %all-to-all-done.x_ref, f32[2,1024,128]{2,1,0:T(8,128)S(1)} %get-tuple-element.23.far_ref, f32[2,8,128]{2,1,0:T(8,128)S(1)} %get-tuple-element.24.far_stat_ref, ...), custom_call_target="tpu_custom_call" | custom-call | tf_op jit(solution)/shard_map/own/pallas_call | solution.py:408
  77.7 4.0 %all-to-all-start.1 = ((bf16[16,264,128]{2,1,0:T(8,128)(2,1)}), bf16[16,264,128]{2,1,0:T(8,128)(2,1)S(1)}, u32[]{:S(2)}, u32[]{:S(2)}) async-start(bf16[16,264,128]{2,1,0:T(8,128)(2,1)} %own.1), calls=%async_computation.1 | async-start | bytes 2162688 | tf_op jit(solution)/shard_map/all_to_all | solution.py:547
  81.7 3.5 %partner.1 = (bf16[264,128]{1,0:T(8,128)(2,1)S(1)}, bf16[264,128]{1,0:T(8,128)(2,1)S(1)}, bf16[264,128]{1,0:T(8,128)(2,1)S(1)}, bf16[264,128]{1,0:T(8,128)(2,1)S...) custom-call(s32[1]{0:T(128)} %bitcast.me_ref, ...), custom_call_target="tpu_custom_call" | custom-call | tf_op jit(solution)/shard_map/partner/pallas_call | solution.py:478
  85.2 0.5 collective-permute-start.7
  85.7 1.7 %collective-permute-start.8 = (bf16[264,128]{1,0:T(8,128)(2,1)S(1)}, bf16[264,128]{1,0:T(8,128)(2,1)S(1)}, u32[]{:S(2)}, u32[]{:S(2)}) collective-permute-start(bf16[264,128]{1,0:T(8,128)(2,1)S(1)} %get-tuple-element.35), channel_id=1, source_target_pairs={{0,2},{1,3},{2,0},{3,1},{4,6},{5,7},{6,4},{7,5},{8,10},{9,11},{10,... | collective-permute-start | bytes 202760 | tf_op jit(solution)/shard_map/ppermute | solution.py:552
  87.4 1.7 %collective-permute-start.10 = (bf16[264,128]{1,0:T(8,128)(2,1)S(1)}, bf16[264,128]{1,0:T(8,128)(2,1)S(1)}, u32[]{:S(2)}, u32[]{:S(2)}) collective-permute-start(bf16[264,128]{1,0:T(8,128)(2,1)S(1)} %get-tuple-element.37), channel_id=1, source_target_pairs={{0,4},{1,5},{2,6},{3,7},{4,0},{5,1},{6,2},{7,3},{8,12},{9,13},{10,... | collective-permute-start | bytes 202760 | tf_op jit(solution)/shard_map/ppermute | solution.py:552
  89.1 0.1 collective-permute-start.11
  89.2 2.6 %collective-permute-start.12 = (bf16[264,128]{1,0:T(8,128)(2,1)S(1)}, bf16[264,128]{1,0:T(8,128)(2,1)S(1)}, u32[]{:S(2)}, u32[]{:S(2)}) collective-permute-start(bf16[264,128]{1,0:T(8,128)(2,1)S(1)} %get-tuple-element.39), channel_id=1, source_target_pairs={{0,6},{1,7},{2,4},{3,5},{4,2},{5,3},{6,0},{7,1},{8,14},{9,15},{10,... | collective-permute-start | bytes 202760 | tf_op jit(solution)/shard_map/ppermute | solution.py:552
  91.8 1.8 %collective-permute-done.8.rest_2_ = bf16[264,128]{1,0:T(8,128)(2,1)S(1)} collective-permute-done((bf16[264,128]{1,0:T(8,128)(2,1)S(1)}, bf16[264,128]{1,0:T(8,128)(2,1)S(1)}, u32[]{:S(2)}, u32[]{:S(2)}) %collective-permute-start.8) | collective-permute-done | bytes 67616 | tf_op jit(solution)/shard_map/ppermute | solution.py:552
  93.6 1.4 %collective-permute-done.9.rest_3_ = bf16[264,128]{1,0:T(8,128)(2,1)S(1)} collective-permute-done((bf16[264,128]{1,0:T(8,128)(2,1)S(1)}, bf16[264,128]{1,0:T(8,128)(2,1)S(1)}, u32[]{:S(2)}, u32[]{:S(2)}) %collective-permute-start.9) | collective-permute-done | bytes 67616 | tf_op jit(solution)/shard_map/ppermute | solution.py:552
  94.9 7.0 %collective-permute-done.10.rest_4_ = bf16[264,128]{1,0:T(8,128)(2,1)S(1)} collective-permute-done((bf16[264,128]{1,0:T(8,128)(2,1)S(1)}, bf16[264,128]{1,0:T(8,128)(2,1)S(1)}, u32[]{:S(2)}, u32[]{:S(2)}) %collective-permute-start.10) | collective-permute-done | bytes 67616 | tf_op jit(solution)/shard_map/ppermute | solution.py:552
  101.9 1.4 %collective-permute-done.11.rest_5_ = bf16[264,128]{1,0:T(8,128)(2,1)S(1)} collective-permute-done((bf16[264,128]{1,0:T(8,128)(2,1)S(1)}, bf16[264,128]{1,0:T(8,128)(2,1)S(1)}, u32[]{:S(2)}, u32[]{:S(2)}) %collective-permute-start.11) | collective-permute-done | bytes 67616 | tf_op jit(solution)/shard_map/ppermute | solution.py:552
  103.4 4.6 %collective-permute-done.12.rest_6_ = bf16[264,128]{1,0:T(8,128)(2,1)S(1)} collective-permute-done((bf16[264,128]{1,0:T(8,128)(2,1)S(1)}, bf16[264,128]{1,0:T(8,128)(2,1)S(1)}, u32[]{:S(2)}, u32[]{:S(2)}) %collective-permute-start.12) | collective-permute-done | bytes 67616 | tf_op jit(solution)/shard_map/ppermute | solution.py:552
  108.0 0.5 collective-permute-done.13.rest_7_
  108.5 1.7 %merge.1 = bf16[128,32,128]{2,1,0:T(8,128)(2,1)} custom-call(s32[1]{0:T(128)} %bitcast.me_ref, bf16[16,264,128]{2,1,0:T(8,128)(2,1)S(1)} %all-to-all-done.1.x_ref, bf16[264,128]{1,0:T(8,128)(2,1)S(1)} %get-tuple-element.33.rest_0_, bf16[264,128]{1,0:T(8,128)(2,1)S(1)} %collective-permute-done.7.rest_1_, bf16[264,128]{1,0:T(8,128)(2,1)S(1)} %collective-permute-done.8.rest_2_, ...), custom_call_target="tpu_custom_call" | custom-call | tf_op jit(solution)/shard_map/merge/pallas_call | solution.py:529
  (16 shorter events, 0.2 us)
Async XLA Ops:
  0.0 1.9 %copy-start = (bf16[128,32,384]{2,1,0:T(8,128)(2,1)S(1)}, bf16[128,32,384]{2,1,0:T(8,128)(2,1)}, u32[]{:S(2)}) copy-start(bf16[128,32,384]{2,1,0:T(8,128)(2,1)} %x_ref.3) | copy-start | bytes 9437188
  1.9 0.7 copy-start.3
  3.7 1.3 %copy-start.2 = (bf16[16,520,128]{2,1,0:T(8,128)(2,1)}, bf16[16,520,128]{2,1,0:T(8,128)(2,1)S(1)}, u32[]{:S(2)}) copy-start(bf16[16,520,128]{2,1,0:T(8,128)(2,1)S(1)} %cross.1) | copy-start | bytes 6389764
  5.0 49.2 %all-to-all-start = ((bf16[16,520,128]{2,1,0:T(8,128)(2,1)}), bf16[16,520,128]{2,1,0:T(8,128)(2,1)S(1)}, u32[]{:S(2)}, u32[]{:S(2)}) async-start(bf16[16,520,128]{2,1,0:T(8,128)(2,1)} %copy-done.2), calls=%async_computation | async-start | bytes 4259840 | tf_op jit(solution)/shard_map/all_to_all | solution.py:547
  12.4 1.9 %copy-start.1 = (bf16[128,32,384]{2,1,0:T(8,128)(2,1)S(1)}, bf16[128,32,384]{2,1,0:T(8,128)(2,1)}, u32[]{:S(2)}) copy-start(bf16[128,32,384]{2,1,0:T(8,128)(2,1)} %x_ref.3) | copy-start | bytes 9437188
  17.1 3.9 %collective-permute-start = (bf16[1024,128]{1,0:T(8,128)(2,1)S(1)}, bf16[1024,128]{1,0:T(8,128)(2,1)S(1)}, u32[]{:S(2)}, u32[]{:S(2)}) collective-permute-start(bf16[1024,128]{1,0:T(8,128)(2,1)S(1)} %get-tuple-element.26), channel_id=1, source_target_pairs={{0,1},{1,0},{2,3},{3,2},{4,5},{5,4},{6,7},{7,6},{8,9},{9,8},{10,11... | collective-permute-start | bytes 786440 | tf_op jit(solution)/shard_map/ppermute | solution.py:552
  17.5 20.4 %collective-permute-start.1 = (bf16[1024,128]{1,0:T(8,128)(2,1)S(1)}, bf16[1024,128]{1,0:T(8,128)(2,1)S(1)}, u32[]{:S(2)}, u32[]{:S(2)}) collective-permute-start(bf16[1024,128]{1,0:T(8,128)(2,1)S(1)} %get-tuple-element.27), channel_id=1, source_target_pairs={{0,2},{1,3},{2,0},{3,1},{4,6},{5,7},{6,4},{7,5},{8,10},{9,11},{10,... | collective-permute-start | bytes 786440 | tf_op jit(solution)/shard_map/ppermute | solution.py:552
  19.2 38.4 %collective-permute-start.2 = (bf16[1024,128]{1,0:T(8,128)(2,1)}, bf16[1024,128]{1,0:T(8,128)(2,1)S(1)}, u32[]{:S(2)}, u32[]{:S(2)}) collective-permute-start(bf16[1024,128]{1,0:T(8,128)(2,1)} %get-tuple-element.28), channel_id=1, source_target_pairs={{0,3},{1,2},{2,1},{3,0},{4,7},{5,6},{6,5},{7,4},{8,11},{9,10},{10,... | collective-permute-start | bytes 786440 | tf_op jit(solution)/shard_map/ppermute | solution.py:552
  19.2 38.4 %collective-permute-start.3 = (bf16[1024,128]{1,0:T(8,128)(2,1)}, bf16[1024,128]{1,0:T(8,128)(2,1)S(1)}, u32[]{:S(2)}, u32[]{:S(2)}) collective-permute-start(bf16[1024,128]{1,0:T(8,128)(2,1)} %get-tuple-element.29), channel_id=1, source_target_pairs={{0,4},{1,5},{2,6},{3,7},{4,0},{5,1},{6,2},{7,3},{8,12},{9,13},{10,... | collective-permute-start | bytes 786440 | tf_op jit(solution)/shard_map/ppermute | solution.py:552
  20.9 39.8 %collective-permute-start.4 = (bf16[1024,128]{1,0:T(8,128)(2,1)}, bf16[1024,128]{1,0:T(8,128)(2,1)}, u32[]{:S(2)}, u32[]{:S(2)}) collective-permute-start(bf16[1024,128]{1,0:T(8,128)(2,1)} %get-tuple-element.30), channel_id=1, source_target_pairs={{0,5},{1,4},{2,7},{3,6},{4,1},{5,0},{6,3},{7,2},{8,13},{9,12},{10,... | collective-permute-start | bytes 786440 | tf_op jit(solution)/shard_map/ppermute | solution.py:552
  21.0 47.3 %collective-permute-start.5 = (bf16[1024,128]{1,0:T(8,128)(2,1)}, bf16[1024,128]{1,0:T(8,128)(2,1)}, u32[]{:S(2)}, u32[]{:S(2)}) collective-permute-start(bf16[1024,128]{1,0:T(8,128)(2,1)} %get-tuple-element.31), channel_id=1, source_target_pairs={{0,6},{1,7},{2,4},{3,5},{4,2},{5,3},{6,0},{7,1},{8,14},{9,15},{10,... | collective-permute-start | bytes 786440 | tf_op jit(solution)/shard_map/ppermute | solution.py:552
  37.8 35.1 %collective-permute-start.6 = (bf16[1024,128]{1,0:T(8,128)(2,1)}, bf16[1024,128]{1,0:T(8,128)(2,1)}, u32[]{:S(2)}, u32[]{:S(2)}) collective-permute-start(bf16[1024,128]{1,0:T(8,128)(2,1)} %get-tuple-element.32), channel_id=1, source_target_pairs={{0,7},{1,6},{2,5},{3,4},{4,3},{5,2},{6,1},{7,0},{8,15},{9,14},{10,... | collective-permute-start | bytes 786440 | tf_op jit(solution)/shard_map/ppermute | solution.py:552
  77.7 30.8 %all-to-all-start.1 = ((bf16[16,264,128]{2,1,0:T(8,128)(2,1)}), bf16[16,264,128]{2,1,0:T(8,128)(2,1)S(1)}, u32[]{:S(2)}, u32[]{:S(2)}) async-start(bf16[16,264,128]{2,1,0:T(8,128)(2,1)} %own.1), calls=%async_computation.1 | async-start | bytes 2162688 | tf_op jit(solution)/shard_map/all_to_all | solution.py:547
  85.2 4.0 %collective-permute-start.7 = (bf16[264,128]{1,0:T(8,128)(2,1)S(1)}, bf16[264,128]{1,0:T(8,128)(2,1)S(1)}, u32[]{:S(2)}, u32[]{:S(2)}) collective-permute-start(bf16[264,128]{1,0:T(8,128)(2,1)S(1)} %get-tuple-element.34), channel_id=1, source_target_pairs={{0,1},{1,0},{2,3},{3,2},{4,5},{5,4},{6,7},{7,6},{8,9},{9,8},{10,11... | collective-permute-start | bytes 202760 | tf_op jit(solution)/shard_map/ppermute | solution.py:552
  85.7 7.8 %collective-permute-start.8 = (bf16[264,128]{1,0:T(8,128)(2,1)S(1)}, bf16[264,128]{1,0:T(8,128)(2,1)S(1)}, u32[]{:S(2)}, u32[]{:S(2)}) collective-permute-start(bf16[264,128]{1,0:T(8,128)(2,1)S(1)} %get-tuple-element.35), channel_id=1, source_target_pairs={{0,2},{1,3},{2,0},{3,1},{4,6},{5,7},{6,4},{7,5},{8,10},{9,11},{10,... | collective-permute-start | bytes 202760 | tf_op jit(solution)/shard_map/ppermute | solution.py:552
  87.4 7.5 %collective-permute-start.9 = (bf16[264,128]{1,0:T(8,128)(2,1)S(1)}, bf16[264,128]{1,0:T(8,128)(2,1)S(1)}, u32[]{:S(2)}, u32[]{:S(2)}) collective-permute-start(bf16[264,128]{1,0:T(8,128)(2,1)S(1)} %get-tuple-element.36), channel_id=1, source_target_pairs={{0,3},{1,2},{2,1},{3,0},{4,7},{5,6},{6,5},{7,4},{8,11},{9,10},{10,... | collective-permute-start | bytes 202760 | tf_op jit(solution)/shard_map/ppermute | solution.py:552
  87.4 14.6 %collective-permute-start.10 = (bf16[264,128]{1,0:T(8,128)(2,1)S(1)}, bf16[264,128]{1,0:T(8,128)(2,1)S(1)}, u32[]{:S(2)}, u32[]{:S(2)}) collective-permute-start(bf16[264,128]{1,0:T(8,128)(2,1)S(1)} %get-tuple-element.37), channel_id=1, source_target_pairs={{0,4},{1,5},{2,6},{3,7},{4,0},{5,1},{6,2},{7,3},{8,12},{9,13},{10,... | collective-permute-start | bytes 202760 | tf_op jit(solution)/shard_map/ppermute | solution.py:552
  89.1 14.3 %collective-permute-start.11 = (bf16[264,128]{1,0:T(8,128)(2,1)S(1)}, bf16[264,128]{1,0:T(8,128)(2,1)S(1)}, u32[]{:S(2)}, u32[]{:S(2)}) collective-permute-start(bf16[264,128]{1,0:T(8,128)(2,1)S(1)} %get-tuple-element.38), channel_id=1, source_target_pairs={{0,5},{1,4},{2,7},{3,6},{4,1},{5,0},{6,3},{7,2},{8,13},{9,12},{10,... | collective-permute-start | bytes 202760 | tf_op jit(solution)/shard_map/ppermute | solution.py:552
  89.2 18.8 %collective-permute-start.12 = (bf16[264,128]{1,0:T(8,128)(2,1)S(1)}, bf16[264,128]{1,0:T(8,128)(2,1)S(1)}, u32[]{:S(2)}, u32[]{:S(2)}) collective-permute-start(bf16[264,128]{1,0:T(8,128)(2,1)S(1)} %get-tuple-element.39), channel_id=1, source_target_pairs={{0,6},{1,7},{2,4},{3,5},{4,2},{5,3},{6,0},{7,1},{8,14},{9,15},{10,... | collective-permute-start | bytes 202760 | tf_op jit(solution)/shard_map/ppermute | solution.py:552
  93.5 14.9 %collective-permute-start.13 = (bf16[264,128]{1,0:T(8,128)(2,1)S(1)}, bf16[264,128]{1,0:T(8,128)(2,1)S(1)}, u32[]{:S(2)}, u32[]{:S(2)}) collective-permute-start(bf16[264,128]{1,0:T(8,128)(2,1)S(1)} %get-tuple-element.40), channel_id=1, source_target_pairs={{0,7},{1,6},{2,5},{3,4},{4,3},{5,2},{6,1},{7,0},{8,15},{9,14},{10,... | collective-permute-start | bytes 202760 | tf_op jit(solution)/shard_map/ppermute | solution.py:552

commit v7 on v6

--- a/solution.py
+++ b/solution.py
@@ -154,28 +154,53 @@
     )(labels, x)
 
 
-def cross_kernel(me_ref, x_ref, lab_ref, o_ref):
-    tok, heads, width = x_ref.shape
+def cross_kernel(me_ref, x_ref, lab_ref, o_ref, buf_ref, labs_ref, out_ref, in_sems, out_sems):
+    steps, count, heads, _ = buf_ref.shape
     nseq = o_ref.shape[0]
     half = nseq // 2
+    tok = steps * count
     lane = pl.multiple_of(jnp.where(me_ref[0] >= half, 0, 128), 128)
+    loads = [
+        pltpu.make_async_copy(
+            x_ref.at[pl.ds(step * count, count), :, pl.ds(lane, 256)],
+            buf_ref.at[step],
+            in_sems.at[step],
+        )
+        for step in range(steps)
+    ]
+    loads.append(pltpu.make_async_copy(lab_ref, labs_ref, in_sems.at[steps]))
+    for load in loads:
+        load.start()
+    stores = []
+
+    def store(row, rows):
+        piece = (slice(None), pl.ds(row, rows), slice(None))
+        stores.append(
+            pltpu.make_async_copy(out_ref.at[piece], o_ref.at[piece], out_sems.at[len(stores)])
+        )
+        stores[-1].start()
+
+    for step in range(steps):
+        loads[step].wait()
+        turned = jnp.swapaxes(buf_ref[step].astype(jnp.float32), 0, 1).astype(jnp.bfloat16)
+        for part in range(4):
+            row = part * tok + step * count
+            lanes = slice(part // 2 * 128, part // 2 * 128 + 128)
+            for dst in range(nseq):
+                out_ref[dst, row : row + count, :] = turned[2 * dst + part % 2, :, lanes]
+            store(row, count)
+    loads[steps].wait()
     pad = jnp.zeros((4, 128), jnp.float32)
     for dst in range(nseq):
         other = dst ^ half
-        labels = [lab_ref[2 * dst : 2 * dst + 2, :], lab_ref[2 * other : 2 * other + 2, :]]
+        labels = [labs_ref[2 * dst : 2 * dst + 2, :], labs_ref[2 * other : 2 * other + 2, :]]
         labels = [piece.astype(jnp.float32) for piece in labels]
-        o_ref[dst, 4 * tok : 4 * tok + 8, :] = jnp.concatenate(labels + [pad], axis=0).astype(
+        out_ref[dst, 4 * tok : 4 * tok + 8, :] = jnp.concatenate(labels + [pad], axis=0).astype(
             jnp.bfloat16
         )
-    for first in range(0, tok, 32):
-        piece = x_ref[first : first + 32, :, pl.ds(lane, 256)].astype(jnp.float32)
-        turned = jnp.swapaxes(piece, 0, 1).astype(jnp.bfloat16)
-        for head in range(heads):
-            for part in range(2):
-                row = (2 * part + head % 2) * tok + first
-                o_ref[head // 2, row : row + 32, :] = turned[
-                    head, :, part * 128 : (part + 1) * 128
-                ]
+    store(4 * tok, 8)
+    for copy in stores:
+        copy.wait()
 
 
 def near_kernel(me_ref, x_ref, *rest):
@@ -206,13 +231,21 @@
     tok, heads, width = qkv.shape
     whole = pl.BlockSpec(memory_space=pltpu.VMEM)
     scalar = pl.BlockSpec(memory_space=pltpu.SMEM)
+    hbm = pl.BlockSpec(memory_space=pl.ANY)
     params = pltpu.CompilerParams(vmem_limit_bytes=12 << 20)
     cross = pl.pallas_call(
         cross_kernel,
         out_shape=jax.ShapeDtypeStruct((nseq, 4 * tok + 8, 128), jnp.bfloat16),
-        in_specs=[scalar, whole, whole],
-        out_specs=whole,
-        compiler_params=params,
+        in_specs=[scalar, hbm, hbm],
+        out_specs=hbm,
+        scratch_shapes=[
+            pltpu.VMEM((4, tok // 4, heads, 256), jnp.bfloat16),
+            pltpu.VMEM(labels.shape, labels.dtype),
+            pltpu.VMEM((nseq, 4 * tok + 8, 128), jnp.bfloat16),
+            pltpu.SemaphoreType.DMA((5,)),
+            pltpu.SemaphoreType.DMA((17,)),
+        ],
+        compiler_params=pltpu.CompilerParams(vmem_limit_bytes=58 << 20),
         name="cross",
     )(me, qkv, labels)
     near = pl.pallas_call(
@@ -283,7 +316,7 @@
     return num / total, rows
 
 
-def far_kernel(lab_ref, x_ref, o_ref, stat_ref, v_ref, *, tok, rate):
+def far_kernel(me_ref, lab_ref, x_ref, o_ref, stat_ref, half_ref, v_ref, *, tok, rate):
     nseq = x_ref.shape[0]
     half = nseq // 2
     span = half * tok
@@ -310,9 +343,14 @@
         o_ref[j, block * QB : (block + 1) * QB, :] = out
 
     run_tasks([(j, block) for block in range(span // QB) for j in range(2)], score, weigh, blend)
-
-
-def far_of(labels, x, tok, rate):
+    first = jnp.where(me_ref[0] >= half, half, 0)
+    for kind in range(4):
+        half_ref[kind] = x_ref[pl.ds(first, half), kind * tok : (kind + 1) * tok, :].reshape(
+            span, 128
+        )
+
+
+def far_of(me, labels, x, tok, rate):
     half = x.shape[0] // 2
     whole = pl.BlockSpec(memory_space=pltpu.VMEM)
     return pl.pallas_call(
@@ -320,39 +358,57 @@
         out_shape=[
             jax.ShapeDtypeStruct((2, half * tok, 128), jnp.float32),
             jax.ShapeDtypeStruct((2, half, 128), jnp.float32),
+            jax.ShapeDtypeStruct((4, half * tok, 128), jnp.bfloat16),
         ],
-        in_specs=[whole, whole],
-        out_specs=[whole, whole],
+        in_specs=[pl.BlockSpec(memory_space=pltpu.SMEM), whole, whole],
+        out_specs=[whole, whole, whole],
         scratch_shapes=[pltpu.VMEM((2, half * tok, 256), jnp.bfloat16)],
         compiler_params=pltpu.CompilerParams(vmem_limit_bytes=16 << 20),
         name="far",
-    )(labels, x)
-
-
-def own_kernel(me_ref, lab_ref, x_ref, far_ref, far_stat_ref, *rest, tok, rate):
-    half = x_ref.shape[0] // 2
+    )(me, labels, x)
+
+
+def own_kernel(me_ref, lab_ref, far_ref, far_stat_ref, half_ref, *rest, tok, rate):
+    half = far_stat_ref.shape[1]
     near_refs, o_ref = rest[:half], rest[half]
-    q_ref, k_ref, v_ref = rest[half + 1 :]
+    q_ref, v_ref, out_ref, sems = rest[half + 1 :]
     span = half * tok
     per = QB // tok
     me = me_ref[0]
     upper = me >= half
     up = upper.astype(jnp.int32)
+    stores = []
+
+    def store(first, count, row, rows):
+        piece = (pl.ds(first, count), pl.ds(row, rows), slice(None))
+        stores.append(
+            pltpu.make_async_copy(out_ref.at[piece], o_ref.at[piece], sems.at[len(stores)])
+        )
+        stores[-1].start()
+
+    for j in range(2):
+        out_ref[pl.ds((1 - up) * half, half), j * tok : (j + 1) * tok, :] = (
+            far_ref[j].astype(jnp.bfloat16).reshape(half, tok, 128)
+        )
+    for i in range(half):
+        stats = three_parts([far_stat_ref[j, i : i + 1, :] for j in range(2)])
+        out_ref[(1 - up) * half + i, 2 * tok : 2 * tok + 8, :] = stats
+        out_ref[up * half + i, 2 * tok : 2 * tok + 8, :] = jnp.zeros((8, 128), jnp.bfloat16)
+    store((1 - up) * half, half, 0, 2 * tok + 8)
+    store(up * half, half, 2 * tok, 8)
     places = [pl.ds(pl.multiple_of(((me ^ k) % half) * tok, tok), tok) for k in range(half)]
 
     @pl.when(upper)
     def _():
         for j in range(2):
-            q_ref[j] = x_ref[half:, j * tok : (j + 1) * tok, :].reshape(span, 128)
-            k_ref[j] = x_ref[half:, (2 + j) * tok : (3 + j) * tok, :].reshape(span, 128)
+            q_ref[j] = half_ref[j]
             for place, near_ref in zip(places, near_refs):
                 v_ref[j, place, :128] = near_ref[j * tok : (j + 1) * tok, :]
 
     @pl.when(jnp.logical_not(upper))
     def _():
         for j in range(2):
-            k_ref[j] = x_ref[:half, j * tok : (j + 1) * tok, :].reshape(span, 128)
-            v_ref[j, :, :128] = x_ref[:half, (2 + j) * tok : (3 + j) * tok, :].reshape(span, 128)
+            v_ref[j, :, :128] = half_ref[2 + j]
             for place, near_ref in zip(places, near_refs):
                 q_ref[j, place, :] = near_ref[j * tok : (j + 1) * tok, :]
 
@@ -363,7 +419,8 @@
         return [lab_ref[j, pl.ds(up * half + first + i, 1), :] for i in range(count)]
 
     def score(j, block):
-        return dot_t(q_ref[j, block * QB : (block + 1) * QB, :], k_ref[j, : (block + 1) * QB, :])
+        k = half_ref[2 * up + j, : (block + 1) * QB, :]
+        return dot_t(q_ref[j, block * QB : (block + 1) * QB, :], k)
 
     def weigh(j, block, s):
         lab_q = columns(lab_of(j, block * per, per))
@@ -382,42 +439,39 @@
         weight = jnp.where(upper, 1.0 / (1.0 + jnp.exp2(gap)), 0.0)
         far = far_ref[j, block * QB : (block + 1) * QB, :]
         out = near + (far - near) * weight
-        o_ref[pl.ds(up * half + block * per, per), j * tok : (j + 1) * tok, :] = out.astype(
+        out_ref[pl.ds(up * half + block * per, per), j * tok : (j + 1) * tok, :] = out.astype(
             jnp.bfloat16
         ).reshape(per, tok, 128)
-        o_ref[pl.ds((1 - up) * half + block * per, per), j * tok : (j + 1) * tok, :] = far.astype(
-            jnp.bfloat16
-        ).reshape(per, tok, 128)
+        store(up * half + block * per, per, j * tok, tok)
 
     blocks = span // QB
     tasks = [
         (j, block if j == 0 else blocks - 1 - block) for block in range(blocks) for j in range(2)
     ]
     run_tasks(tasks, score, weigh, blend)
-    for i in range(half):
-        stats = three_parts([far_stat_ref[j, i : i + 1, :] for j in range(2)])
-        o_ref[(1 - up) * half + i, 2 * tok : 2 * tok + 8, :] = stats
-        o_ref[up * half + i, 2 * tok : 2 * tok + 8, :] = jnp.zeros((8, 128), jnp.bfloat16)
-
-
-def own(me, labels, x, far, near, tok, rate):
-    nseq = x.shape[0]
-    half = nseq // 2
+    for copy in stores:
+        copy.wait()
+
+
+def own(me, labels, far, near, tok, rate):
+    half = len(near)
+    nseq = 2 * half
     span = half * tok
     whole = pl.BlockSpec(memory_space=pltpu.VMEM)
     return pl.pallas_call(
         functools.partial(own_kernel, tok=tok, rate=rate),
         out_shape=jax.ShapeDtypeStruct((nseq, 2 * tok + 8, 128), jnp.bfloat16),
         in_specs=[pl.BlockSpec(memory_space=pltpu.SMEM)] + [whole] * (4 + half),
-        out_specs=whole,
+        out_specs=pl.BlockSpec(memory_space=pl.ANY),
         scratch_shapes=[
             pltpu.VMEM((2, span, 128), jnp.bfloat16),
-            pltpu.VMEM((2, span, 128), jnp.bfloat16),
             pltpu.VMEM((2, span, 256), jnp.bfloat16),
+            pltpu.VMEM((nseq, 2 * tok + 8, 128), jnp.bfloat16),
+            pltpu.SemaphoreType.DMA((2 + 2 * span // QB,)),
         ],
         compiler_params=pltpu.CompilerParams(vmem_limit_bytes=16 << 20),
         name="own",
-    )(me, labels, x, *far, *near)
+    )(me, labels, *far, *near)
 
 
 def partner_kernel(me_ref, lab_ref, *rest, tok, rate):
@@ -495,7 +549,8 @@
 def merge_kernel(me_ref, x_ref, *rest, tok):
     nseq = x_ref.shape[0]
     half = nseq // 2
-    near_refs, o_ref, head_ref = rest[:half], rest[half], rest[half + 1]
+    near_refs, o_ref = rest[:half], rest[half]
+    head_ref, out_ref, sems = rest[half + 1 :]
     me = me_ref[0]
     upper = me >= half
     up = upper.astype(jnp.int32)
@@ -518,9 +573,18 @@
             far = x_ref[down * half + place, j * tok : (j + 1) * tok, :].astype(jnp.float32)
             near = near_ref[j * tok : (j + 1) * tok, :].astype(jnp.float32)
             head_ref[down * (heads // 2) + 2 * place + j] = near + (far - near) * weight
+    stores = []
     for first in range(0, tok, 32):
         piece = head_ref[:, first : first + 32, :]
-        o_ref[first : first + 32] = jnp.swapaxes(piece, 0, 1).astype(jnp.bfloat16)
+        out_ref[first : first + 32] = jnp.swapaxes(piece, 0, 1).astype(jnp.bfloat16)
+        stores.append(
+            pltpu.make_async_copy(
+                out_ref.at[pl.ds(first, 32)], o_ref.at[pl.ds(first, 32)], sems.at[len(stores)]
+            )
+        )
+        stores[-1].start()
+    for copy in stores:
+        copy.wait()
 
 
 def merge(me, x, near, tok):
@@ -530,8 +594,12 @@
         functools.partial(merge_kernel, tok=tok),
         out_shape=jax.ShapeDtypeStruct((tok, 2 * nseq, 128), jnp.bfloat16),
         in_specs=[pl.BlockSpec(memory_space=pltpu.SMEM)] + [whole] * (1 + nseq // 2),
-        out_specs=whole,
-        scratch_shapes=[pltpu.VMEM((2 * nseq, tok, 128), jnp.float32)],
+        out_specs=pl.BlockSpec(memory_space=pl.ANY),
+        scratch_shapes=[
+            pltpu.VMEM((2 * nseq, tok, 128), jnp.float32),
+            pltpu.VMEM((tok, 2 * nseq, 128), jnp.bfloat16),
+            pltpu.SemaphoreType.DMA((tok // 32,)),
+        ],
         compiler_params=pltpu.CompilerParams(vmem_limit_bytes=12 << 20),
         name="merge",
     )(me, x, *near)
@@ -556,8 +624,8 @@
     near = swap(near)
     cross = exchange(cross)
     labels = jnp.transpose(cross[:, 4 * tok : 4 * tok + 4, :].astype(jnp.int32), (1, 0, 2))
-    far = far_of(labels, cross, tok, rate)
-    back = exchange(own(me, labels, cross, far, near, tok, rate))
+    far = far_of(me, labels, cross, tok, rate)
+    back = exchange(own(me, labels, far, near, tok, rate))
     near_back = swap(partner(me, labels, near, tok, rate))
     return merge(me, back, near_back, tok)
 

time: 111 us -> 107 us (0.964)
  local copies, waits for them, and re-layouts: 5.83 us -> 0.77 us
    unnamed x8 -> x2, local copies, waits for them, and re-layouts: 5.82 us -> 0.01 us
    pallas_call x1, Pallas kernels: 1.07 us -> 2.97 us  [spread(): pl.pallas_call(cross_kernel, out_shape=jax.ShapeDtypeStruct((nseq, 4 * to...]
    pallas_call x1, Pallas kernels: 3.25 us -> 4.93 us  [far_of(): pl.pallas_call(functools.partial(far_kernel, tok=tok, rate=rate), out_sha...]
    pallas_call x1, Pallas kernels: 4.79 us -> 3.44 us  [own(): pl.pallas_call(functools.partial(own_kernel, tok=tok, rate=rate), out_sha...]
  transfers between devices with their start and end apart: 16 -> 16, of which waited for: 11 -> 11; matrix products, arithmetic and copies ran while one was open for 0% -> 1% of each run, Pallas kernels for 9% -> 10%
where the time goes in v7:
time: 107 us
  waiting for transfers between devices  63.2 us (59%)
  starting transfers between devices  24.7 us (23%)
  Pallas kernels  18.1 us (17%)
    ppermute x14, waiting for transfers between devices, swap(): moved[k] = lax.ppermute(blocks[k], 'seq', [(i, i ^ k) for i in range(nseq)])  46.7 us
    all_to_all x2, waiting for transfers between devices, exchange(): return lax.all_to_all(x, 'seq', split_axis=0, concat_axis=0, tiled=True)  16.5 us
    ppermute x14, starting transfers between devices, swap(): moved[k] = lax.ppermute(blocks[k], 'seq', [(i, i ^ k) for i in range(nseq)])  13 us
    all_to_all x2, starting transfers between devices, exchange(): return lax.all_to_all(x, 'seq', split_axis=0, concat_axis=0, tiled=True)  11.7 us
    pallas_call x1, Pallas kernels, far_of(): pl.pallas_call(functools.partial(far_kernel, tok=tok, rate=rate), out_sha...  4.93 us
    pallas_call x1, Pallas kernels, own(): pl.pallas_call(functools.partial(own_kernel, tok=tok, rate=rate), out_sha...  3.44 us
    pallas_call x1, Pallas kernels, spread(): pl.pallas_call(cross_kernel, out_shape=jax.ShapeDtypeStruct((nseq, 4 * to...  2.97 us
    pallas_call x1, Pallas kernels, spread(): pl.pallas_call(near_kernel, out_shape=[jax.ShapeDtypeStruct((8 * tok, 128...  2.83 us
  transfers between devices with their start and end apart: 16, of which 11 were waited for; matrix products, arithmetic and copies ran while one was open for 1% of the time, Pallas kernels for 10%

profile of v7, /device:TPU:0, one launch (start us, length us, event | category | flops | bytes accessed | tf_op | source)
XLA Modules:
  0.0 106.9 jit_solution(7159849261996170698)
XLA Ops:
  0.0 3.0 %cross.1 = bf16[16,520,128]{2,1,0:T(8,128)(2,1)} custom-call(s32[1]{0:T(128)} %bitcast.me_ref, bf16[128,32,384]{2,1,0:T(8,128)(2,1)} %x_ref.3, s32[32,128]{1,0:T(8,128)} %bitcast.4), custom_call_target="tpu_custom_call" | custom-call | tf_op jit(solution)/shard_map/cross/pallas_call | solution.py:236
  3.0 0.0 copy-start
  3.0 7.7 %all-to-all-start = ((bf16[16,520,128]{2,1,0:T(8,128)(2,1)}), bf16[16,520,128]{2,1,0:T(8,128)(2,1)}, u32[]{:S(2)}, u32[]{:S(2)}) async-start(bf16[16,520,128]{2,1,0:T(8,128)(2,1)} %cross.1), calls=%async_computation | async-start | bytes 4259840 | tf_op jit(solution)/shard_map/all_to_all | solution.py:615
  10.7 2.8 %near.1 = (bf16[1024,128]{1,0:T(8,128)(2,1)S(1)}, bf16[1024,128]{1,0:T(8,128)(2,1)S(1)}, bf16[1024,128]{1,0:T(8,128)(2,1)S(1)}, bf16[1024,128]{1,0:T(8,128)(2,1)...) custom-call(s32[1]{0:T(128)} %bitcast.me_ref, ...), custom_call_target="tpu_custom_call" | custom-call | tf_op jit(solution)/shard_map/near/pallas_call | solution.py:251
  13.5 0.4 collective-permute-start
  13.9 1.7 %collective-permute-start.1 = (bf16[1024,128]{1,0:T(8,128)(2,1)S(1)}, bf16[1024,128]{1,0:T(8,128)(2,1)S(1)}, u32[]{:S(2)}, u32[]{:S(2)}) collective-permute-start(bf16[1024,128]{1,0:T(8,128)(2,1)S(1)} %get-tuple-element.29), channel_id=1, source_target_pairs={{0,2},{1,3},{2,0},{3,1},{4,6},{5,7},{6,4},{7,5},{8,10},{9,11},{10,... | collective-permute-start | bytes 786440 | tf_op jit(solution)/shard_map/ppermute | solution.py:620
  15.6 1.7 %collective-permute-start.3 = (bf16[1024,128]{1,0:T(8,128)(2,1)}, bf16[1024,128]{1,0:T(8,128)(2,1)S(1)}, u32[]{:S(2)}, u32[]{:S(2)}) collective-permute-start(bf16[1024,128]{1,0:T(8,128)(2,1)} %get-tuple-element.31), channel_id=1, source_target_pairs={{0,4},{1,5},{2,6},{3,7},{4,0},{5,1},{6,2},{7,3},{8,12},{9,13},{10,... | collective-permute-start | bytes 786440 | tf_op jit(solution)/shard_map/ppermute | solution.py:620
  17.2 0.1 collective-permute-start.4
  17.4 0.0 collective-permute-done.rest_1_
  17.4 2.6 %collective-permute-start.5 = (bf16[1024,128]{1,0:T(8,128)(2,1)}, bf16[1024,128]{1,0:T(8,128)(2,1)S(1)}, u32[]{:S(2)}, u32[]{:S(2)}) collective-permute-start(bf16[1024,128]{1,0:T(8,128)(2,1)} %get-tuple-element.33), channel_id=1, source_target_pairs={{0,6},{1,7},{2,4},{3,5},{4,2},{5,3},{6,0},{7,1},{8,14},{9,15},{10,... | collective-permute-start | bytes 786440 | tf_op jit(solution)/shard_map/ppermute | solution.py:620
  19.9 16.1 %collective-permute-done.1.rest_2_ = bf16[1024,128]{1,0:T(8,128)(2,1)S(1)} collective-permute-done((bf16[1024,128]{1,0:T(8,128)(2,1)S(1)}, bf16[1024,128]{1,0:T(8,128)(2,1)S(1)}, u32[]{:S(2)}, u32[]{:S(2)}) %collective-permute-start.1) | collective-permute-done | bytes 262176 | tf_op jit(solution)/shard_map/ppermute | solution.py:620
  36.1 16.5 %all-to-all-done.x_ref = bf16[16,520,128]{2,1,0:T(8,128)(2,1)} async-done(((bf16[16,520,128]{2,1,0:T(8,128)(2,1)}), bf16[16,520,128]{2,1,0:T(8,128)(2,1)}, u32[]{:S(2)}, u32[]{:S(2)}) %all-to-all-start) | async-done | bytes 2129952 | tf_op jit(solution)/shard_map/all_to_all | solution.py:615
  52.6 0.8 slice.4
  53.4 4.9 %far.1 = (f32[2,1024,128]{2,1,0:T(8,128)S(1)}, f32[2,8,128]{2,1,0:T(8,128)S(1)}, bf16[4,1024,128]{2,1,0:T(8,128)(2,1)S(1)}) custom-call(s32[1]{0:T(128)} %bitcast.me_ref, s32[4,16,128]{2,1,0:T(8,128)S(1)} %convert_bitcast_fusion.lab_ref, bf16[16,520,128]{2,1,0:T(8,128)(2,1)} %all-to-all-done.x_ref), custom_call_target="tpu_custom_call" | custom-call | tf_op jit(solution)/shard_map/far/pallas_call | solution.py:356
  58.3 0.5 collective-permute-done.4.rest_5_
  58.8 7.6 %collective-permute-done.5.rest_6_ = bf16[1024,128]{1,0:T(8,128)(2,1)S(1)} collective-permute-done((bf16[1024,128]{1,0:T(8,128)(2,1)}, bf16[1024,128]{1,0:T(8,128)(2,1)S(1)}, u32[]{:S(2)}, u32[]{:S(2)}) %collective-permute-start.5) | collective-permute-done | bytes 262176 | tf_op jit(solution)/shard_map/ppermute | solution.py:620
  66.4 4.7 %collective-permute-done.6.rest_7_ = bf16[1024,128]{1,0:T(8,128)(2,1)S(1)} collective-permute-done((bf16[1024,128]{1,0:T(8,128)(2,1)}, bf16[1024,128]{1,0:T(8,128)(2,1)S(1)}, u32[]{:S(2)}, u32[]{:S(2)}) %collective-permute-start.6) | collective-permute-done | bytes 262176 | tf_op jit(solution)/shard_map/ppermute | solution.py:620
  71.1 3.4 %own.1 = bf16[16,264,128]{2,1,0:T(8,128)(2,1)} custom-call(s32[1]{0:T(128)} %bitcast.me_ref, s32[4,16,128]{2,1,0:T(8,128)S(1)} %convert_bitcast_fusion.lab_ref, f32[2,1024,128]{2,1,0:T(8,128)S(1)} %get-tuple-element.24.far_ref, f32[2,8,128]{2,1,0:T(8,128)S(1)} %get-tuple-element.25.far_stat_ref, bf16[4,1024,128]{2,1,0:T(8,128)(2,1)S(1)} %get-tuple-element.26.half_ref, ...), custom_call_target="tpu_custom_call" | custom-call | tf_op jit(solution)/shard_map/own/pallas_call | solution.py:461
  74.5 4.0 %all-to-all-start.1 = ((bf16[16,264,128]{2,1,0:T(8,128)(2,1)}), bf16[16,264,128]{2,1,0:T(8,128)(2,1)S(1)}, u32[]{:S(2)}, u32[]{:S(2)}) async-start(bf16[16,264,128]{2,1,0:T(8,128)(2,1)} %own.1), calls=%async_computation.1 | async-start | bytes 2162688 | tf_op jit(solution)/shard_map/all_to_all | solution.py:615
  78.5 2.4 %partner.1 = (bf16[264,128]{1,0:T(8,128)(2,1)S(1)}, bf16[264,128]{1,0:T(8,128)(2,1)S(1)}, bf16[264,128]{1,0:T(8,128)(2,1)S(1)}, bf16[264,128]{1,0:T(8,128)(2,1)S...) custom-call(s32[1]{0:T(128)} %bitcast.me_ref, ...), custom_call_target="tpu_custom_call" | custom-call | tf_op jit(solution)/shard_map/partner/pallas_call | solution.py:532
  80.9 0.5 collective-permute-start.7
  81.4 1.7 %collective-permute-start.8 = (bf16[264,128]{1,0:T(8,128)(2,1)S(1)}, bf16[264,128]{1,0:T(8,128)(2,1)S(1)}, u32[]{:S(2)}, u32[]{:S(2)}) collective-permute-start(bf16[264,128]{1,0:T(8,128)(2,1)S(1)} %get-tuple-element.37), channel_id=1, source_target_pairs={{0,2},{1,3},{2,0},{3,1},{4,6},{5,7},{6,4},{7,5},{8,10},{9,11},{10,... | collective-permute-start | bytes 202760 | tf_op jit(solution)/shard_map/ppermute | solution.py:620
  83.1 1.7 %collective-permute-start.10 = (bf16[264,128]{1,0:T(8,128)(2,1)S(1)}, bf16[264,128]{1,0:T(8,128)(2,1)S(1)}, u32[]{:S(2)}, u32[]{:S(2)}) collective-permute-start(bf16[264,128]{1,0:T(8,128)(2,1)S(1)} %get-tuple-element.39), channel_id=1, source_target_pairs={{0,4},{1,5},{2,6},{3,7},{4,0},{5,1},{6,2},{7,3},{8,12},{9,13},{10,... | collective-permute-start | bytes 202760 | tf_op jit(solution)/shard_map/ppermute | solution.py:620
  84.8 0.1 collective-permute-start.11
  84.9 2.6 %collective-permute-start.12 = (bf16[264,128]{1,0:T(8,128)(2,1)S(1)}, bf16[264,128]{1,0:T(8,128)(2,1)S(1)}, u32[]{:S(2)}, u32[]{:S(2)}) collective-permute-start(bf16[264,128]{1,0:T(8,128)(2,1)S(1)} %get-tuple-element.41), channel_id=1, source_target_pairs={{0,6},{1,7},{2,4},{3,5},{4,2},{5,3},{6,0},{7,1},{8,14},{9,15},{10,... | collective-permute-start | bytes 202760 | tf_op jit(solution)/shard_map/ppermute | solution.py:620
  87.5 2.9 %collective-permute-done.8.rest_2_ = bf16[264,128]{1,0:T(8,128)(2,1)S(1)} collective-permute-done((bf16[264,128]{1,0:T(8,128)(2,1)S(1)}, bf16[264,128]{1,0:T(8,128)(2,1)S(1)}, u32[]{:S(2)}, u32[]{:S(2)}) %collective-permute-start.8) | collective-permute-done | bytes 67616 | tf_op jit(solution)/shard_map/ppermute | solution.py:620
  90.4 0.7 collective-permute-done.9.rest_3_
  91.0 7.8 %collective-permute-done.10.rest_4_ = bf16[264,128]{1,0:T(8,128)(2,1)S(1)} collective-permute-done((bf16[264,128]{1,0:T(8,128)(2,1)S(1)}, bf16[264,128]{1,0:T(8,128)(2,1)S(1)}, u32[]{:S(2)}, u32[]{:S(2)}) %collective-permute-start.10) | collective-permute-done | bytes 67616 | tf_op jit(solution)/shard_map/ppermute | solution.py:620
  98.8 1.4 %collective-permute-done.11.rest_5_ = bf16[264,128]{1,0:T(8,128)(2,1)S(1)} collective-permute-done((bf16[264,128]{1,0:T(8,128)(2,1)S(1)}, bf16[264,128]{1,0:T(8,128)(2,1)S(1)}, u32[]{:S(2)}, u32[]{:S(2)}) %collective-permute-start.11) | collective-permute-done | bytes 67616 | tf_op jit(solution)/shard_map/ppermute | solution.py:620
  100.3 4.5 %collective-permute-done.12.rest_6_ = bf16[264,128]{1,0:T(8,128)(2,1)S(1)} collective-permute-done((bf16[264,128]{1,0:T(8,128)(2,1)S(1)}, bf16[264,128]{1,0:T(8,128)(2,1)S(1)}, u32[]{:S(2)}, u32[]{:S(2)}) %collective-permute-start.12) | collective-permute-done | bytes 67616 | tf_op jit(solution)/shard_map/ppermute | solution.py:620
  104.8 0.5 collective-permute-done.13.rest_7_
  105.3 1.5 %merge.1 = bf16[128,32,128]{2,1,0:T(8,128)(2,1)} custom-call(s32[1]{0:T(128)} %bitcast.me_ref, bf16[16,264,128]{2,1,0:T(8,128)(2,1)S(1)} %all-to-all-done.1.x_ref, bf16[264,128]{1,0:T(8,128)(2,1)S(1)} %get-tuple-element.35.rest_0_, bf16[264,128]{1,0:T(8,128)(2,1)S(1)} %collective-permute-done.7.rest_1_, bf16[264,128]{1,0:T(8,128)(2,1)S(1)} %collective-permute-done.8.rest_2_, ...), custom_call_target="tpu_custom_call" | custom-call | tf_op jit(solution)/shard_map/merge/pallas_call | solution.py:593
  (10 shorter events, 0.0 us)
Async XLA Ops:
  3.0 7.7 %copy-start = (bf16[128,32,384]{2,1,0:T(8,128)(2,1)S(1)}, bf16[128,32,384]{2,1,0:T(8,128)(2,1)}, u32[]{:S(2)}) copy-start(bf16[128,32,384]{2,1,0:T(8,128)(2,1)} %x_ref.3) | copy-start | bytes 9437188
  3.0 49.6 %all-to-all-start = ((bf16[16,520,128]{2,1,0:T(8,128)(2,1)}), bf16[16,520,128]{2,1,0:T(8,128)(2,1)}, u32[]{:S(2)}, u32[]{:S(2)}) async-start(bf16[16,520,128]{2,1,0:T(8,128)(2,1)} %cross.1), calls=%async_computation | async-start | bytes 4259840 | tf_op jit(solution)/shard_map/all_to_all | solution.py:615
  13.5 3.9 %collective-permute-start = (bf16[1024,128]{1,0:T(8,128)(2,1)S(1)}, bf16[1024,128]{1,0:T(8,128)(2,1)S(1)}, u32[]{:S(2)}, u32[]{:S(2)}) collective-permute-start(bf16[1024,128]{1,0:T(8,128)(2,1)S(1)} %get-tuple-element.28), channel_id=1, source_target_pairs={{0,1},{1,0},{2,3},{3,2},{4,5},{5,4},{6,7},{7,6},{8,9},{9,8},{10,11... | collective-permute-start | bytes 786440 | tf_op jit(solution)/shard_map/ppermute | solution.py:620
  13.9 22.2 %collective-permute-start.1 = (bf16[1024,128]{1,0:T(8,128)(2,1)S(1)}, bf16[1024,128]{1,0:T(8,128)(2,1)S(1)}, u32[]{:S(2)}, u32[]{:S(2)}) collective-permute-start(bf16[1024,128]{1,0:T(8,128)(2,1)S(1)} %get-tuple-element.29), channel_id=1, source_target_pairs={{0,2},{1,3},{2,0},{3,1},{4,6},{5,7},{6,4},{7,5},{8,10},{9,11},{10,... | collective-permute-start | bytes 786440 | tf_op jit(solution)/shard_map/ppermute | solution.py:620
  15.6 42.8 %collective-permute-start.2 = (bf16[1024,128]{1,0:T(8,128)(2,1)}, bf16[1024,128]{1,0:T(8,128)(2,1)S(1)}, u32[]{:S(2)}, u32[]{:S(2)}) collective-permute-start(bf16[1024,128]{1,0:T(8,128)(2,1)} %get-tuple-element.30), channel_id=1, source_target_pairs={{0,3},{1,2},{2,1},{3,0},{4,7},{5,6},{6,5},{7,4},{8,11},{9,10},{10,... | collective-permute-start | bytes 786440 | tf_op jit(solution)/shard_map/ppermute | solution.py:620
  15.6 42.8 %collective-permute-start.3 = (bf16[1024,128]{1,0:T(8,128)(2,1)}, bf16[1024,128]{1,0:T(8,128)(2,1)S(1)}, u32[]{:S(2)}, u32[]{:S(2)}) collective-permute-start(bf16[1024,128]{1,0:T(8,128)(2,1)} %get-tuple-element.31), channel_id=1, source_target_pairs={{0,4},{1,5},{2,6},{3,7},{4,0},{5,1},{6,2},{7,3},{8,12},{9,13},{10,... | collective-permute-start | bytes 786440 | tf_op jit(solution)/shard_map/ppermute | solution.py:620
  17.2 41.5 %collective-permute-start.4 = (bf16[1024,128]{1,0:T(8,128)(2,1)}, bf16[1024,128]{1,0:T(8,128)(2,1)S(1)}, u32[]{:S(2)}, u32[]{:S(2)}) collective-permute-start(bf16[1024,128]{1,0:T(8,128)(2,1)} %get-tuple-element.32), channel_id=1, source_target_pairs={{0,5},{1,4},{2,7},{3,6},{4,1},{5,0},{6,3},{7,2},{8,13},{9,12},{10,... | collective-permute-start | bytes 786440 | tf_op jit(solution)/shard_map/ppermute | solution.py:620
  17.4 49.0 %collective-permute-start.5 = (bf16[1024,128]{1,0:T(8,128)(2,1)}, bf16[1024,128]{1,0:T(8,128)(2,1)S(1)}, u32[]{:S(2)}, u32[]{:S(2)}) collective-permute-start(bf16[1024,128]{1,0:T(8,128)(2,1)} %get-tuple-element.33), channel_id=1, source_target_pairs={{0,6},{1,7},{2,4},{3,5},{4,2},{5,3},{6,0},{7,1},{8,14},{9,15},{10,... | collective-permute-start | bytes 786440 | tf_op jit(solution)/shard_map/ppermute | solution.py:620
  36.1 35.0 %collective-permute-start.6 = (bf16[1024,128]{1,0:T(8,128)(2,1)}, bf16[1024,128]{1,0:T(8,128)(2,1)S(1)}, u32[]{:S(2)}, u32[]{:S(2)}) collective-permute-start(bf16[1024,128]{1,0:T(8,128)(2,1)} %get-tuple-element.34), channel_id=1, source_target_pairs={{0,7},{1,6},{2,5},{3,4},{4,3},{5,2},{6,1},{7,0},{8,15},{9,14},{10,... | collective-permute-start | bytes 786440 | tf_op jit(solution)/shard_map/ppermute | solution.py:620
  74.5 30.8 %all-to-all-start.1 = ((bf16[16,264,128]{2,1,0:T(8,128)(2,1)}), bf16[16,264,128]{2,1,0:T(8,128)(2,1)S(1)}, u32[]{:S(2)}, u32[]{:S(2)}) async-start(bf16[16,264,128]{2,1,0:T(8,128)(2,1)} %own.1), calls=%async_computation.1 | async-start | bytes 2162688 | tf_op jit(solution)/shard_map/all_to_all | solution.py:615
  80.9 4.0 %collective-permute-start.7 = (bf16[264,128]{1,0:T(8,128)(2,1)S(1)}, bf16[264,128]{1,0:T(8,128)(2,1)S(1)}, u32[]{:S(2)}, u32[]{:S(2)}) collective-permute-start(bf16[264,128]{1,0:T(8,128)(2,1)S(1)} %get-tuple-element.36), channel_id=1, source_target_pairs={{0,1},{1,0},{2,3},{3,2},{4,5},{5,4},{6,7},{7,6},{8,9},{9,8},{10,11... | collective-permute-start | bytes 202760 | tf_op jit(solution)/shard_map/ppermute | solution.py:620
  81.4 9.0 %collective-permute-start.8 = (bf16[264,128]{1,0:T(8,128)(2,1)S(1)}, bf16[264,128]{1,0:T(8,128)(2,1)S(1)}, u32[]{:S(2)}, u32[]{:S(2)}) collective-permute-start(bf16[264,128]{1,0:T(8,128)(2,1)S(1)} %get-tuple-element.37), channel_id=1, source_target_pairs={{0,2},{1,3},{2,0},{3,1},{4,6},{5,7},{6,4},{7,5},{8,10},{9,11},{10,... | collective-permute-start | bytes 202760 | tf_op jit(solution)/shard_map/ppermute | solution.py:620
  83.1 7.9 %collective-permute-start.9 = (bf16[264,128]{1,0:T(8,128)(2,1)S(1)}, bf16[264,128]{1,0:T(8,128)(2,1)S(1)}, u32[]{:S(2)}, u32[]{:S(2)}) collective-permute-start(bf16[264,128]{1,0:T(8,128)(2,1)S(1)} %get-tuple-element.38), channel_id=1, source_target_pairs={{0,3},{1,2},{2,1},{3,0},{4,7},{5,6},{6,5},{7,4},{8,11},{9,10},{10,... | collective-permute-start | bytes 202760 | tf_op jit(solution)/shard_map/ppermute | solution.py:620
  83.1 15.7 %collective-permute-start.10 = (bf16[264,128]{1,0:T(8,128)(2,1)S(1)}, bf16[264,128]{1,0:T(8,128)(2,1)S(1)}, u32[]{:S(2)}, u32[]{:S(2)}) collective-permute-start(bf16[264,128]{1,0:T(8,128)(2,1)S(1)} %get-tuple-element.39), channel_id=1, source_target_pairs={{0,4},{1,5},{2,6},{3,7},{4,0},{5,1},{6,2},{7,3},{8,12},{9,13},{10,... | collective-permute-start | bytes 202760 | tf_op jit(solution)/shard_map/ppermute | solution.py:620
  84.8 15.5 %collective-permute-start.11 = (bf16[264,128]{1,0:T(8,128)(2,1)S(1)}, bf16[264,128]{1,0:T(8,128)(2,1)S(1)}, u32[]{:S(2)}, u32[]{:S(2)}) collective-permute-start(bf16[264,128]{1,0:T(8,128)(2,1)S(1)} %get-tuple-element.40), channel_id=1, source_target_pairs={{0,5},{1,4},{2,7},{3,6},{4,1},{5,0},{6,3},{7,2},{8,13},{9,12},{10,... | collective-permute-start | bytes 202760 | tf_op jit(solution)/shard_map/ppermute | solution.py:620
  84.9 19.9 %collective-permute-start.12 = (bf16[264,128]{1,0:T(8,128)(2,1)S(1)}, bf16[264,128]{1,0:T(8,128)(2,1)S(1)}, u32[]{:S(2)}, u32[]{:S(2)}) collective-permute-start(bf16[264,128]{1,0:T(8,128)(2,1)S(1)} %get-tuple-element.41), channel_id=1, source_target_pairs={{0,6},{1,7},{2,4},{3,5},{4,2},{5,3},{6,0},{7,1},{8,14},{9,15},{10,... | collective-permute-start | bytes 202760 | tf_op jit(solution)/shard_map/ppermute | solution.py:620
  90.4 14.9 %collective-permute-start.13 = (bf16[264,128]{1,0:T(8,128)(2,1)S(1)}, bf16[264,128]{1,0:T(8,128)(2,1)S(1)}, u32[]{:S(2)}, u32[]{:S(2)}) collective-permute-start(bf16[264,128]{1,0:T(8,128)(2,1)S(1)} %get-tuple-element.42), channel_id=1, source_target_pairs={{0,7},{1,6},{2,5},{3,4},{4,3},{5,2},{6,1},{7,0},{8,15},{9,14},{10,... | collective-permute-start | bytes 202760 | tf_op jit(solution)/shard_map/ppermute | solution.py:620

commit v8 on v7

--- a/solution.py
+++ b/solution.py
@@ -11,6 +11,7 @@
 CLEN = 1024
 QB = 256
 STEP = 64
+HOPS = (0, 2, 3, 6, 7, 4, 5, 1)
 NEG = -1e30
 
 
@@ -561,7 +562,7 @@
             head_ref[up * (heads // 2) + 2 * i + j] = x_ref[
                 up * half + i, j * tok : (j + 1) * tok, :
             ].astype(jnp.float32)
-    for k, near_ref in enumerate(near_refs):
+    for k, near_ref in zip(HOPS, near_refs):
         place = (me ^ k) % half
         far_stats = x_ref[down * half + place, 2 * tok : 2 * tok + 8, :].astype(jnp.float32)
         near_stats = near_ref[2 * tok : 2 * tok + 8, :].astype(jnp.float32)
@@ -627,7 +628,7 @@
     far = far_of(me, labels, cross, tok, rate)
     back = exchange(own(me, labels, far, near, tok, rate))
     near_back = swap(partner(me, labels, near, tok, rate))
-    return merge(me, back, near_back, tok)
+    return merge(me, back, [near_back[k] for k in HOPS], tok)
 
 
 def local(qkv, routes):
@@ -644,7 +645,7 @@
         return lax.all_to_all(x, "seq", split_axis=0, concat_axis=0, tiled=True)
 
     labels = jnp.transpose(routes)
-    paired = nseq & (nseq - 1) == 0 and nseq * tok // 2 % QB == 0
+    paired = nseq == 2 * len(HOPS) and nseq * tok // 2 % QB == 0
     if split == 1 and chunks == 2 and paired and tok == 128 and head_size == 128:
         return two_halves(qkv, labels)
     if split == 1:

time: 107 us -> 106 us (level)
  waiting for transfers between devices: 63.2 us -> 61 us
  starting transfers between devices: 24.7 us -> 25.9 us
    ppermute x14, waiting for transfers between devices: 46.7 us -> 44.5 us  [swap(): moved[k] = lax.ppermute(blocks[k], 'seq', [(i, i ^ k) for i in range(nseq)])]
    ppermute x14, starting transfers between devices: 13 us -> 14.2 us  [swap(): moved[k] = lax.ppermute(blocks[k], 'seq', [(i, i ^ k) for i in range(nseq)])]
where the time goes in v8:
time: 106 us
  waiting for transfers between devices  61 us (58%)
  starting transfers between devices  25.9 us (24%)
  Pallas kernels  18.1 us (17%)
    ppermute x14, waiting for transfers between devices, swap(): moved[k] = lax.ppermute(blocks[k], 'seq', [(i, i ^ k) for i in range(nseq)])  44.5 us
    all_to_all x2, waiting for transfers between devices, exchange(): return lax.all_to_all(x, 'seq', split_axis=0, concat_axis=0, tiled=True)  16.5 us
    ppermute x14, starting transfers between devices, swap(): moved[k] = lax.ppermute(blocks[k], 'seq', [(i, i ^ k) for i in range(nseq)])  14.2 us
    all_to_all x2, starting transfers between devices, exchange(): return lax.all_to_all(x, 'seq', split_axis=0, concat_axis=0, tiled=True)  11.7 us
    pallas_call x1, Pallas kernels, far_of(): pl.pallas_call(functools.partial(far_kernel, tok=tok, rate=rate), out_sha...  4.93 us
    pallas_call x1, Pallas kernels, own(): pl.pallas_call(functools.partial(own_kernel, tok=tok, rate=rate), out_sha...  3.44 us
    pallas_call x1, Pallas kernels, spread(): pl.pallas_call(cross_kernel, out_shape=jax.ShapeDtypeStruct((nseq, 4 * to...  2.97 us
    pallas_call x1, Pallas kernels, spread(): pl.pallas_call(near_kernel, out_shape=[jax.ShapeDtypeStruct((8 * tok, 128...  2.83 us
  transfers between devices with their start and end apart: 16, of which 11 were waited for; matrix products, arithmetic and copies ran while one was open for 1% of the time, Pallas kernels for 10%

profile of v8, /device:TPU:0, one launch (start us, length us, event | category | flops | bytes accessed | tf_op | source)
XLA Modules:
  0.0 106.0 jit_solution(16727018051467521716)
XLA Ops:
  0.0 3.0 %cross.1 = bf16[16,520,128]{2,1,0:T(8,128)(2,1)} custom-call(s32[1]{0:T(128)} %bitcast.me_ref, bf16[128,32,384]{2,1,0:T(8,128)(2,1)} %x_ref.3, s32[32,128]{1,0:T(8,128)} %bitcast.4), custom_call_target="tpu_custom_call" | custom-call | tf_op jit(solution)/shard_map/cross/pallas_call | solution.py:237
  3.0 0.0 copy-start
  3.0 7.7 %all-to-all-start = ((bf16[16,520,128]{2,1,0:T(8,128)(2,1)}), bf16[16,520,128]{2,1,0:T(8,128)(2,1)}, u32[]{:S(2)}, u32[]{:S(2)}) async-start(bf16[16,520,128]{2,1,0:T(8,128)(2,1)} %cross.1), calls=%async_computation | async-start | bytes 4259840 | tf_op jit(solution)/shard_map/all_to_all | solution.py:616
  10.7 2.8 %near.1 = (bf16[1024,128]{1,0:T(8,128)(2,1)S(1)}, bf16[1024,128]{1,0:T(8,128)(2,1)S(1)}, bf16[1024,128]{1,0:T(8,128)(2,1)S(1)}, bf16[1024,128]{1,0:T(8,128)(2,1)...) custom-call(s32[1]{0:T(128)} %bitcast.me_ref, ...), custom_call_target="tpu_custom_call" | custom-call | tf_op jit(solution)/shard_map/near/pallas_call | solution.py:252
  13.5 0.4 collective-permute-start
  13.9 1.7 %collective-permute-start.1 = (bf16[1024,128]{1,0:T(8,128)(2,1)S(1)}, bf16[1024,128]{1,0:T(8,128)(2,1)S(1)}, u32[]{:S(2)}, u32[]{:S(2)}) collective-permute-start(bf16[1024,128]{1,0:T(8,128)(2,1)S(1)} %get-tuple-element.29), channel_id=1, source_target_pairs={{0,2},{1,3},{2,0},{3,1},{4,6},{5,7},{6,4},{7,5},{8,10},{9,11},{10,... | collective-permute-start | bytes 786440 | tf_op jit(solution)/shard_map/ppermute | solution.py:621
  15.6 1.7 %collective-permute-start.3 = (bf16[1024,128]{1,0:T(8,128)(2,1)}, bf16[1024,128]{1,0:T(8,128)(2,1)S(1)}, u32[]{:S(2)}, u32[]{:S(2)}) collective-permute-start(bf16[1024,128]{1,0:T(8,128)(2,1)} %get-tuple-element.31), channel_id=1, source_target_pairs={{0,4},{1,5},{2,6},{3,7},{4,0},{5,1},{6,2},{7,3},{8,12},{9,13},{10,... | collective-permute-start | bytes 786440 | tf_op jit(solution)/shard_map/ppermute | solution.py:621
  17.2 0.1 collective-permute-start.4
  17.4 0.0 collective-permute-done.rest_1_
  17.4 2.6 %collective-permute-start.5 = (bf16[1024,128]{1,0:T(8,128)(2,1)}, bf16[1024,128]{1,0:T(8,128)(2,1)S(1)}, u32[]{:S(2)}, u32[]{:S(2)}) collective-permute-start(bf16[1024,128]{1,0:T(8,128)(2,1)} %get-tuple-element.33), channel_id=1, source_target_pairs={{0,6},{1,7},{2,4},{3,5},{4,2},{5,3},{6,0},{7,1},{8,14},{9,15},{10,... | collective-permute-start | bytes 786440 | tf_op jit(solution)/shard_map/ppermute | solution.py:621
  19.9 16.1 %collective-permute-done.1.rest_2_ = bf16[1024,128]{1,0:T(8,128)(2,1)S(1)} collective-permute-done((bf16[1024,128]{1,0:T(8,128)(2,1)S(1)}, bf16[1024,128]{1,0:T(8,128)(2,1)S(1)}, u32[]{:S(2)}, u32[]{:S(2)}) %collective-permute-start.1) | collective-permute-done | bytes 262176 | tf_op jit(solution)/shard_map/ppermute | solution.py:621
  36.1 16.5 %all-to-all-done.x_ref = bf16[16,520,128]{2,1,0:T(8,128)(2,1)} async-done(((bf16[16,520,128]{2,1,0:T(8,128)(2,1)}), bf16[16,520,128]{2,1,0:T(8,128)(2,1)}, u32[]{:S(2)}, u32[]{:S(2)}) %all-to-all-start) | async-done | bytes 2129952 | tf_op jit(solution)/shard_map/all_to_all | solution.py:616
  52.6 0.8 slice.4
  53.4 4.9 %far.1 = (f32[2,1024,128]{2,1,0:T(8,128)S(1)}, f32[2,8,128]{2,1,0:T(8,128)S(1)}, bf16[4,1024,128]{2,1,0:T(8,128)(2,1)S(1)}) custom-call(s32[1]{0:T(128)} %bitcast.me_ref, s32[4,16,128]{2,1,0:T(8,128)S(1)} %convert_bitcast_fusion.lab_ref, bf16[16,520,128]{2,1,0:T(8,128)(2,1)} %all-to-all-done.x_ref), custom_call_target="tpu_custom_call" | custom-call | tf_op jit(solution)/shard_map/far/pallas_call | solution.py:357
  58.3 0.5 collective-permute-done.4.rest_5_
  58.8 7.6 %collective-permute-done.5.rest_6_ = bf16[1024,128]{1,0:T(8,128)(2,1)S(1)} collective-permute-done((bf16[1024,128]{1,0:T(8,128)(2,1)}, bf16[1024,128]{1,0:T(8,128)(2,1)S(1)}, u32[]{:S(2)}, u32[]{:S(2)}) %collective-permute-start.5) | collective-permute-done | bytes 262176 | tf_op jit(solution)/shard_map/ppermute | solution.py:621
  66.4 4.7 %collective-permute-done.6.rest_7_ = bf16[1024,128]{1,0:T(8,128)(2,1)S(1)} collective-permute-done((bf16[1024,128]{1,0:T(8,128)(2,1)}, bf16[1024,128]{1,0:T(8,128)(2,1)S(1)}, u32[]{:S(2)}, u32[]{:S(2)}) %collective-permute-start.6) | collective-permute-done | bytes 262176 | tf_op jit(solution)/shard_map/ppermute | solution.py:621
  71.1 3.4 %own.1 = bf16[16,264,128]{2,1,0:T(8,128)(2,1)} custom-call(s32[1]{0:T(128)} %bitcast.me_ref, s32[4,16,128]{2,1,0:T(8,128)S(1)} %convert_bitcast_fusion.lab_ref, f32[2,1024,128]{2,1,0:T(8,128)S(1)} %get-tuple-element.24.far_ref, f32[2,8,128]{2,1,0:T(8,128)S(1)} %get-tuple-element.25.far_stat_ref, bf16[4,1024,128]{2,1,0:T(8,128)(2,1)S(1)} %get-tuple-element.26.half_ref, ...), custom_call_target="tpu_custom_call" | custom-call | tf_op jit(solution)/shard_map/own/pallas_call | solution.py:462
  74.5 4.0 %all-to-all-start.1 = ((bf16[16,264,128]{2,1,0:T(8,128)(2,1)}), bf16[16,264,128]{2,1,0:T(8,128)(2,1)S(1)}, u32[]{:S(2)}, u32[]{:S(2)}) async-start(bf16[16,264,128]{2,1,0:T(8,128)(2,1)} %own.1), calls=%async_computation.1 | async-start | bytes 2162688 | tf_op jit(solution)/shard_map/all_to_all | solution.py:616
  78.5 2.4 %partner.1 = (bf16[264,128]{1,0:T(8,128)(2,1)S(1)}, bf16[264,128]{1,0:T(8,128)(2,1)S(1)}, bf16[264,128]{1,0:T(8,128)(2,1)S(1)}, bf16[264,128]{1,0:T(8,128)(2,1)S...) custom-call(s32[1]{0:T(128)} %bitcast.me_ref, ...), custom_call_target="tpu_custom_call" | custom-call | tf_op jit(solution)/shard_map/partner/pallas_call | solution.py:533
  80.9 2.0 %collective-permute-start.7 = (bf16[264,128]{1,0:T(8,128)(2,1)S(1)}, bf16[264,128]{1,0:T(8,128)(2,1)S(1)}, u32[]{:S(2)}, u32[]{:S(2)}) collective-permute-start(bf16[264,128]{1,0:T(8,128)(2,1)S(1)} %get-tuple-element.36), channel_id=1, source_target_pairs={{0,2},{1,3},{2,0},{3,1},{4,6},{5,7},{6,4},{7,5},{8,10},{9,11},{10,... | collective-permute-start | bytes 202760 | tf_op jit(solution)/shard_map/ppermute | solution.py:621
  82.9 2.4 %collective-permute-start.9 = (bf16[264,128]{1,0:T(8,128)(2,1)S(1)}, bf16[264,128]{1,0:T(8,128)(2,1)S(1)}, u32[]{:S(2)}, u32[]{:S(2)}) collective-permute-start(bf16[264,128]{1,0:T(8,128)(2,1)S(1)} %get-tuple-element.38), channel_id=1, source_target_pairs={{0,6},{1,7},{2,4},{3,5},{4,2},{5,3},{6,0},{7,1},{8,14},{9,15},{10,... | collective-permute-start | bytes 202760 | tf_op jit(solution)/shard_map/ppermute | solution.py:621
  85.3 0.3 collective-permute-start.10
  85.6 1.7 %collective-permute-start.11 = (bf16[264,128]{1,0:T(8,128)(2,1)S(1)}, bf16[264,128]{1,0:T(8,128)(2,1)S(1)}, u32[]{:S(2)}, u32[]{:S(2)}) collective-permute-start(bf16[264,128]{1,0:T(8,128)(2,1)S(1)} %get-tuple-element.40), channel_id=1, source_target_pairs={{0,4},{1,5},{2,6},{3,7},{4,0},{5,1},{6,2},{7,3},{8,12},{9,13},{10,... | collective-permute-start | bytes 202760 | tf_op jit(solution)/shard_map/ppermute | solution.py:621
  87.3 3.0 %collective-permute-done.7.rest_1_ = bf16[264,128]{1,0:T(8,128)(2,1)S(1)} collective-permute-done((bf16[264,128]{1,0:T(8,128)(2,1)S(1)}, bf16[264,128]{1,0:T(8,128)(2,1)S(1)}, u32[]{:S(2)}, u32[]{:S(2)}) %collective-permute-start.7) | collective-permute-done | bytes 67616 | tf_op jit(solution)/shard_map/ppermute | solution.py:621
  90.4 0.6 collective-permute-done.8.rest_2_
  91.0 1.4 %collective-permute-start.13 = (bf16[264,128]{1,0:T(8,128)(2,1)S(1)}, bf16[264,128]{1,0:T(8,128)(2,1)S(1)}, u32[]{:S(2)}, u32[]{:S(2)}) collective-permute-start(bf16[264,128]{1,0:T(8,128)(2,1)S(1)} %get-tuple-element.42), channel_id=1, source_target_pairs={{0,1},{1,0},{2,3},{3,2},{4,5},{5,4},{6,7},{7,6},{8,9},{9,8},{10,11... | collective-permute-start | bytes 202760 | tf_op jit(solution)/shard_map/ppermute | solution.py:621
  92.4 6.9 %collective-permute-done.9.rest_3_ = bf16[264,128]{1,0:T(8,128)(2,1)S(1)} collective-permute-done((bf16[264,128]{1,0:T(8,128)(2,1)S(1)}, bf16[264,128]{1,0:T(8,128)(2,1)S(1)}, u32[]{:S(2)}, u32[]{:S(2)}) %collective-permute-start.9) | collective-permute-done | bytes 67616 | tf_op jit(solution)/shard_map/ppermute | solution.py:621
  99.2 1.8 %collective-permute-done.10.rest_4_ = bf16[264,128]{1,0:T(8,128)(2,1)S(1)} collective-permute-done((bf16[264,128]{1,0:T(8,128)(2,1)S(1)}, bf16[264,128]{1,0:T(8,128)(2,1)S(1)}, u32[]{:S(2)}, u32[]{:S(2)}) %collective-permute-start.10) | collective-permute-done | bytes 67616 | tf_op jit(solution)/shard_map/ppermute | solution.py:621
  101.0 2.8 %collective-permute-done.11.rest_5_ = bf16[264,128]{1,0:T(8,128)(2,1)S(1)} collective-permute-done((bf16[264,128]{1,0:T(8,128)(2,1)S(1)}, bf16[264,128]{1,0:T(8,128)(2,1)S(1)}, u32[]{:S(2)}, u32[]{:S(2)}) %collective-permute-start.11) | collective-permute-done | bytes 67616 | tf_op jit(solution)/shard_map/ppermute | solution.py:621
  103.8 0.5 collective-permute-done.12.rest_6_
  104.3 1.5 %merge.1 = bf16[128,32,128]{2,1,0:T(8,128)(2,1)} custom-call(s32[1]{0:T(128)} %bitcast.me_ref, bf16[16,264,128]{2,1,0:T(8,128)(2,1)S(1)} %all-to-all-done.1.x_ref, bf16[264,128]{1,0:T(8,128)(2,1)S(1)} %get-tuple-element.35.rest_0_, bf16[264,128]{1,0:T(8,128)(2,1)S(1)} %collective-permute-done.7.rest_1_, bf16[264,128]{1,0:T(8,128)(2,1)S(1)} %collective-permute-done.8.rest_2_, ...), custom_call_target="tpu_custom_call" | custom-call | tf_op jit(solution)/shard_map/merge/pallas_call | solution.py:594
  (10 shorter events, 0.0 us)
Async XLA Ops:
  3.0 7.7 %copy-start = (bf16[128,32,384]{2,1,0:T(8,128)(2,1)S(1)}, bf16[128,32,384]{2,1,0:T(8,128)(2,1)}, u32[]{:S(2)}) copy-start(bf16[128,32,384]{2,1,0:T(8,128)(2,1)} %x_ref.3) | copy-start | bytes 9437188
  3.0 49.6 %all-to-all-start = ((bf16[16,520,128]{2,1,0:T(8,128)(2,1)}), bf16[16,520,128]{2,1,0:T(8,128)(2,1)}, u32[]{:S(2)}, u32[]{:S(2)}) async-start(bf16[16,520,128]{2,1,0:T(8,128)(2,1)} %cross.1), calls=%async_computation | async-start | bytes 4259840 | tf_op jit(solution)/shard_map/all_to_all | solution.py:616
  13.5 3.9 %collective-permute-start = (bf16[1024,128]{1,0:T(8,128)(2,1)S(1)}, bf16[1024,128]{1,0:T(8,128)(2,1)S(1)}, u32[]{:S(2)}, u32[]{:S(2)}) collective-permute-start(bf16[1024,128]{1,0:T(8,128)(2,1)S(1)} %get-tuple-element.28), channel_id=1, source_target_pairs={{0,1},{1,0},{2,3},{3,2},{4,5},{5,4},{6,7},{7,6},{8,9},{9,8},{10,11... | collective-permute-start | bytes 786440 | tf_op jit(solution)/shard_map/ppermute | solution.py:621
  13.9 22.2 %collective-permute-start.1 = (bf16[1024,128]{1,0:T(8,128)(2,1)S(1)}, bf16[1024,128]{1,0:T(8,128)(2,1)S(1)}, u32[]{:S(2)}, u32[]{:S(2)}) collective-permute-start(bf16[1024,128]{1,0:T(8,128)(2,1)S(1)} %get-tuple-element.29), channel_id=1, source_target_pairs={{0,2},{1,3},{2,0},{3,1},{4,6},{5,7},{6,4},{7,5},{8,10},{9,11},{10,... | collective-permute-start | bytes 786440 | tf_op jit(solution)/shard_map/ppermute | solution.py:621
  15.6 42.8 %collective-permute-start.2 = (bf16[1024,128]{1,0:T(8,128)(2,1)}, bf16[1024,128]{1,0:T(8,128)(2,1)S(1)}, u32[]{:S(2)}, u32[]{:S(2)}) collective-permute-start(bf16[1024,128]{1,0:T(8,128)(2,1)} %get-tuple-element.30), channel_id=1, source_target_pairs={{0,3},{1,2},{2,1},{3,0},{4,7},{5,6},{6,5},{7,4},{8,11},{9,10},{10,... | collective-permute-start | bytes 786440 | tf_op jit(solution)/shard_map/ppermute | solution.py:621
  15.6 42.8 %collective-permute-start.3 = (bf16[1024,128]{1,0:T(8,128)(2,1)}, bf16[1024,128]{1,0:T(8,128)(2,1)S(1)}, u32[]{:S(2)}, u32[]{:S(2)}) collective-permute-start(bf16[1024,128]{1,0:T(8,128)(2,1)} %get-tuple-element.31), channel_id=1, source_target_pairs={{0,4},{1,5},{2,6},{3,7},{4,0},{5,1},{6,2},{7,3},{8,12},{9,13},{10,... | collective-permute-start | bytes 786440 | tf_op jit(solution)/shard_map/ppermute | solution.py:621
  17.2 41.5 %collective-permute-start.4 = (bf16[1024,128]{1,0:T(8,128)(2,1)}, bf16[1024,128]{1,0:T(8,128)(2,1)S(1)}, u32[]{:S(2)}, u32[]{:S(2)}) collective-permute-start(bf16[1024,128]{1,0:T(8,128)(2,1)} %get-tuple-element.32), channel_id=1, source_target_pairs={{0,5},{1,4},{2,7},{3,6},{4,1},{5,0},{6,3},{7,2},{8,13},{9,12},{10,... | collective-permute-start | bytes 786440 | tf_op jit(solution)/shard_map/ppermute | solution.py:621
  17.4 49.0 %collective-permute-start.5 = (bf16[1024,128]{1,0:T(8,128)(2,1)}, bf16[1024,128]{1,0:T(8,128)(2,1)S(1)}, u32[]{:S(2)}, u32[]{:S(2)}) collective-permute-start(bf16[1024,128]{1,0:T(8,128)(2,1)} %get-tuple-element.33), channel_id=1, source_target_pairs={{0,6},{1,7},{2,4},{3,5},{4,2},{5,3},{6,0},{7,1},{8,14},{9,15},{10,... | collective-permute-start | bytes 786440 | tf_op jit(solution)/shard_map/ppermute | solution.py:621
  36.1 35.0 %collective-permute-start.6 = (bf16[1024,128]{1,0:T(8,128)(2,1)}, bf16[1024,128]{1,0:T(8,128)(2,1)S(1)}, u32[]{:S(2)}, u32[]{:S(2)}) collective-permute-start(bf16[1024,128]{1,0:T(8,128)(2,1)} %get-tuple-element.34), channel_id=1, source_target_pairs={{0,7},{1,6},{2,5},{3,4},{4,3},{5,2},{6,1},{7,0},{8,15},{9,14},{10,... | collective-permute-start | bytes 786440 | tf_op jit(solution)/shard_map/ppermute | solution.py:621
  74.5 29.8 %all-to-all-start.1 = ((bf16[16,264,128]{2,1,0:T(8,128)(2,1)}), bf16[16,264,128]{2,1,0:T(8,128)(2,1)S(1)}, u32[]{:S(2)}, u32[]{:S(2)}) async-start(bf16[16,264,128]{2,1,0:T(8,128)(2,1)} %own.1), calls=%async_computation.1 | async-start | bytes 2162688 | tf_op jit(solution)/shard_map/all_to_all | solution.py:616
  80.9 9.4 %collective-permute-start.7 = (bf16[264,128]{1,0:T(8,128)(2,1)S(1)}, bf16[264,128]{1,0:T(8,128)(2,1)S(1)}, u32[]{:S(2)}, u32[]{:S(2)}) collective-permute-start(bf16[264,128]{1,0:T(8,128)(2,1)S(1)} %get-tuple-element.36), channel_id=1, source_target_pairs={{0,2},{1,3},{2,0},{3,1},{4,6},{5,7},{6,4},{7,5},{8,10},{9,11},{10,... | collective-permute-start | bytes 202760 | tf_op jit(solution)/shard_map/ppermute | solution.py:621
  82.9 8.1 %collective-permute-start.8 = (bf16[264,128]{1,0:T(8,128)(2,1)S(1)}, bf16[264,128]{1,0:T(8,128)(2,1)S(1)}, u32[]{:S(2)}, u32[]{:S(2)}) collective-permute-start(bf16[264,128]{1,0:T(8,128)(2,1)S(1)} %get-tuple-element.37), channel_id=1, source_target_pairs={{0,3},{1,2},{2,1},{3,0},{4,7},{5,6},{6,5},{7,4},{8,11},{9,10},{10,... | collective-permute-start | bytes 202760 | tf_op jit(solution)/shard_map/ppermute | solution.py:621
  82.9 16.3 %collective-permute-start.9 = (bf16[264,128]{1,0:T(8,128)(2,1)S(1)}, bf16[264,128]{1,0:T(8,128)(2,1)S(1)}, u32[]{:S(2)}, u32[]{:S(2)}) collective-permute-start(bf16[264,128]{1,0:T(8,128)(2,1)S(1)} %get-tuple-element.38), channel_id=1, source_target_pairs={{0,6},{1,7},{2,4},{3,5},{4,2},{5,3},{6,0},{7,1},{8,14},{9,15},{10,... | collective-permute-start | bytes 202760 | tf_op jit(solution)/shard_map/ppermute | solution.py:621
  85.3 15.7 %collective-permute-start.10 = (bf16[264,128]{1,0:T(8,128)(2,1)S(1)}, bf16[264,128]{1,0:T(8,128)(2,1)S(1)}, u32[]{:S(2)}, u32[]{:S(2)}) collective-permute-start(bf16[264,128]{1,0:T(8,128)(2,1)S(1)} %get-tuple-element.39), channel_id=1, source_target_pairs={{0,7},{1,6},{2,5},{3,4},{4,3},{5,2},{6,1},{7,0},{8,15},{9,14},{10,... | collective-permute-start | bytes 202760 | tf_op jit(solution)/shard_map/ppermute | solution.py:621
  85.6 18.2 %collective-permute-start.11 = (bf16[264,128]{1,0:T(8,128)(2,1)S(1)}, bf16[264,128]{1,0:T(8,128)(2,1)S(1)}, u32[]{:S(2)}, u32[]{:S(2)}) collective-permute-start(bf16[264,128]{1,0:T(8,128)(2,1)S(1)} %get-tuple-element.40), channel_id=1, source_target_pairs={{0,4},{1,5},{2,6},{3,7},{4,0},{5,1},{6,2},{7,3},{8,12},{9,13},{10,... | collective-permute-start | bytes 202760 | tf_op jit(solution)/shard_map/ppermute | solution.py:621
  90.4 14.0 %collective-permute-start.12 = (bf16[264,128]{1,0:T(8,128)(2,1)S(1)}, bf16[264,128]{1,0:T(8,128)(2,1)S(1)}, u32[]{:S(2)}, u32[]{:S(2)}) collective-permute-start(bf16[264,128]{1,0:T(8,128)(2,1)S(1)} %get-tuple-element.41), channel_id=1, source_target_pairs={{0,5},{1,4},{2,7},{3,6},{4,1},{5,0},{6,3},{7,2},{8,13},{9,12},{10,... | collective-permute-start | bytes 202760 | tf_op jit(solution)/shard_map/ppermute | solution.py:621
  91.0 13.3 %collective-permute-start.13 = (bf16[264,128]{1,0:T(8,128)(2,1)S(1)}, bf16[264,128]{1,0:T(8,128)(2,1)S(1)}, u32[]{:S(2)}, u32[]{:S(2)}) collective-permute-start(bf16[264,128]{1,0:T(8,128)(2,1)S(1)} %get-tuple-element.42), channel_id=1, source_target_pairs={{0,1},{1,0},{2,3},{3,2},{4,5},{5,4},{6,7},{7,6},{8,9},{9,8},{10,11... | collective-permute-start | bytes 202760 | tf_op jit(solution)/shard_map/ppermute | solution.py:621

commit v9 on v8

--- a/solution.py
+++ b/solution.py
@@ -11,7 +11,7 @@
 CLEN = 1024
 QB = 256
 STEP = 64
-HOPS = (0, 2, 3, 6, 7, 4, 5, 1)
+HOPS = (0, 2, 6, 3, 7, 4, 5, 1)
 NEG = -1e30
 
 

time: 106 us -> 106 us (level)
  waiting for transfers between devices: 61 us -> 62.1 us
  starting transfers between devices: 25.9 us -> 24.8 us
    ppermute x14, starting transfers between devices: 14.2 us -> 13.1 us  [swap(): moved[k] = lax.ppermute(blocks[k], 'seq', [(i, i ^ k) for i in range(nseq)])]
    ppermute x14, waiting for transfers between devices: 44.5 us -> 45.6 us  [swap(): moved[k] = lax.ppermute(blocks[k], 'seq', [(i, i ^ k) for i in range(nseq)])]
  transfers between devices with their start and end apart: 16 -> 16, of which waited for: 11 -> 10; matrix products, arithmetic and copies ran while one was open for 1% -> 1% of each run, Pallas kernels for 10% -> 10%
where the time goes in v9:
time: 106 us
  waiting for transfers between devices  62.1 us (59%)
  starting transfers between devices  24.8 us (23%)
  Pallas kernels  18.1 us (17%)
    ppermute x14, waiting for transfers between devices, swap(): moved[k] = lax.ppermute(blocks[k], 'seq', [(i, i ^ k) for i in range(nseq)])  45.6 us
    all_to_all x2, waiting for transfers between devices, exchange(): return lax.all_to_all(x, 'seq', split_axis=0, concat_axis=0, tiled=True)  16.5 us
    ppermute x14, starting transfers between devices, swap(): moved[k] = lax.ppermute(blocks[k], 'seq', [(i, i ^ k) for i in range(nseq)])  13.1 us
    all_to_all x2, starting transfers between devices, exchange(): return lax.all_to_all(x, 'seq', split_axis=0, concat_axis=0, tiled=True)  11.7 us
    pallas_call x1, Pallas kernels, far_of(): pl.pallas_call(functools.partial(far_kernel, tok=tok, rate=rate), out_sha...  4.93 us
    pallas_call x1, Pallas kernels, own(): pl.pallas_call(functools.partial(own_kernel, tok=tok, rate=rate), out_sha...  3.44 us
    pallas_call x1, Pallas kernels, spread(): pl.pallas_call(cross_kernel, out_shape=jax.ShapeDtypeStruct((nseq, 4 * to...  2.97 us
    pallas_call x1, Pallas kernels, spread(): pl.pallas_call(near_kernel, out_shape=[jax.ShapeDtypeStruct((8 * tok, 128...  2.83 us
  transfers between devices with their start and end apart: 16, of which 10 were waited for; matrix products, arithmetic and copies ran while one was open for 1% of the time, Pallas kernels for 10%

profile of v9, /device:TPU:0, one launch (start us, length us, event | category | flops | bytes accessed | tf_op | source)
XLA Modules:
  0.0 106.0 jit_solution(14075485217141732077)
XLA Ops:
  0.0 3.0 %cross.1 = bf16[16,520,128]{2,1,0:T(8,128)(2,1)} custom-call(s32[1]{0:T(128)} %bitcast.me_ref, bf16[128,32,384]{2,1,0:T(8,128)(2,1)} %x_ref.3, s32[32,128]{1,0:T(8,128)} %bitcast.4), custom_call_target="tpu_custom_call" | custom-call | tf_op jit(solution)/shard_map/cross/pallas_call | solution.py:237
  3.0 0.0 copy-start
  3.0 7.7 %all-to-all-start = ((bf16[16,520,128]{2,1,0:T(8,128)(2,1)}), bf16[16,520,128]{2,1,0:T(8,128)(2,1)}, u32[]{:S(2)}, u32[]{:S(2)}) async-start(bf16[16,520,128]{2,1,0:T(8,128)(2,1)} %cross.1), calls=%async_computation | async-start | bytes 4259840 | tf_op jit(solution)/shard_map/all_to_all | solution.py:616
  10.7 2.8 %near.1 = (bf16[1024,128]{1,0:T(8,128)(2,1)S(1)}, bf16[1024,128]{1,0:T(8,128)(2,1)S(1)}, bf16[1024,128]{1,0:T(8,128)(2,1)S(1)}, bf16[1024,128]{1,0:T(8,128)(2,1)...) custom-call(s32[1]{0:T(128)} %bitcast.me_ref, ...), custom_call_target="tpu_custom_call" | custom-call | tf_op jit(solution)/shard_map/near/pallas_call | solution.py:252
  13.5 0.4 collective-permute-start
  13.9 1.7 %collective-permute-start.1 = (bf16[1024,128]{1,0:T(8,128)(2,1)S(1)}, bf16[1024,128]{1,0:T(8,128)(2,1)S(1)}, u32[]{:S(2)}, u32[]{:S(2)}) collective-permute-start(bf16[1024,128]{1,0:T(8,128)(2,1)S(1)} %get-tuple-element.29), channel_id=1, source_target_pairs={{0,2},{1,3},{2,0},{3,1},{4,6},{5,7},{6,4},{7,5},{8,10},{9,11},{10,... | collective-permute-start | bytes 786440 | tf_op jit(solution)/shard_map/ppermute | solution.py:621
  15.6 1.7 %collective-permute-start.3 = (bf16[1024,128]{1,0:T(8,128)(2,1)}, bf16[1024,128]{1,0:T(8,128)(2,1)S(1)}, u32[]{:S(2)}, u32[]{:S(2)}) collective-permute-start(bf16[1024,128]{1,0:T(8,128)(2,1)} %get-tuple-element.31), channel_id=1, source_target_pairs={{0,4},{1,5},{2,6},{3,7},{4,0},{5,1},{6,2},{7,3},{8,12},{9,13},{10,... | collective-permute-start | bytes 786440 | tf_op jit(solution)/shard_map/ppermute | solution.py:621
  17.2 0.1 collective-permute-start.4
  17.4 2.6 %collective-permute-start.5 = (bf16[1024,128]{1,0:T(8,128)(2,1)}, bf16[1024,128]{1,0:T(8,128)(2,1)S(1)}, u32[]{:S(2)}, u32[]{:S(2)}) collective-permute-start(bf16[1024,128]{1,0:T(8,128)(2,1)} %get-tuple-element.33), channel_id=1, source_target_pairs={{0,6},{1,7},{2,4},{3,5},{4,2},{5,3},{6,0},{7,1},{8,14},{9,15},{10,... | collective-permute-start | bytes 786440 | tf_op jit(solution)/shard_map/ppermute | solution.py:621
  19.9 16.1 %collective-permute-done.1.rest_2_ = bf16[1024,128]{1,0:T(8,128)(2,1)S(1)} collective-permute-done((bf16[1024,128]{1,0:T(8,128)(2,1)S(1)}, bf16[1024,128]{1,0:T(8,128)(2,1)S(1)}, u32[]{:S(2)}, u32[]{:S(2)}) %collective-permute-start.1) | collective-permute-done | bytes 262176 | tf_op jit(solution)/shard_map/ppermute | solution.py:621
  36.1 0.0 collective-permute-start.6
  36.1 16.5 %all-to-all-done.x_ref = bf16[16,520,128]{2,1,0:T(8,128)(2,1)} async-done(((bf16[16,520,128]{2,1,0:T(8,128)(2,1)}), bf16[16,520,128]{2,1,0:T(8,128)(2,1)}, u32[]{:S(2)}, u32[]{:S(2)}) %all-to-all-start) | async-done | bytes 2129952 | tf_op jit(solution)/shard_map/all_to_all | solution.py:616
  52.6 0.8 slice.4
  53.4 4.9 %far.1 = (f32[2,1024,128]{2,1,0:T(8,128)S(1)}, f32[2,8,128]{2,1,0:T(8,128)S(1)}, bf16[4,1024,128]{2,1,0:T(8,128)(2,1)S(1)}) custom-call(s32[1]{0:T(128)} %bitcast.me_ref, s32[4,16,128]{2,1,0:T(8,128)S(1)} %convert_bitcast_fusion.lab_ref, bf16[16,520,128]{2,1,0:T(8,128)(2,1)} %all-to-all-done.x_ref), custom_call_target="tpu_custom_call" | custom-call | tf_op jit(solution)/shard_map/far/pallas_call | solution.py:357
  58.3 0.5 collective-permute-done.4.rest_5_
  58.8 7.6 %collective-permute-done.5.rest_6_ = bf16[1024,128]{1,0:T(8,128)(2,1)S(1)} collective-permute-done((bf16[1024,128]{1,0:T(8,128)(2,1)}, bf16[1024,128]{1,0:T(8,128)(2,1)S(1)}, u32[]{:S(2)}, u32[]{:S(2)}) %collective-permute-start.5) | collective-permute-done | bytes 262176 | tf_op jit(solution)/shard_map/ppermute | solution.py:621
  66.4 4.7 %collective-permute-done.6.rest_7_ = bf16[1024,128]{1,0:T(8,128)(2,1)S(1)} collective-permute-done((bf16[1024,128]{1,0:T(8,128)(2,1)}, bf16[1024,128]{1,0:T(8,128)(2,1)S(1)}, u32[]{:S(2)}, u32[]{:S(2)}) %collective-permute-start.6) | collective-permute-done | bytes 262176 | tf_op jit(solution)/shard_map/ppermute | solution.py:621
  71.1 3.4 %own.1 = bf16[16,264,128]{2,1,0:T(8,128)(2,1)} custom-call(s32[1]{0:T(128)} %bitcast.me_ref, s32[4,16,128]{2,1,0:T(8,128)S(1)} %convert_bitcast_fusion.lab_ref, f32[2,1024,128]{2,1,0:T(8,128)S(1)} %get-tuple-element.24.far_ref, f32[2,8,128]{2,1,0:T(8,128)S(1)} %get-tuple-element.25.far_stat_ref, bf16[4,1024,128]{2,1,0:T(8,128)(2,1)S(1)} %get-tuple-element.26.half_ref, ...), custom_call_target="tpu_custom_call" | custom-call | tf_op jit(solution)/shard_map/own/pallas_call | solution.py:462
  74.5 4.0 %all-to-all-start.1 = ((bf16[16,264,128]{2,1,0:T(8,128)(2,1)}), bf16[16,264,128]{2,1,0:T(8,128)(2,1)S(1)}, u32[]{:S(2)}, u32[]{:S(2)}) async-start(bf16[16,264,128]{2,1,0:T(8,128)(2,1)} %own.1), calls=%async_computation.1 | async-start | bytes 2162688 | tf_op jit(solution)/shard_map/all_to_all | solution.py:616
  78.5 2.4 %partner.1 = (bf16[264,128]{1,0:T(8,128)(2,1)S(1)}, bf16[264,128]{1,0:T(8,128)(2,1)S(1)}, bf16[264,128]{1,0:T(8,128)(2,1)S(1)}, bf16[264,128]{1,0:T(8,128)(2,1)S...) custom-call(s32[1]{0:T(128)} %bitcast.me_ref, ...), custom_call_target="tpu_custom_call" | custom-call | tf_op jit(solution)/shard_map/partner/pallas_call | solution.py:533
  80.9 2.0 %collective-permute-start.7 = (bf16[264,128]{1,0:T(8,128)(2,1)S(1)}, bf16[264,128]{1,0:T(8,128)(2,1)S(1)}, u32[]{:S(2)}, u32[]{:S(2)}) collective-permute-start(bf16[264,128]{1,0:T(8,128)(2,1)S(1)} %get-tuple-element.36), channel_id=1, source_target_pairs={{0,2},{1,3},{2,0},{3,1},{4,6},{5,7},{6,4},{7,5},{8,10},{9,11},{10,... | collective-permute-start | bytes 202760 | tf_op jit(solution)/shard_map/ppermute | solution.py:621
  82.9 1.5 %collective-permute-start.8 = (bf16[264,128]{1,0:T(8,128)(2,1)S(1)}, bf16[264,128]{1,0:T(8,128)(2,1)S(1)}, u32[]{:S(2)}, u32[]{:S(2)}) collective-permute-start(bf16[264,128]{1,0:T(8,128)(2,1)S(1)} %get-tuple-element.37), channel_id=1, source_target_pairs={{0,6},{1,7},{2,4},{3,5},{4,2},{5,3},{6,0},{7,1},{8,14},{9,15},{10,... | collective-permute-start | bytes 202760 | tf_op jit(solution)/shard_map/ppermute | solution.py:621
  84.4 0.7 collective-permute-start.9
  85.0 0.6 collective-permute-start.10
  85.7 1.9 %collective-permute-start.11 = (bf16[264,128]{1,0:T(8,128)(2,1)S(1)}, bf16[264,128]{1,0:T(8,128)(2,1)S(1)}, u32[]{:S(2)}, u32[]{:S(2)}) collective-permute-start(bf16[264,128]{1,0:T(8,128)(2,1)S(1)} %get-tuple-element.40), channel_id=1, source_target_pairs={{0,4},{1,5},{2,6},{3,7},{4,0},{5,1},{6,2},{7,3},{8,12},{9,13},{10,... | collective-permute-start | bytes 202760 | tf_op jit(solution)/shard_map/ppermute | solution.py:621
  87.6 2.8 %collective-permute-done.7.rest_1_ = bf16[264,128]{1,0:T(8,128)(2,1)S(1)} collective-permute-done((bf16[264,128]{1,0:T(8,128)(2,1)S(1)}, bf16[264,128]{1,0:T(8,128)(2,1)S(1)}, u32[]{:S(2)}, u32[]{:S(2)}) %collective-permute-start.7) | collective-permute-done | bytes 67616 | tf_op jit(solution)/shard_map/ppermute | solution.py:621
  90.4 0.0 collective-permute-start.12
  90.4 8.9 %collective-permute-done.8.rest_2_ = bf16[264,128]{1,0:T(8,128)(2,1)S(1)} collective-permute-done((bf16[264,128]{1,0:T(8,128)(2,1)S(1)}, bf16[264,128]{1,0:T(8,128)(2,1)S(1)}, u32[]{:S(2)}, u32[]{:S(2)}) %collective-permute-start.8) | collective-permute-done | bytes 67616 | tf_op jit(solution)/shard_map/ppermute | solution.py:621
  99.2 1.8 %collective-permute-done.10.rest_4_ = bf16[264,128]{1,0:T(8,128)(2,1)S(1)} collective-permute-done((bf16[264,128]{1,0:T(8,128)(2,1)S(1)}, bf16[264,128]{1,0:T(8,128)(2,1)S(1)}, u32[]{:S(2)}, u32[]{:S(2)}) %collective-permute-start.10) | collective-permute-done | bytes 67616 | tf_op jit(solution)/shard_map/ppermute | solution.py:621
  101.0 2.8 %collective-permute-done.11.rest_5_ = bf16[264,128]{1,0:T(8,128)(2,1)S(1)} collective-permute-done((bf16[264,128]{1,0:T(8,128)(2,1)S(1)}, bf16[264,128]{1,0:T(8,128)(2,1)S(1)}, u32[]{:S(2)}, u32[]{:S(2)}) %collective-permute-start.11) | collective-permute-done | bytes 67616 | tf_op jit(solution)/shard_map/ppermute | solution.py:621
  103.8 0.5 collective-permute-done.12.rest_6_
  104.3 1.5 %merge.1 = bf16[128,32,128]{2,1,0:T(8,128)(2,1)} custom-call(s32[1]{0:T(128)} %bitcast.me_ref, bf16[16,264,128]{2,1,0:T(8,128)(2,1)S(1)} %all-to-all-done.1.x_ref, bf16[264,128]{1,0:T(8,128)(2,1)S(1)} %get-tuple-element.35.rest_0_, bf16[264,128]{1,0:T(8,128)(2,1)S(1)} %collective-permute-done.7.rest_1_, bf16[264,128]{1,0:T(8,128)(2,1)S(1)} %collective-permute-done.8.rest_2_, ...), custom_call_target="tpu_custom_call" | custom-call | tf_op jit(solution)/shard_map/merge/pallas_call | solution.py:594
  (10 shorter events, 0.0 us)
Async XLA Ops:
  3.0 7.7 %copy-start = (bf16[128,32,384]{2,1,0:T(8,128)(2,1)S(1)}, bf16[128,32,384]{2,1,0:T(8,128)(2,1)}, u32[]{:S(2)}) copy-start(bf16[128,32,384]{2,1,0:T(8,128)(2,1)} %x_ref.3) | copy-start | bytes 9437188
  3.0 49.6 %all-to-all-start = ((bf16[16,520,128]{2,1,0:T(8,128)(2,1)}), bf16[16,520,128]{2,1,0:T(8,128)(2,1)}, u32[]{:S(2)}, u32[]{:S(2)}) async-start(bf16[16,520,128]{2,1,0:T(8,128)(2,1)} %cross.1), calls=%async_computation | async-start | bytes 4259840 | tf_op jit(solution)/shard_map/all_to_all | solution.py:616
  13.5 3.9 %collective-permute-start = (bf16[1024,128]{1,0:T(8,128)(2,1)S(1)}, bf16[1024,128]{1,0:T(8,128)(2,1)S(1)}, u32[]{:S(2)}, u32[]{:S(2)}) collective-permute-start(bf16[1024,128]{1,0:T(8,128)(2,1)S(1)} %get-tuple-element.28), channel_id=1, source_target_pairs={{0,1},{1,0},{2,3},{3,2},{4,5},{5,4},{6,7},{7,6},{8,9},{9,8},{10,11... | collective-permute-start | bytes 786440 | tf_op jit(solution)/shard_map/ppermute | solution.py:621
  13.9 22.2 %collective-permute-start.1 = (bf16[1024,128]{1,0:T(8,128)(2,1)S(1)}, bf16[1024,128]{1,0:T(8,128)(2,1)S(1)}, u32[]{:S(2)}, u32[]{:S(2)}) collective-permute-start(bf16[1024,128]{1,0:T(8,128)(2,1)S(1)} %get-tuple-element.29), channel_id=1, source_target_pairs={{0,2},{1,3},{2,0},{3,1},{4,6},{5,7},{6,4},{7,5},{8,10},{9,11},{10,... | collective-permute-start | bytes 786440 | tf_op jit(solution)/shard_map/ppermute | solution.py:621
  15.6 42.8 %collective-permute-start.2 = (bf16[1024,128]{1,0:T(8,128)(2,1)}, bf16[1024,128]{1,0:T(8,128)(2,1)S(1)}, u32[]{:S(2)}, u32[]{:S(2)}) collective-permute-start(bf16[1024,128]{1,0:T(8,128)(2,1)} %get-tuple-element.30), channel_id=1, source_target_pairs={{0,3},{1,2},{2,1},{3,0},{4,7},{5,6},{6,5},{7,4},{8,11},{9,10},{10,... | collective-permute-start | bytes 786440 | tf_op jit(solution)/shard_map/ppermute | solution.py:621
  15.6 42.8 %collective-permute-start.3 = (bf16[1024,128]{1,0:T(8,128)(2,1)}, bf16[1024,128]{1,0:T(8,128)(2,1)S(1)}, u32[]{:S(2)}, u32[]{:S(2)}) collective-permute-start(bf16[1024,128]{1,0:T(8,128)(2,1)} %get-tuple-element.31), channel_id=1, source_target_pairs={{0,4},{1,5},{2,6},{3,7},{4,0},{5,1},{6,2},{7,3},{8,12},{9,13},{10,... | collective-permute-start | bytes 786440 | tf_op jit(solution)/shard_map/ppermute | solution.py:621
  17.2 41.5 %collective-permute-start.4 = (bf16[1024,128]{1,0:T(8,128)(2,1)}, bf16[1024,128]{1,0:T(8,128)(2,1)S(1)}, u32[]{:S(2)}, u32[]{:S(2)}) collective-permute-start(bf16[1024,128]{1,0:T(8,128)(2,1)} %get-tuple-element.32), channel_id=1, source_target_pairs={{0,5},{1,4},{2,7},{3,6},{4,1},{5,0},{6,3},{7,2},{8,13},{9,12},{10,... | collective-permute-start | bytes 786440 | tf_op jit(solution)/shard_map/ppermute | solution.py:621
  17.4 49.0 %collective-permute-start.5 = (bf16[1024,128]{1,0:T(8,128)(2,1)}, bf16[1024,128]{1,0:T(8,128)(2,1)S(1)}, u32[]{:S(2)}, u32[]{:S(2)}) collective-permute-start(bf16[1024,128]{1,0:T(8,128)(2,1)} %get-tuple-element.33), channel_id=1, source_target_pairs={{0,6},{1,7},{2,4},{3,5},{4,2},{5,3},{6,0},{7,1},{8,14},{9,15},{10,... | collective-permute-start | bytes 786440 | tf_op jit(solution)/shard_map/ppermute | solution.py:621
  36.1 35.0 %collective-permute-start.6 = (bf16[1024,128]{1,0:T(8,128)(2,1)}, bf16[1024,128]{1,0:T(8,128)(2,1)S(1)}, u32[]{:S(2)}, u32[]{:S(2)}) collective-permute-start(bf16[1024,128]{1,0:T(8,128)(2,1)} %get-tuple-element.34), channel_id=1, source_target_pairs={{0,7},{1,6},{2,5},{3,4},{4,3},{5,2},{6,1},{7,0},{8,15},{9,14},{10,... | collective-permute-start | bytes 786440 | tf_op jit(solution)/shard_map/ppermute | solution.py:621
  74.5 29.8 %all-to-all-start.1 = ((bf16[16,264,128]{2,1,0:T(8,128)(2,1)}), bf16[16,264,128]{2,1,0:T(8,128)(2,1)S(1)}, u32[]{:S(2)}, u32[]{:S(2)}) async-start(bf16[16,264,128]{2,1,0:T(8,128)(2,1)} %own.1), calls=%async_computation.1 | async-start | bytes 2162688 | tf_op jit(solution)/shard_map/all_to_all | solution.py:616
  80.9 9.4 %collective-permute-start.7 = (bf16[264,128]{1,0:T(8,128)(2,1)S(1)}, bf16[264,128]{1,0:T(8,128)(2,1)S(1)}, u32[]{:S(2)}, u32[]{:S(2)}) collective-permute-start(bf16[264,128]{1,0:T(8,128)(2,1)S(1)} %get-tuple-element.36), channel_id=1, source_target_pairs={{0,2},{1,3},{2,0},{3,1},{4,6},{5,7},{6,4},{7,5},{8,10},{9,11},{10,... | collective-permute-start | bytes 202760 | tf_op jit(solution)/shard_map/ppermute | solution.py:621
  82.9 16.3 %collective-permute-start.8 = (bf16[264,128]{1,0:T(8,128)(2,1)S(1)}, bf16[264,128]{1,0:T(8,128)(2,1)S(1)}, u32[]{:S(2)}, u32[]{:S(2)}) collective-permute-start(bf16[264,128]{1,0:T(8,128)(2,1)S(1)} %get-tuple-element.37), channel_id=1, source_target_pairs={{0,6},{1,7},{2,4},{3,5},{4,2},{5,3},{6,0},{7,1},{8,14},{9,15},{10,... | collective-permute-start | bytes 202760 | tf_op jit(solution)/shard_map/ppermute | solution.py:621
  84.4 14.9 %collective-permute-start.9 = (bf16[264,128]{1,0:T(8,128)(2,1)S(1)}, bf16[264,128]{1,0:T(8,128)(2,1)S(1)}, u32[]{:S(2)}, u32[]{:S(2)}) collective-permute-start(bf16[264,128]{1,0:T(8,128)(2,1)S(1)} %get-tuple-element.38), channel_id=1, source_target_pairs={{0,3},{1,2},{2,1},{3,0},{4,7},{5,6},{6,5},{7,4},{8,11},{9,10},{10,... | collective-permute-start | bytes 202760 | tf_op jit(solution)/shard_map/ppermute | solution.py:621
  85.0 16.0 %collective-permute-start.10 = (bf16[264,128]{1,0:T(8,128)(2,1)S(1)}, bf16[264,128]{1,0:T(8,128)(2,1)S(1)}, u32[]{:S(2)}, u32[]{:S(2)}) collective-permute-start(bf16[264,128]{1,0:T(8,128)(2,1)S(1)} %get-tuple-element.39), channel_id=1, source_target_pairs={{0,7},{1,6},{2,5},{3,4},{4,3},{5,2},{6,1},{7,0},{8,15},{9,14},{10,... | collective-permute-start | bytes 202760 | tf_op jit(solution)/shard_map/ppermute | solution.py:621
  85.7 18.2 %collective-permute-start.11 = (bf16[264,128]{1,0:T(8,128)(2,1)S(1)}, bf16[264,128]{1,0:T(8,128)(2,1)S(1)}, u32[]{:S(2)}, u32[]{:S(2)}) collective-permute-start(bf16[264,128]{1,0:T(8,128)(2,1)S(1)} %get-tuple-element.40), channel_id=1, source_target_pairs={{0,4},{1,5},{2,6},{3,7},{4,0},{5,1},{6,2},{7,3},{8,12},{9,13},{10,... | collective-permute-start | bytes 202760 | tf_op jit(solution)/shard_map/ppermute | solution.py:621
  90.4 14.0 %collective-permute-start.12 = (bf16[264,128]{1,0:T(8,128)(2,1)S(1)}, bf16[264,128]{1,0:T(8,128)(2,1)S(1)}, u32[]{:S(2)}, u32[]{:S(2)}) collective-permute-start(bf16[264,128]{1,0:T(8,128)(2,1)S(1)} %get-tuple-element.41), channel_id=1, source_target_pairs={{0,5},{1,4},{2,7},{3,6},{4,1},{5,0},{6,3},{7,2},{8,13},{9,12},{10,... | collective-permute-start | bytes 202760 | tf_op jit(solution)/shard_map/ppermute | solution.py:621
  99.2 5.1 %collective-permute-start.13 = (bf16[264,128]{1,0:T(8,128)(2,1)S(1)}, bf16[264,128]{1,0:T(8,128)(2,1)S(1)}, u32[]{:S(2)}, u32[]{:S(2)}) collective-permute-start(bf16[264,128]{1,0:T(8,128)(2,1)S(1)} %get-tuple-element.42), channel_id=1, source_target_pairs={{0,1},{1,0},{2,3},{3,2},{4,5},{5,4},{6,7},{7,6},{8,9},{9,8},{10,11... | collective-permute-start | bytes 202760 | tf_op jit(solution)/shard_map/ppermute | solution.py:621
